TPU v7x, 32 devices: a whole 2x2x4 slice. The times are simulated.
32 devices in a mesh: dp: 8 (over y, x, core), tensor: 4 (over z).
Axes of the slice: x: 2, y: 2, z: 4, core: 2. Of those that a mesh axis runs over, the one named last changes fastest.
Arguments:
- tokens: bfloat16 [16384, 1024], P(('dp', 'tensor')), may hold values from -6 to 6
- cotangent: bfloat16 [16384, 1024], P(('dp', 'tensor')), may hold values from -6 to 6
- lengths: int32 [32], replicated, may hold values from 1 to 1024, as said below
- deal: int32 [32], replicated, may hold values from 0 to 31, as said below
- w_qkv: bfloat16 [3, 1024, 1024], P(None, 'dp', 'tensor'), may hold values from -0.1875 to 0.1875
- w_o: bfloat16 [1024, 1024], P('tensor', 'dp'), may hold values from -0.1875 to 0.1875
- w_1: bfloat16 [1024, 4096], P('dp', 'tensor'), may hold values from -0.1875 to 0.1875
- w_2: bfloat16 [4096, 1024], P('tensor', 'dp'), may hold values from -0.09375 to 0.09375
- b_qv: float32 [2, 1024], P(None, 'tensor'), may hold values from -1.8 to 1.8
- b_o: float32 [1024], replicated, may hold values from -0.3 to 0.3
- b_1: float32 [4096], P('tensor'), may hold values from -1.8 to 1.8
- b_2: float32 [1024], replicated, may hold values from -1.2 to 1.2
- ln_gain: float32 [4, 1024], replicated, may hold values from 0.25 to 1.75
- ln_bias: float32 [4, 1024], replicated, may hold values from -1.8 to 1.8
Outputs:
- output: bfloat16 [16384, 1024], P(('dp', 'tensor'))
- input_grad: bfloat16 [16384, 1024], P(('dp', 'tensor'))
- w_qkv_grad: float32 [3, 1024, 1024], P(None, 'dp', 'tensor')
- w_o_grad: float32 [1024, 1024], P('tensor', 'dp')
- w_1_grad: float32 [1024, 4096], P('dp', 'tensor')
- w_2_grad: float32 [4096, 1024], P('tensor', 'dp')
- b_qv_grad: float32 [2, 1024], P(None, 'tensor')
- b_o_grad: float32 [1024], replicated
- b_1_grad: float32 [4096], P('tensor')
- b_2_grad: float32 [1024], replicated
- ln_gain_grad: float32 [4, 1024], replicated
- ln_bias_grad: float32 [4, 1024], replicated
Inputs may be any that keep to these rules, and one draw needn't show every extreme that they name: The 4 sequences that deal gives to one data group have lengths that sum to 2048, and one of them has exactly 1024 tokens. `deal`: A permutation of the sequences; slots b * 4 to b * 4 + 3 belong to data group b.
All inputs are finite; a program needn't handle non-finite values. Where the computation divides by a largest or mean magnitude, that divisor is 1e-20 or more.
Results may differ from a plain program's by a relative error of at most 0.015.
Values may be sent and summed in bfloat16 or wider, within the bound.
A program may use at most 192 MiB of HBM per device.

v0:
```python
from functools import partial
import math

import jax
import jax.numpy as jnp
from jax import lax
from jax.sharding import PartitionSpec as P

DH = 64
MAXLEN = 1024
QBLK = 512


NORM_EPS = 1e-05
RELAX_FACTOR = 32.0
MASKED_OUT = -1000000000.0


def scaled_norm(values, norm_gain, norm_shift):
    peak = jnp.max(jnp.abs(values), axis=-1, keepdims=True) + NORM_EPS
    scaled = values / peak
    centred = scaled - jnp.mean(scaled, axis=-1, keepdims=True)
    spread = jnp.mean(centred * centred, axis=-1, keepdims=True)
    return centred * lax.rsqrt(spread + NORM_EPS) * norm_gain + norm_shift


def norm_back(values, norm_gain, norm_shift, row_grad):
    result, pull = jax.vjp(scaled_norm, values, norm_gain, norm_shift)
    return pull(row_grad)


def segment_of(seq_lens, row_total):
    seq_ends = jnp.cumsum(seq_lens)
    token_positions = jnp.arange(row_total, dtype=jnp.int32)
    return jnp.sum((token_positions[:, None] >= seq_ends[None, :]).astype(jnp.int32), axis=1)


def lane_gather(rows_low):
    return lax.all_gather(rows_low, "tensor", axis=0, tiled=True)


def lane_sum(term_fn, rows_here):
    return lax.psum_scatter(
        term_fn(jnp.int32(0), rows_here * lax.axis_size("tensor")).astype(jnp.bfloat16),
        "tensor",
        scatter_dimension=0,
        tiled=True,
    ).astype(jnp.float32)


def grad_gather(rows_low):
    return lax.all_gather(rows_low, "tensor", axis=0, tiled=True)


def grad_sum(term_fn, rows_here):
    return lax.psum_scatter(
        term_fn(jnp.int32(0), rows_here * lax.axis_size("tensor")).astype(jnp.bfloat16),
        "tensor",
        scatter_dimension=0,
        tiled=True,
    ).astype(jnp.float32)


def window_of(block_index, query_heads, key_pad, value_pad, segment, seg_pad):
    span = QBLK + MAXLEN
    first = block_index * QBLK
    query_block = lax.dynamic_slice_in_dim(query_heads, first, QBLK, 0)
    key_block = lax.dynamic_slice_in_dim(key_pad, first, span, 0)
    value_block = lax.dynamic_slice_in_dim(value_pad, first, span, 0)
    query_seg = lax.dynamic_slice_in_dim(segment, first, QBLK, 0)
    key_seg = lax.dynamic_slice_in_dim(seg_pad, first, span, 0)
    query_pos = first + jnp.arange(QBLK, dtype=jnp.int32)
    key_pos = first - MAXLEN + jnp.arange(span, dtype=jnp.int32)
    allowed = (key_pos[None, :] <= query_pos[:, None]) & (key_seg[None, :] == query_seg[:, None])
    return (query_block, key_block, value_block, allowed)


def block_scores(query_block, key_block, allowed):
    factor = 1.0 / (RELAX_FACTOR * math.sqrt(DH))
    raw_score = (
        jnp.einsum("qhd,khd->hqk", query_block, key_block, preferred_element_type=jnp.float32)
        * factor
    )
    return jnp.where(allowed[None], raw_score, MASKED_OUT)


def attn_forward(query_heads, key_pad, value_pad, segment, seg_pad):
    row_total = query_heads.shape[0]

    def one_block(block_index):
        query_block, key_block, value_block, allowed = window_of(
            block_index, query_heads, key_pad, value_pad, segment, seg_pad
        )
        masked = block_scores(query_block, key_block, allowed)
        row_peak = jnp.max(masked, axis=-1, keepdims=True)
        exponent = jnp.exp(RELAX_FACTOR * (masked - row_peak))
        row_totals = jnp.sum(exponent, axis=-1, keepdims=True)
        attn_prob = (exponent / row_totals).astype(jnp.bfloat16)
        mixed = jnp.einsum(
            "hqk,khd->qhd", attn_prob, value_block, preferred_element_type=jnp.float32
        )
        return (mixed.astype(jnp.bfloat16), row_peak, row_totals)

    mixed_all, peaks, sums_all = lax.map(one_block, jnp.arange(row_total // QBLK, dtype=jnp.int32))
    return (mixed_all.reshape(row_total, -1), peaks, sums_all)


def attn_backward(query_heads, key_pad, value_pad, segment, seg_pad, peaks, sums_all, grad_heads):
    row_total = query_heads.shape[0]
    span = QBLK + MAXLEN
    factor = 1.0 / (RELAX_FACTOR * math.sqrt(DH))
    start_grads = (jnp.zeros(key_pad.shape, jnp.float32), jnp.zeros(value_pad.shape, jnp.float32))

    def one_step(carry, block_index):
        key_grad, value_grad = carry
        first = block_index * QBLK
        query_block, key_block, value_block, allowed = window_of(
            block_index, query_heads, key_pad, value_pad, segment, seg_pad
        )
        grad_block = lax.dynamic_slice_in_dim(grad_heads, first, QBLK, 0)
        masked = block_scores(query_block, key_block, allowed)
        exponent = jnp.exp(RELAX_FACTOR * (masked - peaks[block_index]))
        attn_prob = exponent / sums_all[block_index]
        prob_low = attn_prob.astype(jnp.bfloat16)
        grad_prob = jnp.einsum(
            "qhd,khd->hqk", grad_block, value_block, preferred_element_type=jnp.float32
        )
        value_term = jnp.einsum(
            "hqk,qhd->khd", prob_low, grad_block, preferred_element_type=jnp.float32
        )
        inner = jnp.sum(grad_prob * attn_prob, axis=-1, keepdims=True)
        grad_score = jnp.where(
            allowed[None], RELAX_FACTOR * attn_prob * (grad_prob - inner), 0.0
        ).astype(jnp.bfloat16)
        query_term = (
            jnp.einsum("hqk,khd->qhd", grad_score, key_block, preferred_element_type=jnp.float32)
            * factor
        )
        key_term = (
            jnp.einsum("hqk,qhd->khd", grad_score, query_block, preferred_element_type=jnp.float32)
            * factor
        )
        key_grad = lax.dynamic_update_slice_in_dim(
            key_grad, lax.dynamic_slice_in_dim(key_grad, first, span, 0) + key_term, first, 0
        )
        value_grad = lax.dynamic_update_slice_in_dim(
            value_grad, lax.dynamic_slice_in_dim(value_grad, first, span, 0) + value_term, first, 0
        )
        return ((key_grad, value_grad), query_term)

    (key_grad, value_grad), query_terms = lax.scan(
        one_step, start_grads, jnp.arange(row_total // QBLK, dtype=jnp.int32)
    )
    query_grad = query_terms.reshape(row_total, -1)
    return (
        query_grad,
        key_grad[MAXLEN:].reshape(row_total, -1),
        value_grad[MAXLEN:].reshape(row_total, -1),
    )


def body(
    tokens, cotangent, lengths, deal, w_qkv, w_o, w_1, w_2, b_qv, b_o, b_1, b_2, ln_gain, ln_bias
):
    local_in, local_cot = (
        lax.all_to_all(tokens, "dp", split_axis=0, concat_axis=0, tiled=True),
        lax.all_to_all(cotangent, "dp", split_axis=0, concat_axis=0, tiled=True),
    )
    lane_count = lax.axis_size("tensor")
    group_index = lax.axis_index("dp")
    rows_here = local_in.shape[0]
    row_total = rows_here * lane_count
    seq_per = lengths.shape[0] // lax.axis_size("dp")
    picked = lax.dynamic_slice_in_dim(deal, group_index * seq_per, seq_per)
    lookup = picked[:, None] == jnp.arange(lengths.shape[0], dtype=jnp.int32)[None, :]
    seq_lens = jnp.sum(jnp.where(lookup, lengths[None, :], 0), axis=1)
    segment = segment_of(seq_lens, row_total)
    seg_pad = jnp.concatenate([jnp.full((MAXLEN,), -1, jnp.int32), segment])
    qkv_full, out_full = (
        lax.all_gather(w_qkv, "dp", axis=1, tiled=True),
        lax.all_gather(w_o, "dp", axis=1, tiled=True),
    )
    local_width = qkv_full.shape[2]
    head_count = local_width // DH
    hidden = local_in.astype(jnp.float32)
    normed_in = lane_gather(scaled_norm(hidden, ln_gain[0], ln_bias[0]).astype(jnp.bfloat16))
    projected = jnp.einsum("rd,sde->sre", normed_in, qkv_full, preferred_element_type=jnp.float32)
    query_rows = (projected[0] + b_qv[0]).astype(jnp.bfloat16)
    key_rows = projected[1].astype(jnp.bfloat16)
    value_rows = (projected[2] + b_qv[1]).astype(jnp.bfloat16)
    head_shape = (row_total, head_count, DH)
    pad_rows = jnp.zeros((MAXLEN, head_count, DH), jnp.bfloat16)
    query_heads = query_rows.reshape(head_shape)
    key_pad = jnp.concatenate([pad_rows, key_rows.reshape(head_shape)], 0)
    value_pad = jnp.concatenate([pad_rows, value_rows.reshape(head_shape)], 0)
    heads_out, peaks, sums_all = attn_forward(query_heads, key_pad, value_pad, segment, seg_pad)

    def out_term(first_row, row_count):
        return jnp.dot(heads_out, out_full, preferred_element_type=jnp.float32)

    attn_out = lane_sum(out_term, rows_here) + b_o
    first_sum = hidden + scaled_norm(attn_out, ln_gain[1], ln_bias[1])
    normed_mid = lane_gather(scaled_norm(first_sum, ln_gain[2], ln_bias[2]).astype(jnp.bfloat16))
    up_full, down_full = (
        lax.all_gather(w_1, "dp", axis=0, tiled=True),
        lax.all_gather(w_2, "dp", axis=1, tiled=True),
    )
    pre_act = jnp.dot(normed_mid, up_full, preferred_element_type=jnp.float32) + b_1
    act = jax.nn.gelu(pre_act, approximate=False).astype(jnp.bfloat16)

    def down_term(first_row, row_count):
        return jnp.dot(act, down_full, preferred_element_type=jnp.float32)

    feedforward_output = lane_sum(down_term, rows_here) + b_2
    result = first_sum + scaled_norm(feedforward_output, ln_gain[3], ln_bias[3])
    grad_result = local_cot.astype(jnp.float32)
    grad_ffn, gain_three, shift_three = norm_back(
        feedforward_output, ln_gain[3], ln_bias[3], grad_result
    )
    grad_ffn_low = grad_ffn.astype(jnp.bfloat16)
    bias_two_grad = jnp.sum(grad_ffn_low.astype(jnp.float32), axis=0)
    grad_ffn_full = grad_gather(grad_ffn_low)
    up_back, down_back = (
        lax.all_gather(w_1, "dp", axis=0, tiled=True),
        lax.all_gather(w_2, "dp", axis=1, tiled=True),
    )
    grad_act = jnp.einsum("rd,fd->rf", grad_ffn_full, down_back, preferred_element_type=jnp.float32)
    down_grad = jnp.einsum("rf,rd->fd", act, grad_ffn_full, preferred_element_type=jnp.float32)
    gelu_value, gelu_pull = jax.vjp(partial(jax.nn.gelu, approximate=False), pre_act)
    grad_pre = gelu_pull(grad_act)[0].astype(jnp.bfloat16)
    bias_one_grad = jnp.sum(grad_pre.astype(jnp.float32), axis=0)
    up_grad = jnp.einsum("rd,rf->df", normed_mid, grad_pre, preferred_element_type=jnp.float32)
    up_shard, down_shard = (up_grad, down_grad)

    def mid_term(first_row, row_count):
        return jnp.einsum("rf,df->rd", grad_pre, up_back, preferred_element_type=jnp.float32)

    grad_mid = grad_sum(mid_term, rows_here)
    grad_first_part, gain_two, shift_two = norm_back(first_sum, ln_gain[2], ln_bias[2], grad_mid)
    grad_first = grad_result + grad_first_part
    grad_attn, gain_one, shift_one = norm_back(attn_out, ln_gain[1], ln_bias[1], grad_first)
    grad_attn_low = grad_attn.astype(jnp.bfloat16)
    bias_out_grad = jnp.sum(grad_attn_low.astype(jnp.float32), axis=0)
    grad_attn_full = grad_gather(grad_attn_low)
    qkv_back, out_back = (
        lax.all_gather(w_qkv, "dp", axis=1, tiled=True),
        lax.all_gather(w_o, "dp", axis=1, tiled=True),
    )
    grad_heads = jnp.einsum(
        "rd,ed->re", grad_attn_full, out_back, preferred_element_type=jnp.float32
    ).astype(jnp.bfloat16)
    out_grad = jnp.einsum(
        "re,rd->ed", heads_out, grad_attn_full, preferred_element_type=jnp.float32
    )
    query_grad, key_grad, value_grad = attn_backward(
        query_heads,
        key_pad,
        value_pad,
        segment,
        seg_pad,
        peaks,
        sums_all,
        grad_heads.reshape(head_shape),
    )
    grad_qkv = jnp.stack([query_grad, key_grad, value_grad]).astype(jnp.bfloat16)
    grad_qkv_wide = grad_qkv.astype(jnp.float32)
    bias_qv_grad = jnp.stack([jnp.sum(grad_qkv_wide[0], axis=0), jnp.sum(grad_qkv_wide[2], axis=0)])
    qkv_grad = jnp.einsum("rd,sre->sde", normed_in, grad_qkv, preferred_element_type=jnp.float32)

    def input_term(first_row, row_count):
        return jnp.einsum("sre,sde->rd", grad_qkv, qkv_back, preferred_element_type=jnp.float32)

    grad_in = grad_sum(input_term, rows_here)
    grad_hidden_part, gain_zero, shift_zero = norm_back(hidden, ln_gain[0], ln_bias[0], grad_in)
    grad_hidden = grad_first + grad_hidden_part
    qkv_shard, out_shard, up_shard, down_shard = (
        lax.psum_scatter(qkv_grad, "dp", scatter_dimension=1, tiled=True),
        lax.psum_scatter(out_grad, "dp", scatter_dimension=1, tiled=True),
        lax.psum_scatter(up_grad, "dp", scatter_dimension=0, tiled=True),
        lax.psum_scatter(down_grad, "dp", scatter_dimension=1, tiled=True),
    )
    head_bias_qv, head_bias_one = lax.psum((bias_qv_grad, bias_one_grad), "dp")
    gain_stack = jnp.stack([gain_zero, gain_one, gain_two, gain_three])
    shift_stack = jnp.stack([shift_zero, shift_one, shift_two, shift_three])
    gain_total, offset_overall, bias_out_total, bias_two_total = lax.psum(
        (gain_stack, shift_stack, bias_out_grad, bias_two_grad), ("dp", "tensor")
    )
    output_rows, input_rows = (
        lax.all_to_all(result.astype(jnp.bfloat16), "dp", split_axis=0, concat_axis=0, tiled=True),
        lax.all_to_all(
            grad_hidden.astype(jnp.bfloat16), "dp", split_axis=0, concat_axis=0, tiled=True
        ),
    )
    return (
        output_rows,
        input_rows,
        qkv_shard,
        out_shard,
        up_shard,
        down_shard,
        head_bias_qv,
        bias_out_total,
        head_bias_one,
        bias_two_total,
        gain_total,
        offset_overall,
    )


def solution(mesh):
    placed = (
        P(("dp", "tensor"), None),
        P(("dp", "tensor"), None),
        P(),
        P(),
        P(None, "dp", "tensor"),
        P("tensor", "dp"),
        P("dp", "tensor"),
        P("tensor", "dp"),
        P(None, "tensor"),
        P(),
        P("tensor"),
        P(),
        P(),
        P(),
    )
    return jax.shard_map(
        body,
        mesh=mesh,
        in_specs=placed,
        out_specs=(
            P(("dp", "tensor"), None),
            P(("dp", "tensor"), None),
            P(None, "dp", "tensor"),
            P("tensor", "dp"),
            P("dp", "tensor"),
            P("tensor", "dp"),
            P(None, "tensor"),
            P(),
            P("tensor"),
            P(),
            P(),
            P(),
        ),
        check_vma=False,
    )
```

profile of v0, /device:TPU:1, one launch (start us, length us, event | category | flops | bytes accessed | tf_op | source)
XLA Modules:
  0.0 1348.1 jit_solution(9678845861428645542)
XLA Ops:
  7.2 5.4 all-to-all-start
  14.7 9.8 all-to-all-done
  30.5 14.3 %all_gather.30 = bf16[256,1024]{1,0:T(8,128)(2,1)S(1)} all-gather(bf16[256,128]{1,0:T(8,128)(2,1)S(1)} %copy-done.32), channel_id=1, replica_groups=mesh['dp'=8,'tensor'=4] {'dp'}, dimensions={1}, use_global_device_ids=true | all-gather | bytes 589824 | tf_op jit(solution)/shard_map/all_gather | solution.py:181
  45.0 82.6 %all-gather.8.cloned.1.call-done = bf16[2048,1024]{1,0:T(8,128)(2,1)} async-done(((bf16[512,1024]{1,0:T(8,128)(2,1)}), bf16[2048,1024]{1,0:T(8,128)(2,1)}) %all-gather.8.cloned.1.call-update) | async-done | bytes 4194320 | tf_op jit(solution)/shard_map/all_gather | solution.py:39
  127.6 5.7 fusion.84
  136.9 58.6 %while.32 = (s32[]{:T(128)}, bf16[4,512,4,64]{1,3,2,0:T(8,128)(2,1)}, f32[4,4,512,1]{2,1,3,0:T(4,128)S(1)}, f32[4,4,512,1]{2,1,3,0:T(4,128)S(1)}, s32[4]{0:T(128...) while((s32[]{:T(128)}, ...), condition=%wide.region_9.10_spmd, body=%wide.region_6.9_spmd.sunk | while | flops 851834880 | bytes 43106592 | solution.py:104
  139.0 3.7 fusion.195
  142.7 3.9 fusion.196
  146.6 4.9 fusion.197
  157.4 3.9 fusion.196
  161.3 4.9 fusion.197
  172.0 3.9 fusion.196
  175.9 4.9 fusion.197
  186.7 3.9 fusion.196
  190.6 4.9 fusion.197
  203.4 74.7 %reduce-scatter.9.cloned.1.call-done = bf16[512,1024]{1,0:T(8,128)(2,1)} async-done(((bf16[2048,1024]{1,0:T(8,128)(2,1)}), bf16[512,1024]{1,0:T(8,128)(2,1)}) %reduce-scatter.9.cloned.1.call-update) | async-done | bytes 1048592 | tf_op jit(solution)/shard_map/reduce_scatter | solution.py:43
  285.9 23.0 %all-gather.14.cloned.1.call-done = bf16[1024,1024]{1,0:T(8,128)(2,1)} async-done(((bf16[128,1024]{1,0:T(8,128)(2,1)}), bf16[1024,1024]{1,0:T(8,128)(2,1)}) %all-gather.14.cloned.1.call-update) | async-done | bytes 2097168 | tf_op jit(solution)/shard_map/all_gather | solution.py:205
  308.8 82.4 %all-gather.12.cloned.1.call-done = bf16[2048,1024]{1,0:T(8,128)(2,1)} async-done(((bf16[512,1024]{1,0:T(8,128)(2,1)}), bf16[2048,1024]{1,0:T(8,128)(2,1)}) %all-gather.12.cloned.1.call-update) | async-done | bytes 4194320 | tf_op jit(solution)/shard_map/all_gather | solution.py:39
  391.3 26.2 %multiply_convert_fusion = (bf16[2048,1024]{1,0:T(8,128)(2,1)}, f32[2048,1024]{1,0:T(8,128)}, f32[2048,1024]{1,0:T(8,128)}) fusion(f32[1024]{0:T(1024)S(1)} %copy-done.58, bf16[2048,1024]{1,0:T(8,128)(2,1)} %all-gather.12.cloned.1.call-done, bf16[1024,1024]{1,0:T(8,128)(2,1)} %all-gather.14.cloned.1.call-done), kind=kOutput, calls=%fused_computation.69 | convolution fusion | flops 4433379328 | bytes 27267072 | tf_op jit(solution)/shard_map/dot_general | solution.py:208
  420.3 9.3 convolution_convert_fusion.2
  429.7 4.4 all-to-all-start.2
  434.3 71.9 %reduce-scatter.11.cloned.1.call-done = bf16[512,1024]{1,0:T(8,128)(2,1)} async-done(((bf16[2048,1024]{1,0:T(8,128)(2,1)}), bf16[512,1024]{1,0:T(8,128)(2,1)}) %reduce-scatter.11.cloned.1.call-update) | async-done | bytes 1048592 | tf_op jit(solution)/shard_map/reduce_scatter | solution.py:43
  518.8 81.4 %all-gather.18.cloned.1.call-done = bf16[2048,1024]{1,0:T(8,128)(2,1)} async-done(((bf16[512,1024]{1,0:T(8,128)(2,1)}), bf16[2048,1024]{1,0:T(8,128)(2,1)}) %all-gather.18.cloned.1.call-update) | async-done | bytes 4194320 | tf_op jit(solution)/shard_map/all_gather | solution.py:52
  600.1 14.0 %convert_reduce_fusion = (f32[1024]{0:T(1024)}, bf16[2048,1024]{1,0:T(8,128)(2,1)S(1)}) fusion(f32[2048,1024]{1,0:T(8,128)} %get-tuple-element.431, f32[2048,1024]{1,0:T(8,128)} %get-tuple-element.460, f32[1024]{0:T(1024)S(1)} %copy-done.58, bf16[2048,1024]{1,0:T(8,128)(2,1)} %all-gather.18.cloned.1.call-done, ...), kind=kOutput, calls=%fused_computation.67 | convolution fusion | flops 4330617856 | bytes 27271168 | tf_op jit(solution)/shard_map/rd,fd->rf/dot_general | solution.py:227
  616.1 6.3 convolution_convert_fusion.1
  622.9 75.0 %reduce-scatter.13.cloned.1.call-done = bf16[512,1024]{1,0:T(8,128)(2,1)} async-done(((bf16[2048,1024]{1,0:T(8,128)(2,1)}), bf16[512,1024]{1,0:T(8,128)(2,1)}) %reduce-scatter.13.cloned.1.call-update) | async-done | bytes 1048592 | tf_op jit(solution)/shard_map/reduce_scatter | solution.py:56
  704.4 4.3 multiply_reduce_fusion.1
  713.2 81.3 %all-gather.20.cloned.1.call-done = bf16[2048,1024]{1,0:T(8,128)(2,1)} async-done(((bf16[512,1024]{1,0:T(8,128)(2,1)}), bf16[2048,1024]{1,0:T(8,128)(2,1)}) %all-gather.20.cloned.1.call-update) | async-done | bytes 4194320 | tf_op jit(solution)/shard_map/all_gather | solution.py:52
  794.6 4.4 convolution_convert_fusion.3
  803.0 238.6 %while.33 = (s32[]{:T(128)}, f32[3072,4,64]{0,2,1:T(8,128)}, f32[3072,4,64]{0,2,1:T(8,128)}, bf16[4,512,4,64]{1,3,2,0:T(8,128)(2,1)}, s32[4]{0:T(128)S(1)}, /*in...) while((s32[]{:T(128)}, f32[3072,4,64]{0,2,1:T(8,128)}, ...), condition=%wide.region_36.37_spmd, body=%wide.region_34.36_spmd.sunk | while | flops 2073568256 | bytes 206397872 | solution.py:151
  807.3 5.4 exponential_divide_fusion.2
  812.7 5.1 fusion.210
  817.9 6.3 fusion.208
  824.2 18.0 %fusion.211 = bf16[4,512,4,64]{1,3,2,0:T(8,128)(2,1)} fusion(bf16[4,512,4,64]{1,3,2,0:T(8,128)(2,1)} %get-tuple-element.686, s32[]{:T(128)S(6)} %copy.78, f32[4,512,1536]{2,1,0:T(8,128)} %fusion.208, f32[4,512,1536]{2,1,0:T(8,128)} %copy-done, pred[512,1536]{1,0:T(8,128)(4,1)S(1)} %compare_and_fusion.5, ...), kind=kOutput, calls=%fused_computation.42.clone.1 | convolution fusion | flops 421662208 | bytes 52428808 | tf_op jit(solution)/shard_map/while/body/eval_jaxpr/hqk,khd->qhd/dot_general | solution.py:136
  842.2 20.6 %fusion.209 = f32[3072,4,64]{0,2,1:T(8,128)} fusion(f32[3072,4,64]{0,2,1:T(8,128)} %get-tuple-element.684, s32[]{:T(128)S(6)} %select_n.214, f32[4,512,1536]{2,1,0:T(8,128)} %fusion.208, f32[4,512,1536]{2,1,0:T(8,128)} %copy-done, pred[512,1536]{1,0:T(8,128)(4,1)S(1)} %compare_and_fusion.5, bf16[2048,4,64]{0,2,1:T(8,128)(2,1)} %get-tuple-element.708, ...), kind=kOutput, calls=%fused_computation.36.clone.1 | convolution fusion | flops 422317568 | bytes 54525960 | tf_op jit(solution)/shard_map/while/body/eval_jaxpr/hqk,qhd->khd/dot_general | solution.py:140
  866.9 5.4 exponential_divide_fusion.2
  872.3 5.1 fusion.210
  877.5 6.3 fusion.208
  883.8 18.1 %fusion.211 = bf16[4,512,4,64]{1,3,2,0:T(8,128)(2,1)} fusion(bf16[4,512,4,64]{1,3,2,0:T(8,128)(2,1)} %get-tuple-element.686, s32[]{:T(128)S(6)} %copy.78, f32[4,512,1536]{2,1,0:T(8,128)} %fusion.208, f32[4,512,1536]{2,1,0:T(8,128)} %copy-done, pred[512,1536]{1,0:T(8,128)(4,1)S(1)} %compare_and_fusion.5, ...), kind=kOutput, calls=%fused_computation.42.clone.1 | convolution fusion | flops 421662208 | bytes 52428808 | tf_op jit(solution)/shard_map/while/body/eval_jaxpr/hqk,khd->qhd/dot_general | solution.py:136
  901.9 20.5 %fusion.209 = f32[3072,4,64]{0,2,1:T(8,128)} fusion(f32[3072,4,64]{0,2,1:T(8,128)} %get-tuple-element.684, s32[]{:T(128)S(6)} %select_n.214, f32[4,512,1536]{2,1,0:T(8,128)} %fusion.208, f32[4,512,1536]{2,1,0:T(8,128)} %copy-done, pred[512,1536]{1,0:T(8,128)(4,1)S(1)} %compare_and_fusion.5, bf16[2048,4,64]{0,2,1:T(8,128)(2,1)} %get-tuple-element.708, ...), kind=kOutput, calls=%fused_computation.36.clone.1 | convolution fusion | flops 422317568 | bytes 54525960 | tf_op jit(solution)/shard_map/while/body/eval_jaxpr/hqk,qhd->khd/dot_general | solution.py:140
  926.5 5.4 exponential_divide_fusion.2
  931.9 5.1 fusion.210
  937.1 6.3 fusion.208
  943.4 18.1 %fusion.211 = bf16[4,512,4,64]{1,3,2,0:T(8,128)(2,1)} fusion(bf16[4,512,4,64]{1,3,2,0:T(8,128)(2,1)} %get-tuple-element.686, s32[]{:T(128)S(6)} %copy.78, f32[4,512,1536]{2,1,0:T(8,128)} %fusion.208, f32[4,512,1536]{2,1,0:T(8,128)} %copy-done, pred[512,1536]{1,0:T(8,128)(4,1)S(1)} %compare_and_fusion.5, ...), kind=kOutput, calls=%fused_computation.42.clone.1 | convolution fusion | flops 421662208 | bytes 52428808 | tf_op jit(solution)/shard_map/while/body/eval_jaxpr/hqk,khd->qhd/dot_general | solution.py:136
  961.5 20.5 %fusion.209 = f32[3072,4,64]{0,2,1:T(8,128)} fusion(f32[3072,4,64]{0,2,1:T(8,128)} %get-tuple-element.684, s32[]{:T(128)S(6)} %select_n.214, f32[4,512,1536]{2,1,0:T(8,128)} %fusion.208, f32[4,512,1536]{2,1,0:T(8,128)} %copy-done, pred[512,1536]{1,0:T(8,128)(4,1)S(1)} %compare_and_fusion.5, bf16[2048,4,64]{0,2,1:T(8,128)(2,1)} %get-tuple-element.708, ...), kind=kOutput, calls=%fused_computation.36.clone.1 | convolution fusion | flops 422317568 | bytes 54525960 | tf_op jit(solution)/shard_map/while/body/eval_jaxpr/hqk,qhd->khd/dot_general | solution.py:140
  986.0 5.4 exponential_divide_fusion.2
  991.4 5.1 fusion.210
  996.6 6.3 fusion.208
  1002.9 18.1 %fusion.211 = bf16[4,512,4,64]{1,3,2,0:T(8,128)(2,1)} fusion(bf16[4,512,4,64]{1,3,2,0:T(8,128)(2,1)} %get-tuple-element.686, s32[]{:T(128)S(6)} %copy.78, f32[4,512,1536]{2,1,0:T(8,128)} %fusion.208, f32[4,512,1536]{2,1,0:T(8,128)} %copy-done, pred[512,1536]{1,0:T(8,128)(4,1)S(1)} %compare_and_fusion.5, ...), kind=kOutput, calls=%fused_computation.42.clone.1 | convolution fusion | flops 421662208 | bytes 52428808 | tf_op jit(solution)/shard_map/while/body/eval_jaxpr/hqk,khd->qhd/dot_general | solution.py:136
  1021.1 20.4 %fusion.209 = f32[3072,4,64]{0,2,1:T(8,128)} fusion(f32[3072,4,64]{0,2,1:T(8,128)} %get-tuple-element.684, s32[]{:T(128)S(6)} %select_n.214, f32[4,512,1536]{2,1,0:T(8,128)} %fusion.208, f32[4,512,1536]{2,1,0:T(8,128)} %copy-done, pred[512,1536]{1,0:T(8,128)(4,1)S(1)} %compare_and_fusion.5, bf16[2048,4,64]{0,2,1:T(8,128)(2,1)} %get-tuple-element.708, ...), kind=kOutput, calls=%fused_computation.36.clone.1 | convolution fusion | flops 422317568 | bytes 54525960 | tf_op jit(solution)/shard_map/while/body/eval_jaxpr/hqk,qhd->khd/dot_general | solution.py:140
  1052.8 6.7 bitcast_convert_fusion
  1059.6 7.4 fusion.131
  1067.2 10.0 fusion.154
  1077.5 10.0 fusion.155
  1088.2 4.8 all-to-all-start.1
  1093.1 4.5 fusion.153
  1097.7 37.4 %reduce-scatter.15.cloned.1.call-done = bf16[512,1024]{1,0:T(8,128)(2,1)} async-done(((bf16[2048,1024]{1,0:T(8,128)(2,1)}), bf16[512,1024]{1,0:T(8,128)(2,1)}) %reduce-scatter.15.cloned.1.call-update) | async-done | bytes 1048592 | tf_op jit(solution)/shard_map/reduce_scatter | solution.py:56
  1142.6 4.9 all-to-all-start.3
  1150.2 19.4 %all-reduce.4 = (f32[2,256]{1,0:T(2,128)}, f32[1024]{0:T(1024)}) all-reduce(f32[2,256]{1,0:T(2,128)S(1)} %pad_maximum_fusion.3, f32[1024]{0:T(1024)S(1)} %copy-done.55), channel_id=1, replica_groups=mesh['dp'=8,'tensor'=4] {'dp'}, use_global_device_ids=true, to_apply=%region_48.49 | all-reduce | flops 1536 | bytes 12288 | tf_op jit(solution)/shard_map/psum | solution.py:282
  1169.6 15.8 %reduce-scatter.17.cloned.1.call-done = f32[3,128,256]{1,2,0:T(8,128)} async-done(((f32[3,1024,256]{1,2,0:T(8,128)}), f32[3,128,256]{1,2,0:T(8,128)}) %reduce-scatter.17.cloned.1.call-update) | async-done | bytes 393232 | tf_op jit(solution)/shard_map/reduce_scatter | solution.py:277
  1187.4 40.2 %all-reduce.3 = (f32[1024]{0:T(1024)}, f32[1024]{0:T(1024)}, f32[4,1024]{1,0:T(4,128)}, f32[4,1024]{1,0:T(4,128)}) all-reduce(f32[1024]{0:T(1024)S(1)} %copy-done.53, f32[1024]{0:T(1024)S(1)} %copy-done.52, f32[4,1024]{1,0:T(4,128)S(1)} %get-tuple-element.461, ...), channel_id=1, replica_groups=mesh['dp'=8,'tensor'=4] {'dp','tensor'}, use_global_device_ids=true, to_apply=%region_50.51 | all-reduce | flops 10240 | bytes 81920 | tf_op jit(solution)/shard_map/psum | solution.py:285
  1227.6 14.0 %reduce-scatter.21.cloned.1.call-done = f32[128,1024]{1,0:T(8,128)} async-done(((f32[1024,1024]{1,0:T(8,128)}), f32[128,1024]{1,0:T(8,128)}) %reduce-scatter.21.cloned.1.call-update) | async-done | bytes 524304 | tf_op jit(solution)/shard_map/reduce_scatter | solution.py:279
  1241.6 55.1 %reduce-scatter.23.cloned.1.call-done = f32[1024,128]{1,0:T(8,128)} async-done(((f32[1024,1024]{1,0:T(8,128)}), f32[1024,128]{1,0:T(8,128)}) %reduce-scatter.23.cloned.1.call-update) | async-done | bytes 524304 | tf_op jit(solution)/shard_map/reduce_scatter | solution.py:280
  1296.7 39.9 %reduce-scatter.19.cloned.1.call-done = f32[256,128]{1,0:T(8,128)} async-done(((f32[256,1024]{1,0:T(8,128)}), f32[256,128]{1,0:T(8,128)}) %reduce-scatter.19.cloned.1.call-update) | async-done | bytes 131088 | tf_op jit(solution)/shard_map/reduce_scatter | solution.py:278
  (330 shorter events, 112.2 us)
Async XLA Ops:
  7.2 5.4 copy-start.24
  7.2 6.3 copy-start.50
  7.2 6.9 copy-start.51
  7.2 17.3 %all-to-all-start = ((bf16[8,64,1024]{2,1,0:T(8,128)(2,1)}), bf16[8,64,1024]{2,1,0:T(8,128)(2,1)S(1)}, u32[]{:S(2)}, u32[]{:S(2)}) async-start(bf16[8,64,1024]{2,1,0:T(8,128)(2,1)} %bitcast.177), calls=%async_computation | async-start | bytes 2097152 | tf_op jit(solution)/shard_map/all_to_all | solution.py:166
  12.6 32.4 %all-gather.10.cloned.1.call-start = ((), (), s32[]{:S(2)}) async-start(), calls=%async_computation.13 | async-start | bytes 1769472 | tf_op jit(solution)/shard_map/all_gather | solution.py:180
  13.4 114.2 %all-gather.8.cloned.1.call-start = ((), (), s32[]{:S(2)}) async-start(), calls=%async_computation.12 | async-start | bytes 5242880 | tf_op jit(solution)/shard_map/all_gather | solution.py:39
  14.1 15.6 %copy-start.25 = (f32[1,1024]{1,0:T(1,128)}, f32[1,1024]{1,0:T(1,128)S(1)}, u32[]{:S(2)}) copy-start(f32[1,1024]{1,0:T(1,128)S(1)} %get-tuple-element.446) | copy-start | bytes 12292
  24.5 257.4 %copy-start.1 = (bf16[8,64,1024]{2,1,0:T(8,128)(2,1)}, bf16[8,64,1024]{2,1,0:T(8,128)(2,1)S(1)}, u32[]{:S(2)}) copy-start(bf16[8,64,1024]{2,1,0:T(8,128)(2,1)S(1)} %all-to-all-done) | copy-start | bytes 3145732
  25.3 4.9 copy-start.56
  25.3 5.2 copy-start.32
  26.9 106.4 %copy-start.39 = (f32[512]{0:T(512)}, f32[512]{0:T(512)S(1)}, u32[]{:S(2)}) copy-start(f32[512]{0:T(512)S(1)} %add.362) | copy-start | bytes 6148
  26.9 106.4 %copy-start.35 = (f32[512]{0:T(512)}, f32[512]{0:T(512)S(1)}, u32[]{:S(2)}) copy-start(f32[512]{0:T(512)S(1)} %rsqrt.44) | copy-start | bytes 6148
  29.7 248.4 %reduce-scatter.9.cloned.1.call-start = ((), (), s32[]{:S(2)}) async-start(), calls=%async_computation.14 | async-start | bytes 5242880 | tf_op jit(solution)/shard_map/reduce_scatter | solution.py:43
  44.8 153.6 %copy-start.20 = (bf16[256,1024]{1,0:T(8,128)(2,1)}, bf16[256,1024]{1,0:T(8,128)(2,1)S(1)}, u32[]{:S(2)}) copy-start(bf16[256,1024]{1,0:T(8,128)(2,1)S(1)} %all_gather.30) | copy-start | bytes 1572868
  202.6 75.5 %copy-start.22 = (f32[1024]{0:T(1024)S(1)}, f32[1024]{0:T(1024)}, u32[]{:S(2)}) copy-start(f32[1024]{0:T(1024)} %param.27) | copy-start | bytes 12292
  202.6 79.3 %copy-start.31 = (f32[1,1024]{1,0:T(1,128)S(1)}, f32[1,1024]{1,0:T(1,128)}, u32[]{:S(2)}) copy-start(f32[1,1024]{1,0:T(1,128)} %get-tuple-element.445) | copy-start | bytes 12292
  202.6 79.3 %copy-start.49 = (f32[1,1024]{1,0:T(1,128)S(1)}, f32[1,1024]{1,0:T(1,128)}, u32[]{:S(2)}) copy-start(f32[1,1024]{1,0:T(1,128)} %get-tuple-element.449) | copy-start | bytes 12292
  202.6 106.2 %all-gather.14.cloned.1.call-start = ((), (), s32[]{:S(2)}) async-start(), calls=%async_computation.16 | async-start | bytes 2359296 | tf_op jit(solution)/shard_map/all_gather | solution.py:205
  203.2 188.1 %all-gather.12.cloned.1.call-start = ((), (), s32[]{:S(2)}) async-start(), calls=%async_computation.15 | async-start | bytes 5242880 | tf_op jit(solution)/shard_map/all_gather | solution.py:39
  283.8 107.5 %copy-start.58 = (f32[1024]{0:T(1024)S(1)}, f32[1024]{0:T(1024)}, u32[]{:S(2)}) copy-start(f32[1024]{0:T(1024)} %param.28) | copy-start | bytes 12292
  285.3 135.1 %all-gather.16.cloned.1.call-start = ((), (), s32[]{:S(2)}) async-start(), calls=%async_computation.17 | async-start | bytes 2359296 | tf_op jit(solution)/shard_map/all_gather | solution.py:206
  285.8 220.4 %reduce-scatter.11.cloned.1.call-start = ((), (), s32[]{:S(2)}) async-start(), calls=%async_computation.18 | async-start | bytes 5242880 | tf_op jit(solution)/shard_map/reduce_scatter | solution.py:43
  429.7 76.5 %copy-start.23 = (f32[1024]{0:T(1024)S(1)}, f32[1024]{0:T(1024)}, u32[]{:S(2)}) copy-start(f32[1024]{0:T(1024)} %param.29) | copy-start | bytes 12292
  429.7 80.3 %all-to-all-start.2 = ((bf16[8,64,1024]{2,1,0:T(8,128)(2,1)}), bf16[8,64,1024]{2,1,0:T(8,128)(2,1)}, u32[]{:S(2)}, u32[]{:S(2)}) async-start(bf16[8,64,1024]{2,1,0:T(8,128)(2,1)} %bitcast.31), calls=%async_computation.4 | async-start | bytes 2097152 | tf_op jit(solution)/shard_map/all_to_all | solution.py:167
  434.1 76.0 %copy-start.33 = (f32[1,1024]{1,0:T(1,128)S(1)}, f32[1,1024]{1,0:T(1,128)}, u32[]{:S(2)}) copy-start(f32[1,1024]{1,0:T(1,128)} %get-tuple-element.447) | copy-start | bytes 12292
  434.1 166.0 %all-gather.18.cloned.1.call-start = ((), (), s32[]{:S(2)}) async-start(), calls=%async_computation.19 | async-start | bytes 5242880 | tf_op jit(solution)/shard_map/all_gather | solution.py:52
  518.7 179.2 %reduce-scatter.13.cloned.1.call-start = ((), (), s32[]{:S(2)}) async-start(), calls=%async_computation.20 | async-start | bytes 5242880 | tf_op jit(solution)/shard_map/reduce_scatter | solution.py:56
  600.1 15.9 %copy-start.57 = (bf16[1024,1024]{1,0:T(8,128)(2,1)S(1)}, bf16[1024,1024]{1,0:T(8,128)(2,1)}, u32[]{:S(2)}) copy-start(bf16[1024,1024]{1,0:T(8,128)(2,1)} %all-gather.14.cloned.1.call-done) | copy-start | bytes 6291460
  622.4 172.2 %all-gather.20.cloned.1.call-start = ((), (), s32[]{:S(2)}) async-start(), calls=%async_computation.21 | async-start | bytes 5242880 | tf_op jit(solution)/shard_map/all_gather | solution.py:52
  710.5 84.1 %copy-start.21 = (bf16[256,1024]{1,0:T(8,128)(2,1)S(1)}, bf16[256,1024]{1,0:T(8,128)(2,1)}, u32[]{:S(2)}) copy-start(bf16[256,1024]{1,0:T(8,128)(2,1)} %copy-done.20) | copy-start | bytes 1572868
  713.2 421.9 %reduce-scatter.15.cloned.1.call-start = ((), (), s32[]{:S(2)}) async-start(), calls=%async_computation.22 | async-start | bytes 5242880 | tf_op jit(solution)/shard_map/reduce_scatter | solution.py:56
  807.3 5.4 copy-start.14
  812.7 5.2 copy-start
  866.9 5.4 copy-start.14
  872.3 5.2 copy-start
  926.5 5.4 copy-start.14
  931.9 5.2 copy-start
  986.0 5.4 copy-start.14
  991.4 5.2 copy-start
  1046.0 13.7 %copy-start.15 = (bf16[1,2048,256]{2,1,0:T(8,128)(2,1)}, bf16[1,2048,256]{2,1,0:T(8,128)(2,1)S(1)}, u32[]{:S(2)}) copy-start(bf16[1,2048,256]{2,1,0:T(8,128)(2,1)S(1)} %reshape.485) | copy-start | bytes 3145732
  1052.8 6.8 copy-start.17
  1059.6 125.8 %reduce-scatter.17.cloned.1.call-start = ((), (), s32[]{:S(2)}) async-start(), calls=%async_computation.23 | async-start | bytes 3538944 | tf_op jit(solution)/shard_map/reduce_scatter | solution.py:277
  1067.1 174.5 %reduce-scatter.21.cloned.1.call-start = ((), (), s32[]{:S(2)}) async-start(), calls=%async_computation.25 | async-start | bytes 4718592 | tf_op jit(solution)/shard_map/reduce_scatter | solution.py:279
  1077.2 219.6 %reduce-scatter.23.cloned.1.call-start = ((), (), s32[]{:S(2)}) async-start(), calls=%async_computation.26 | async-start | bytes 4718592 | tf_op jit(solution)/shard_map/reduce_scatter | solution.py:280
  1087.5 5.6 copy-start.13
  1088.2 54.3 %all-to-all-start.1 = ((bf16[8,64,1024]{2,1,0:T(8,128)(2,1)}), bf16[8,64,1024]{2,1,0:T(8,128)(2,1)}, u32[]{:S(2)}, u32[]{:S(2)}) async-start(bf16[8,64,1024]{2,1,0:T(8,128)(2,1)} %bitcast.29), calls=%async_computation.3 | async-start | bytes 2097152 | tf_op jit(solution)/shard_map/all_to_all | solution.py:289
  1093.0 42.0 %copy-start.2 = (bf16[8,64,1024]{2,1,0:T(8,128)(2,1)S(1)}, bf16[8,64,1024]{2,1,0:T(8,128)(2,1)}, u32[]{:S(2)}) copy-start(bf16[8,64,1024]{2,1,0:T(8,128)(2,1)} %copy-done.1) | copy-start | bytes 3145732
  1093.0 42.0 %copy-start.26 = (f32[1,1024]{1,0:T(1,128)S(1)}, f32[1,1024]{1,0:T(1,128)}, u32[]{:S(2)}) copy-start(f32[1,1024]{1,0:T(1,128)} %copy-done.25) | copy-start | bytes 12292
  1093.0 42.0 %copy-start.28 = (f32[512]{0:T(512)S(1)}, f32[512]{0:T(512)}, u32[]{:S(2)}) copy-start(f32[512]{0:T(512)} %copy-done.27) | copy-start | bytes 6148
  1093.0 42.0 %copy-start.30 = (f32[512]{0:T(512)S(1)}, f32[512]{0:T(512)}, u32[]{:S(2)}) copy-start(f32[512]{0:T(512)} %copy-done.29) | copy-start | bytes 6148
  1093.0 243.6 %reduce-scatter.19.cloned.1.call-start = ((), (), s32[]{:S(2)}) async-start(), calls=%async_computation.24 | async-start | bytes 1179648 | tf_op jit(solution)/shard_map/reduce_scatter | solution.py:278
  1097.6 39.6 %copy-start.40 = (f32[512]{0:T(512)S(1)}, f32[512]{0:T(512)}, u32[]{:S(2)}) copy-start(f32[512]{0:T(512)} %copy-done.39) | copy-start | bytes 6148
  1097.6 39.6 %copy-start.36 = (f32[512]{0:T(512)S(1)}, f32[512]{0:T(512)}, u32[]{:S(2)}) copy-start(f32[512]{0:T(512)} %copy-done.35) | copy-start | bytes 6148
  1097.6 40.5 %copy-start.54 = (f32[512]{0:T(512)S(1)}, f32[512]{0:T(512)}, u32[]{:S(2)}) copy-start(f32[512]{0:T(512)} %get-tuple-element.452) | copy-start | bytes 6148
  1142.6 6.4 copy-start.16
  1142.6 6.4 copy-start.18
  1142.6 85.0 %all-to-all-start.3 = ((bf16[8,64,1024]{2,1,0:T(8,128)(2,1)}), bf16[8,64,1024]{2,1,0:T(8,128)(2,1)}, u32[]{:S(2)}, u32[]{:S(2)}) async-start(bf16[8,64,1024]{2,1,0:T(8,128)(2,1)} %bitcast.172), calls=%async_computation.7 | async-start | bytes 2097152 | tf_op jit(solution)/shard_map/all_to_all | solution.py:290
  1149.5 37.8 %copy-start.41 = (f32[1024]{0:T(1024)S(1)}, f32[1024]{0:T(1024)}, u32[]{:S(2)}) copy-start(f32[1024]{0:T(1024)} %get-tuple-element.350) | copy-start | bytes 12292
  1149.5 37.8 %copy-start.42 = (f32[1024]{0:T(1024)S(1)}, f32[1024]{0:T(1024)}, u32[]{:S(2)}) copy-start(f32[1024]{0:T(1024)} %get-tuple-element.348) | copy-start | bytes 12292
  1149.5 37.8 %copy-start.43 = (f32[1024]{0:T(1024)S(1)}, f32[1024]{0:T(1024)}, u32[]{:S(2)}) copy-start(f32[1024]{0:T(1024)} %get-tuple-element.360) | copy-start | bytes 12292
  1149.5 37.8 %copy-start.44 = (f32[1024]{0:T(1024)S(1)}, f32[1024]{0:T(1024)}, u32[]{:S(2)}) copy-start(f32[1024]{0:T(1024)} %get-tuple-element.346) | copy-start | bytes 12292
  1149.5 37.8 %copy-start.45 = (f32[1024]{0:T(1024)S(1)}, f32[1024]{0:T(1024)}, u32[]{:S(2)}) copy-start(f32[1024]{0:T(1024)} %get-tuple-element.354) | copy-start | bytes 12292
  1149.5 37.8 %copy-start.52 = (f32[1024]{0:T(1024)S(1)}, f32[1024]{0:T(1024)}, u32[]{:S(2)}) copy-start(f32[1024]{0:T(1024)} %get-tuple-element.417) | copy-start | bytes 12292
  1149.6 37.8 %copy-start.53 = (f32[1024]{0:T(1024)S(1)}, f32[1024]{0:T(1024)}, u32[]{:S(2)}) copy-start(f32[1024]{0:T(1024)} %get-tuple-element.419) | copy-start | bytes 12292
  (23 other events, 52.6 us)
Sparse Core Ops, SparseCore 0:
  15.8 29.0 all-gather.9
  47.1 80.4 all-gather.7
  202.7 75.3 reduce-scatter.8
  280.0 28.7 all-gather.13
  310.9 80.3 all-gather.11
  393.2 27.1 all-gather.15
  429.8 76.3 reduce-scatter.10
  518.8 81.2 all-gather.17
  622.5 75.3 reduce-scatter.12
  713.3 81.2 all-gather.19
  1059.7 75.2 reduce-scatter.14
  1138.3 47.0 reduce-scatter.16
  1189.7 51.8 reduce-scatter.20
  1245.4 51.3 reduce-scatter.22
  1300.6 35.9 reduce-scatter.18
where the time goes:
time: 1350 us
  waiting for transfers between devices  749 us (55%)
  matrix products  364 us (27%)
  blocking collectives  73.9 us (5%)
  other arithmetic  70.9 us (5%)
  local copies, waits for them, and re-layouts  40.9 us (3%)
  starting transfers between devices  21 us (2%)
  between operations  15.2 us (1%)
  loops' own time  13.7 us (1%)
    all_gather x2, waiting for transfers between devices, lane_gather(): return lax.all_gather(rows_low, 'tensor', axis=0, tiled=True)  165 us
    all_gather x2, waiting for transfers between devices, grad_gather(): return lax.all_gather(rows_low, 'tensor', axis=0, tiled=True)  163 us
    reduce_scatter x2, waiting for transfers between devices, lane_sum(): lax.psum_scatter(term_fn(jnp.int32(0), rows_here * lax.axis_size('tensor'...  147 us
    reduce_scatter x2, waiting for transfers between devices, grad_sum(): lax.psum_scatter(term_fn(jnp.int32(0), rows_here * lax.axis_size('tensor'...  112 us
    dot_general x4, matrix products, one_step(): jnp.einsum('hqk,qhd->khd', grad_score, query_block, preferred_element_typ...  82 us
    dot_general x4, matrix products, one_step(): jnp.einsum('hqk,khd->qhd', grad_score, key_block, preferred_element_type=...  72.3 us
    reduce_scatter x1, waiting for transfers between devices, body(): lax.psum_scatter(down_grad, 'dp', scatter_dimension=1, tiled=True)  55.1 us
    psum x1, blocking collectives, body(): lax.psum((gain_stack, shift_stack, bias_out_grad, bias_two_grad), ('dp',...  40.2 us
  transfers between devices with their start and end apart: 19, of which 16 were waited for; matrix products, arithmetic and copies ran while one was open for 7% of the time, Pallas kernels for 0%

commit v1 on v0

v1 whole, which is shorter than its diff:
```python
from functools import partial

import jax
import jax.numpy as jnp
from jax import lax
from jax.experimental import pallas as pl
from jax.experimental.pallas import tpu as pltpu
from jax.sharding import PartitionSpec as P

DH = 64
HALF = 1024
NORM_EPS = 1e-05
MASKED_OUT = -1e30
BF, F32 = jnp.bfloat16, jnp.float32
QB = 256


def scaled_norm(values, norm_gain, norm_shift):
    peak = jnp.max(jnp.abs(values), axis=-1, keepdims=True) + NORM_EPS
    scaled = values / peak
    centred = scaled - jnp.mean(scaled, axis=-1, keepdims=True)
    spread = jnp.mean(centred * centred, axis=-1, keepdims=True)
    return centred * lax.rsqrt(spread + NORM_EPS) * norm_gain + norm_shift


def norm_back(values, norm_gain, norm_shift, row_grad):
    result, pull = jax.vjp(scaled_norm, values, norm_gain, norm_shift)
    return pull(row_grad)


def attn_fwd_kernel(qpos_ref, qstart_ref, kpos_ref, q_ref, k_ref, v_ref, o_ref, lse_ref):
    kpos = kpos_ref[...]
    allowed = (kpos <= qpos_ref[...]) & (kpos >= qstart_ref[...])
    bias = jnp.where(allowed, 0.0, MASKED_OUT)
    lane = lax.broadcasted_iota(jnp.int32, (1, 2 * DH), 1)
    wide = lax.broadcasted_iota(jnp.int32, lse_ref.shape, 1)
    stats = jnp.zeros(lse_ref.shape, F32)
    for pair in range(q_ref.shape[1] // (2 * DH)):
        cols = slice(pair * 2 * DH, (pair + 1) * 2 * DH)
        query, key, value = q_ref[:, cols], k_ref[:, cols], v_ref[:, cols]
        total = jnp.zeros(query.shape, F32)
        for side in range(2):
            mine = (lane >= side * DH) & (lane < (side + 1) * DH)
            part = jnp.where(mine, query * 0.125, 0.0).astype(BF)
            score = lax.dot_general(part, key, (((1,), (1,)), ((), ())), preferred_element_type=F32) + bias
            peak = jnp.max(score, axis=-1, keepdims=True)
            expo = jnp.exp(score - peak)
            norm = jnp.sum(expo, axis=-1, keepdims=True)
            prob = (expo * (1.0 / norm)).astype(BF)
            total += jnp.dot(prob, jnp.where(mine, value, jnp.zeros_like(value)), preferred_element_type=F32)
            stats = jnp.where(wide == pair * 2 + side, peak + jnp.log(norm), stats)
        o_ref[:, cols] = total.astype(BF)
    lse_ref[...] = stats


def attn_forward(qpos, qstart, kpos, q, k, v):
    rows, width = q.shape
    col = pl.BlockSpec((QB, 1), lambda i: (i, 0))
    full = pl.BlockSpec((rows, width), lambda i: (0, 0))
    return pl.pallas_call(
        attn_fwd_kernel,
        grid=(rows // QB,),
        in_specs=[col, col, pl.BlockSpec((1, rows), lambda i: (0, 0)), pl.BlockSpec((QB, width), lambda i: (i, 0)), full, full],
        out_specs=[pl.BlockSpec((QB, width), lambda i: (i, 0)), pl.BlockSpec((QB, 128), lambda i: (i, 0))],
        out_shape=[jax.ShapeDtypeStruct((rows, width), BF), jax.ShapeDtypeStruct((rows, 128), F32)],
        cost_estimate=pl.CostEstimate(flops=4 * rows * rows * width, bytes_accessed=8 * rows * width, transcendentals=rows * rows * width // DH),
        compiler_params=pltpu.CompilerParams(vmem_limit_bytes=48 << 20),
        name="attn_fwd",
    )(qpos, qstart, kpos, q, k, v)


def attn_bwd_kernel(qpos_ref, qstart_ref, kpos_ref, lse_ref, q_ref, g_ref, k_ref, v_ref, dq_ref, dk_ref, dv_ref, dk_acc, dv_acc):
    step = pl.program_id(0)

    @pl.when(step == 0)
    def _():
        dk_acc[...] = jnp.zeros_like(dk_acc)
        dv_acc[...] = jnp.zeros_like(dv_acc)

    kpos = kpos_ref[...]
    allowed = (kpos <= qpos_ref[...]) & (kpos >= qstart_ref[...])
    bias = jnp.where(allowed, 0.0, MASKED_OUT)
    lane = lax.broadcasted_iota(jnp.int32, (1, 2 * DH), 1)
    for pair in range(q_ref.shape[1] // (2 * DH)):
        cols = slice(pair * 2 * DH, (pair + 1) * 2 * DH)
        query, grad, key, value = q_ref[:, cols], g_ref[:, cols], k_ref[:, cols], v_ref[:, cols]
        dq = jnp.zeros(query.shape, F32)
        dk = jnp.zeros(key.shape, F32)
        dv = jnp.zeros(key.shape, F32)
        for side in range(2):
            mine = (lane >= side * DH) & (lane < (side + 1) * DH)
            part = jnp.where(mine, query * 0.125, 0.0).astype(BF)
            gpart = jnp.where(mine, grad, jnp.zeros_like(grad))
            score = lax.dot_general(part, key, (((1,), (1,)), ((), ())), preferred_element_type=F32) + bias
            index = pair * 2 + side
            prob = jnp.exp(score - lse_ref[:, index:index + 1])
            gprob = lax.dot_general(gpart, value, (((1,), (1,)), ((), ())), preferred_element_type=F32)
            inner = jnp.sum(prob * gprob, axis=-1, keepdims=True)
            gscore = (prob * (gprob - inner)).astype(BF)
            dq += jnp.dot(gscore, jnp.where(mine, key, jnp.zeros_like(key)), preferred_element_type=F32)
            dk += lax.dot_general(gscore, part, (((0,), (0,)), ((), ())), preferred_element_type=F32)
            dv += lax.dot_general(prob.astype(BF), gpart, (((0,), (0,)), ((), ())), preferred_element_type=F32)
        dq_ref[:, cols] = (dq * 0.125).astype(BF)
        dk_acc[:, cols] += dk
        dv_acc[:, cols] += dv

    @pl.when(step == pl.num_programs(0) - 1)
    def _():
        dk_ref[...] = dk_acc[...].astype(BF)
        dv_ref[...] = dv_acc[...].astype(BF)


def attn_backward(qpos, qstart, kpos, lse, q, grad, k, v):
    rows, width = q.shape
    col = pl.BlockSpec((QB, 1), lambda i: (i, 0))
    blk = pl.BlockSpec((QB, width), lambda i: (i, 0))
    full = pl.BlockSpec((rows, width), lambda i: (0, 0))
    wide = jax.ShapeDtypeStruct((rows, width), BF)
    return pl.pallas_call(
        attn_bwd_kernel,
        grid=(rows // QB,),
        in_specs=[col, col, pl.BlockSpec((1, rows), lambda i: (0, 0)), pl.BlockSpec((QB, 128), lambda i: (i, 0)), blk, blk, full, full],
        out_specs=[blk, full, full],
        out_shape=[wide, wide, wide],
        scratch_shapes=[pltpu.VMEM((rows, width), F32), pltpu.VMEM((rows, width), F32)],
        cost_estimate=pl.CostEstimate(flops=10 * rows * rows * width, bytes_accessed=14 * rows * width, transcendentals=rows * rows * width // DH),
        compiler_params=pltpu.CompilerParams(vmem_limit_bytes=48 << 20),
        name="attn_bwd",
    )(qpos, qstart, kpos, lse, q, grad, k, v)


def swap_dp(x, bit):
    n = lax.axis_size("dp")
    return lax.ppermute(x, "dp", [(i, i ^ bit) for i in range(n)])


def turn(x, shift):
    n = lax.axis_size("tensor")
    return lax.ppermute(x, "tensor", [(i, (i + shift) % n) for i in range(n)])


def chip_bits():
    n = lax.axis_size("dp")
    return [1 << b for b in range(1, n.bit_length() - 1)]


def core_pair(mine, other):
    core = lax.axis_index("dp") % 2
    return jnp.where(core == 0, jnp.stack([mine, other]), jnp.stack([other, mine]))


def gather_weights(mine, other):
    pair = core_pair(mine, swap_dp(other, 1)).reshape(2 * mine.shape[0], mine.shape[1])
    lanes = lax.axis_size("tensor")
    column = jnp.stack([pair] + [turn(pair, k) for k in range(1, lanes)])
    bits = chip_bits()
    if len(bits) == 2:
        low, high = bits
        first, second = swap_dp(column, low), swap_dp(column, high)
        mid = lanes // 2
        far = jnp.concatenate([swap_dp(first[:mid], high), swap_dp(second[mid:], low)])
        return {0: column, low: first, high: second, low | high: far}
    blocks = {0: column}
    for bit in bits:
        got = swap_dp(jnp.stack([blocks[m] for m in sorted(blocks)]), bit)
        blocks.update({m | bit: got[i] for i, m in enumerate(sorted(blocks))})
    return blocks


def weight_of(blocks, start, width):
    out = []
    for mask in sorted(blocks):
        part = blocks[mask][:, :, start:start + width]
        out.append(jnp.concatenate([part[k] for k in range(part.shape[0])], axis=1))
    return jnp.concatenate(out, axis=0)


def scatter_grads(parts):
    lanes = lax.axis_size("tensor")
    bits = chip_bits()
    count = 1 << len(bits)
    feats = parts[0].shape[0]
    per = feats // count

    def block(mask_index, k):
        cut = []
        for p in parts:
            w = p.shape[1] // lanes
            cut.append(p[mask_index * per:(mask_index + 1) * per, k * w:(k + 1) * w])
        return jnp.concatenate(cut, axis=1) if len(cut) > 1 else cut[0]

    def col(mask_index, ks):
        return jnp.stack([block(mask_index, k) for k in ks])

    if len(bits) == 2:
        low, high = bits
        mid = lanes // 2
        ka, kb = list(range(mid)), list(range(mid, lanes))
        sent_a = jnp.stack([col(1, ka), col(3, ka)]).astype(BF)
        sent_b = jnp.stack([col(2, kb), col(3, kb)]).astype(BF)
        got_a, got_b = swap_dp(sent_a, low), swap_dp(sent_b, high)
        pass_a = (col(2, ka) + got_a[1].astype(F32)).astype(BF)
        pass_b = (col(1, kb) + got_b[1].astype(F32)).astype(BF)
        end_a, end_b = swap_dp(pass_a, high), swap_dp(pass_b, low)
        keep_a = col(0, ka) + got_a[0].astype(F32) + end_a.astype(F32)
        keep_b = col(0, kb) + got_b[0].astype(F32) + end_b.astype(F32)
        total = [keep_a[i] for i in range(mid)] + [keep_b[i] for i in range(lanes - mid)]
    else:
        sums = {m: col(m, range(lanes)) for m in range(count)}
        for level in reversed(range(len(bits))):
            keys = [m for m in sorted(sums) if m >> level & 1]
            got = swap_dp(jnp.stack([sums[m] for m in keys]).astype(BF), bits[level])
            sums = {m ^ (1 << level): sums[m ^ (1 << level)] + got[i].astype(F32) for i, m in enumerate(keys)}
        total = [sums[0][k] for k in range(lanes)]
    own = total[0]
    for k in range(1, lanes):
        own = own + turn(total[k].astype(BF), -k).astype(F32)
    rows = own.shape[0] // 2
    core = lax.axis_index("dp") % 2
    mine = lax.dynamic_slice_in_dim(own, core * rows, rows, 0)
    other = lax.dynamic_slice_in_dim(own, (1 - core) * rows, rows, 0)
    return core_pair(mine, swap_dp(other.astype(BF), 1).astype(F32))


def deal_perms(n_dp):
    near, far = [], []
    for chip in range(n_dp // 2):
        for c in range(2):
            for j in range(4):
                source = (chip * 2 + c) * 4 + j
                near.append((source, (chip * 2 + j % 2) * 4 + 2 * c + j // 2))
                far.append((source, (chip * 2 + j % 2) * 4 + 2 * c + 1 - j // 2))
    return near, far


def feature_turn(x):
    n = lax.axis_size("dp") // 2
    chip = lax.axis_index("dp") // 2
    lead = x.shape[:-1]
    width = x.shape[-1] // n
    bits = n.bit_length() - 1
    y = x.reshape(lead + (2,) * bits + (width,))
    for b in range(bits):
        axis = len(lead) + bits - 1 - b
        y = jnp.where((chip >> b) & 1 == 1, jnp.flip(y, axis), y)
    return y.reshape(x.shape)


def body(tokens, cotangent, lengths, deal, w_qkv, w_o, w_1, w_2, b_qv, b_o, b_1, b_2, ln_gain, ln_bias):
    n_dp, lanes = lax.axis_size("dp"), lax.axis_size("tensor")
    dp, lane = lax.axis_index("dp"), lax.axis_index("tensor")
    core, chip = dp % 2, dp // 2
    rows = tokens.shape[0]
    both = ("dp", "tensor")
    near, far = deal_perms(n_dp)
    back_near, back_far = [(b, a) for a, b in near], [(b, a) for a, b in far]

    per = lengths.shape[0] // n_dp

    def pack_ends(pack):
        picked = lax.dynamic_slice_in_dim(deal, pack * per, per)
        lookup = picked[:, None] == jnp.arange(lengths.shape[0], dtype=jnp.int32)[None, :]
        lens = jnp.sum(jnp.where(lookup, lengths[None, :], 0), axis=1)
        ends = jnp.sum(jnp.where(jnp.arange(per)[:, None] >= jnp.arange(per)[None, :], lens[None, :], 0), axis=1)
        return ends, ends - lens, jnp.sum(jnp.where(lens == HALF, ends - lens, 0))

    half = lane % 2
    ends, starts, cut = pack_ends(chip * 2 + lane // 2)
    _, _, cut_home = pack_ends(dp)
    index = jnp.arange(rows, dtype=jnp.int32)
    slots = jnp.concatenate([core * rows + index, (1 - core) * rows + index])
    place = jnp.where(slots >= cut, slots + HALF * half, slots + HALF * (1 - half))
    seg_start = jnp.max(jnp.where(place[:, None] >= starts[None, :], starts[None, :], 0), axis=1)
    qpos, qstart, kpos = place[:, None], seg_start[:, None], place[None, :]
    keep = ((core * rows + index) >= cut)[:, None]
    keep_home = (((lane % 2) * rows + index) >= cut_home)[:, None]

    def deal_in(x):
        moved = lax.all_to_all(x, "dp", split_axis=0, concat_axis=0, tiled=True)
        return jnp.where(keep, lax.ppermute(moved, both, near), lax.ppermute(moved, both, far))

    def deal_out(x):
        moved = jnp.where(keep_home, lax.ppermute(x, both, back_near), lax.ppermute(x, both, back_far))
        return lax.all_to_all(moved, "dp", split_axis=0, concat_axis=0, tiled=True)

    def halves(x):
        w = x.shape[-1] // 2
        return (lax.dynamic_slice_in_dim(x, core * w, w, x.ndim - 1), lax.dynamic_slice_in_dim(x, (1 - core) * w, w, x.ndim - 1))

    qm, qo = halves(w_qkv)
    flat = lambda x: jnp.concatenate([x[0], x[1], x[2]], axis=1)
    qkv_blocks = gather_weights(flat(qm), flat(qo))
    om, oo = halves(w_o.T)
    um, uo = halves(w_1)
    dm, do = halves(w_2.T)
    up_blocks = gather_weights(jnp.concatenate([om, um], axis=1), jnp.concatenate([oo, uo], axis=1))
    down_blocks = gather_weights(dm, do)
    hw, fw = om.shape[1], um.shape[1]

    biases = lax.all_gather(jnp.concatenate([b_qv.reshape(-1), b_1]), "tensor")
    order = (lane - jnp.arange(lanes)) % lanes
    biases = jnp.take(biases, order, axis=0)
    cut_bias = lambda x: lax.dynamic_slice_in_dim(x, core * (x.shape[1] // 2), x.shape[1] // 2, 1).reshape(-1)
    nq = b_qv.shape[1]
    bias_q, bias_v, bias_1 = cut_bias(biases[:, :nq]), cut_bias(biases[:, nq:2 * nq]), cut_bias(biases[:, 2 * nq:])
    gain, shift = feature_turn(ln_gain), feature_turn(ln_bias)
    bias_o, bias_2 = feature_turn(b_o[None])[0], feature_turn(b_2[None])[0]

    def join(x):
        return jnp.concatenate([x, swap_dp(x, 1)], axis=0)

    def fold(x):
        return x[:rows] + swap_dp(x[rows:].astype(BF), 1).astype(F32)

    hidden = feature_turn(deal_in(tokens)).astype(F32)
    normed_in = join(scaled_norm(hidden, gain[0], shift[0]).astype(BF))
    weights_q, weights_k, weights_v = (weight_of(qkv_blocks, i * hw, hw) for i in range(3))
    mm = partial(jnp.dot, preferred_element_type=F32)
    mm_t = lambda a, b: lax.dot_general(a, b, (((1,), (1,)), ((), ())), preferred_element_type=F32)
    mm_g = lambda a, b: lax.dot_general(a, b, (((0,), (0,)), ((), ())), preferred_element_type=F32)
    q = (mm(normed_in, weights_q) + bias_q).astype(BF)
    k = mm(normed_in, weights_k).astype(BF)
    v = (mm(normed_in, weights_v) + bias_v).astype(BF)
    heads_out, lse = attn_forward(qpos, qstart, kpos, q, k, v)
    weights_o = weight_of(up_blocks, 0, hw)
    attn_out = fold(mm_t(heads_out, weights_o)) + bias_o
    first_sum = hidden + scaled_norm(attn_out, gain[1], shift[1])
    normed_mid = join(scaled_norm(first_sum, gain[2], shift[2]).astype(BF))
    weights_1 = weight_of(up_blocks, hw, fw)
    pre_act = mm(normed_mid, weights_1) + bias_1
    act = jax.nn.gelu(pre_act, approximate=False).astype(BF)
    weights_2 = weight_of(down_blocks, 0, fw)
    ffn_out = fold(mm_t(act, weights_2)) + bias_2
    result = first_sum + scaled_norm(ffn_out, gain[3], shift[3])
    output = deal_out(feature_turn(result.astype(BF)))

    grad_result = feature_turn(deal_in(cotangent)).astype(F32)
    grad_ffn, gain_3, shift_3 = norm_back(ffn_out, gain[3], shift[3], grad_result)
    grad_ffn_low = grad_ffn.astype(BF)
    bias_2_grad = jnp.sum(grad_ffn_low.astype(F32), axis=0)
    grad_ffn_full = join(grad_ffn_low)
    grad_act = mm(grad_ffn_full, weights_2)
    down_grad = scatter_grads([mm_g(grad_ffn_full, act)])
    _, gelu_pull = jax.vjp(partial(jax.nn.gelu, approximate=False), pre_act)
    grad_pre = gelu_pull(grad_act)[0].astype(BF)
    bias_1_grad = jnp.sum(grad_pre.astype(F32), axis=0)
    grad_mid = fold(mm_t(grad_pre, weights_1))
    up_part = mm_g(normed_mid, grad_pre)
    grad_first_part, gain_2, shift_2 = norm_back(first_sum, gain[2], shift[2], grad_mid)
    grad_first = grad_result + grad_first_part
    grad_attn, gain_1, shift_1 = norm_back(attn_out, gain[1], shift[1], grad_first)
    grad_attn_low = grad_attn.astype(BF)
    bias_o_grad = jnp.sum(grad_attn_low.astype(F32), axis=0)
    grad_attn_full = join(grad_attn_low)
    grad_heads = mm(grad_attn_full, weights_o).astype(BF)
    out_up_grad = scatter_grads([mm_g(grad_attn_full, heads_out), up_part])
    grad_q, grad_k, grad_v = attn_backward(qpos, qstart, kpos, lse, q, grad_heads, k, v)
    bias_q_grad = jnp.sum(grad_q.astype(F32), axis=0)
    bias_v_grad = jnp.sum(grad_v.astype(F32), axis=0)
    grad_in = fold(mm_t(grad_q, weights_q) + mm_t(grad_k, weights_k) + mm_t(grad_v, weights_v))
    grad_hidden_part, gain_0, shift_0 = norm_back(hidden, gain[0], shift[0], grad_in)
    input_grad = deal_out(feature_turn((grad_first + grad_hidden_part).astype(BF)))
    qkv_grad = scatter_grads([mm_g(normed_in, g) for g in (grad_q, grad_k, grad_v)])

    def by_lane(x):
        x = jnp.take(x.reshape(lanes, -1), order, axis=0)
        both_halves = jnp.stack([jnp.where(core == 0, x, 0.0), jnp.where(core == 1, x, 0.0)], axis=1)
        return both_halves.reshape(-1)

    stack = jnp.stack([gain_0, gain_1, gain_2, gain_3, shift_0, shift_1, shift_2, shift_3, bias_o_grad, bias_2_grad])
    vector = jnp.concatenate([feature_turn(stack).reshape(-1), by_lane(bias_q_grad), by_lane(bias_v_grad), by_lane(bias_1_grad)])
    vector = lax.psum(vector, both)
    d = tokens.shape[1]
    gain_total, shift_total = vector[:4 * d].reshape(4, d), vector[4 * d:8 * d].reshape(4, d)
    bias_o_total, bias_2_total = vector[8 * d:9 * d], vector[9 * d:10 * d]
    e = d
    own = lambda x: lax.dynamic_slice_in_dim(x.reshape(lanes, -1), lane, 1, 0)[0]
    bias_qv_total = jnp.stack([own(vector[10 * d:10 * d + e]), own(vector[10 * d + e:10 * d + 2 * e])])
    bias_1_total = own(vector[10 * d + 2 * e:])

    spread = lambda x: jnp.concatenate([x[0], x[1]], axis=-1)
    qkv_out = jnp.stack([spread(qkv_grad[:, :, i * hw:(i + 1) * hw]) for i in range(3)])
    return (
        output, input_grad, qkv_out,
        spread(out_up_grad[:, :, :hw]).T, spread(out_up_grad[:, :, hw:]), spread(down_grad).T,
        bias_qv_total, bias_o_total, bias_1_total, bias_2_total, gain_total, shift_total,
    )


def solution(mesh):
    rows = P(("dp", "tensor"), None)
    weights = (P(None, "dp", "tensor"), P("tensor", "dp"), P("dp", "tensor"), P("tensor", "dp"))
    vectors = (P(None, "tensor"), P(), P("tensor"), P(), P(), P())
    return jax.shard_map(
        body,
        mesh=mesh,
        in_specs=(rows, rows, P(), P()) + weights + vectors,
        out_specs=(rows, rows) + weights + vectors,
        check_vma=False,
    )
```

time: 1350 us -> 1010 us (0.75); the launches traced: 1350 us -> 993 us
  waiting for transfers between devices: 749 us -> 339 us
  matrix products: 364 us -> 155 us
  starting transfers between devices: 21 us -> 136 us
  other arithmetic: 70.9 us -> 164 us
  local copies, waits for them, and re-layouts: 40.9 us -> 114 us
  blocking collectives: 73.9 us -> 10.5 us
  Pallas kernels: 0 us -> 54.8 us
  loops' own time: 13.7 us -> 0 us
    reduce_scatter x8 -> x0, waiting for transfers between devices: 384 us -> none  [the longest x2 147 us: lane_sum(): lax.psum_scatter(term_fn(jnp.int32(0), rows_here * lax.axis_size('tensor'...]
    all_gather x7 -> x0, waiting for transfers between devices: 354 us -> none  [the longest x2 165 us: lane_gather(): return lax.all_gather(rows_low, 'tensor', axis=0, tiled=True)]
    dot_general x40 -> x18, matrix products: 364 us -> 155 us  [the longest x6 66.6 us: body(): lax.dot_general(a, b, (((1,), (1,)), ((), ())), preferred_element_type=F32)]
    ppermute x0 -> x64, waiting for transfers between devices: none -> 164 us  [the longest x18 51.9 us: turn(): return lax.ppermute(x, 'tensor', [(i, (i + shift) % n) for i in range(n)])]
    ppermute x0 -> x64, starting transfers between devices: none -> 116 us  [the longest x38 65 us: swap_dp(): return lax.ppermute(x, 'dp', [(i, i ^ bit) for i in range(n)])]
    psum x0 -> x1, waiting for transfers between devices: none -> 113 us  [body(): vector = lax.psum(vector, both)]
    concatenate x0 -> x6, other arithmetic: none -> 60.3 us  [the longest x1 57.5 us: weight_of(): return jnp.concatenate(out, axis=0)]
    psum x2 -> x0, blocking collectives: 59.6 us -> none  [the longest x1 40.2 us: body(): lax.psum((gain_stack, shift_stack, bias_out_grad, bias_two_grad), ('dp',...]
  transfers between devices with their start and end apart: 19 -> 69, of which waited for: 16 -> 22; matrix products, arithmetic and copies ran while one was open for 7% -> 33% of each run, Pallas kernels for 0% -> 6%
where the time goes in v1:
time: 1010 us; the launch traced here: 993 us
  waiting for transfers between devices  339 us (34%)
  other arithmetic  164 us (16%)
  matrix products  155 us (15%)
  starting transfers between devices  136 us (13%)
  local copies, waits for them, and re-layouts  114 us (11%)
  Pallas kernels  54.8 us (5%)
  between operations  19 us (2%)
  blocking collectives  10.5 us (1%)
    psum x1, waiting for transfers between devices, body(): vector = lax.psum(vector, both)  113 us
    dot_general x6, matrix products, body(): lax.dot_general(a, b, (((1,), (1,)), ((), ())), preferred_element_type=F32)  66.6 us
    ppermute x38, starting transfers between devices, swap_dp(): return lax.ppermute(x, 'dp', [(i, i ^ bit) for i in range(n)])  65 us
    concatenate x1, other arithmetic, weight_of(): return jnp.concatenate(out, axis=0)  57.5 us
    ppermute x18, waiting for transfers between devices, turn(): return lax.ppermute(x, 'tensor', [(i, (i + shift) % n) for i in range(n)])  51.9 us
    all_to_all x2, waiting for transfers between devices, deal_in(): moved = lax.all_to_all(x, 'dp', split_axis=0, concat_axis=0, tiled=True)  45.3 us
    ppermute x18, starting transfers between devices, turn(): return lax.ppermute(x, 'tensor', [(i, (i + shift) % n) for i in range(n)])  36.1 us
    ppermute x2, waiting for transfers between devices, deal_out(): lax.ppermute(x, both, back_near)  35.9 us
  transfers between devices with their start and end apart: 69, of which 22 were waited for; matrix products, arithmetic and copies ran while one was open for 33% of the time, Pallas kernels for 6%

profile of v1, /device:TPU:1, one launch (start us, length us, event | category | flops | bytes accessed | tf_op | source)
XLA Modules:
  0.0 992.8 jit_solution(11093665700394440507)
XLA Ops:
  9.3 5.4 all-to-all-start
  20.0 10.5 %all-gather.1 = f32[4,1,1536]{2,1,0:T(1,128)S(1)} all-gather(f32[1,1,1536]{2,1,0:T(1,128)S(1)} %reshape.801), channel_id=2, replica_groups=mesh['dp'=8,'tensor'=4] {'tensor'}, dimensions={0}, use_global_device_ids=true | all-gather | bytes 30720 | tf_op jit(solution)/shard_map/all_gather | solution.py:300
  55.0 8.4 collective-permute-done.5
  64.1 12.1 %collective-permute-start.13 = (bf16[256,640]{1,0:T(8,128)(2,1)S(1)}, bf16[256,640]{1,0:T(8,128)(2,1)S(1)}, u32[]{:S(2)}, u32[]{:S(2)}) collective-permute-start(bf16[256,640]{1,0:T(8,128)(2,1)S(1)} %bitcast.652), channel_id=1, source_target_pairs={{0,2},{1,3},{2,0},{3,1},{4,6},{5,7},{6,4},{7,5},{8,10},{9,11},{10,... | collective-permute-start | bytes 983048 | tf_op jit(solution)/shard_map/ppermute | solution.py:139
  76.2 3.6 collective-permute-start.14
  81.5 13.7 %collective-permute-done.23 = bf16[256,512]{1,0:T(8,128)(2,1)S(1)} collective-permute-done((bf16[256,512]{1,0:T(8,128)(2,1)S(1)}, bf16[256,512]{1,0:T(8,128)(2,1)S(1)}, u32[]{:S(2)}, u32[]{:S(2)}) %collective-permute-start.23) | collective-permute-done | bytes 262176 | tf_op jit(solution)/shard_map/ppermute | solution.py:139
  99.2 8.7 collective-permute-done.13
  113.2 4.6 all-to-all-start.2
  129.7 45.3 %all-to-all-done.2 = bf16[8,64,1024]{2,1,0:T(8,128)(2,1)S(1)} async-done(((bf16[8,64,1024]{2,1,0:T(8,128)(2,1)}), bf16[8,64,1024]{2,1,0:T(8,128)(2,1)S(1)}, u32[]{:S(2)}, u32[]{:S(2)}) %all-to-all-start.2) | async-done | bytes 1048608 | tf_op jit(solution)/shard_map/all_to_all | solution.py:279
  178.2 4.5 collective-permute-start
  184.3 4.2 collective-permute-start.32
  192.5 2.2 slice_bitcast_fusion.50
  204.3 22.6 %collective-permute-done.1 = bf16[512,1024]{0,1:T(8,128)(2,1)S(1)} collective-permute-done((bf16[512,1024]{0,1:T(8,128)(2,1)}, bf16[512,1024]{0,1:T(8,128)(2,1)S(1)}, u32[]{:S(2)}, u32[]{:S(2)}) %collective-permute-start.1) | collective-permute-done | bytes 1048608 | tf_op jit(solution)/shard_map/ppermute | solution.py:280
  227.2 12.5 %collective-permute-done.32 = bf16[512,1024]{0,1:T(8,128)(2,1)S(1)} collective-permute-done((bf16[512,1024]{0,1:T(8,128)(2,1)S(1)}, bf16[512,1024]{0,1:T(8,128)(2,1)S(1)}, u32[]{:S(2)}, u32[]{:S(2)}) %collective-permute-start.32) | collective-permute-done | bytes 1048608 | tf_op jit(solution)/shard_map/ppermute | solution.py:280
  241.1 9.8 collective-permute-done.33
  258.1 26.4 %collective-permute-start.2 = (bf16[512,1024]{0,1:T(8,128)(2,1)S(1)}, bf16[512,1024]{0,1:T(8,128)(2,1)}, u32[]{:S(2)}, u32[]{:S(2)}) collective-permute-start(bf16[512,1024]{0,1:T(8,128)(2,1)S(1)} %add_convert_fusion.5), channel_id=1, source_target_pairs={{0,4},{4,0},{8,12},{12,8},{16,20},{20,16},{24,28},{28,24},{1,5},{5... | collective-permute-start | bytes 3145736 | tf_op jit(solution)/shard_map/ppermute | solution.py:134
  289.7 2.6 convolution_convert_fusion.1.k_ref
  292.6 2.8 add_convert_fusion.3.v_ref
  295.5 2.8 add_convert_fusion.4.q_ref
  298.4 20.5 %attn_fwd.1 = (bf16[1024,512]{1,0:T(8,128)(2,1)S(1)}, f32[1024,128]{1,0:T(8,128)S(1)}) custom-call(s32[1024,1]{1,0:T(8,128)S(1)} %select_n.475.qpos_ref, s32[1024,1]{1,0:T(8,128)S(1)} %copy.194.qstart_ref, s32[1,1024]{1,0:T(1,128)S(1)} %compare_select_fusion.kpos_ref, bf16[1024,512]{1,0:T(8,128)(2,1)S(1)} %add_convert_fusion.4.q_ref, ...), custom_call_target="tpu_custom_call" | custom-call | flops 2147483648 | bytes 4194304 | tf_op jit(solution)/shard_map/attn_fwd/pallas_call | solution.py:60
  319.0 4.0 fusion.95
  331.5 57.5 %maximum_maximum_fusion = bf16[1024,2048]{1,0:T(8,128)(2,1)S(1)} fusion(bf16[256,512]{1,0:T(8,128)(2,1)S(1)} %get-tuple-element.277, bf16[256,512]{1,0:T(8,128)(2,1)S(1)} %get-tuple-element.276, bf16[256,512]{1,0:T(8,128)(2,1)S(1)} %get-tuple-element.275, bf16[256,512]{1,0:T(8,128)(2,1)S(1)} %get-tuple-element.274, ...), kind=kLoop, calls=%fused_computation.22 | loop fusion | flops 67108864 | bytes 8388608 | tf_op jit(solution)/shard_map/concatenate | solution.py:175
  389.2 24.4 %multiply_convert_fusion = (bf16[1024,2048]{1,0:T(8,128)(2,1)S(1)}, f32[1024,2048]{1,0:T(8,128)}, f32[1024,2048]{1,0:T(8,128)}) fusion(f32[2048]{0:T(1024)S(1)} %bitcast.732, bf16[1024,2048]{1,0:T(8,128)(2,1)S(1)} %maximum_maximum_fusion, bf16[512,1024]{0,1:T(8,128)(2,1)S(1)} %collective-permute-done.20, bf16[512,1024]{0,1:T(8,128)(2,1)S(1)} %add_convert_fusion.2), kind=kOutput, calls=%fused_computation.8 | convolution fusion | flops 4437573632 | bytes 27271168 | tf_op jit(solution)/shard_map/dot_general | solution.py:330
  413.8 47.1 %fusion.101 = f32[1024,1024]{0,1:T(8,128)} fusion(bf16[1024,2048]{1,0:T(8,128)(2,1)S(1)} %get-tuple-element.115, bf16[256,512]{1,0:T(8,128)(2,1)S(1)} %get-tuple-element.289, bf16[256,512]{1,0:T(8,128)(2,1)S(1)} %get-tuple-element.288, bf16[256,512]{1,0:T(8,128)(2,1)S(1)} %get-tuple-element.287, bf16[256,512]{1,0:T(8,128)(2,1)S(1)} %get-tuple-element.286, ...), kind=kOutput, calls=%fused_computation.563 | convolution fusion | flops 4362076160 | bytes 12582912 | tf_op jit(solution)/shard_map/dot_general | solution.py:319
  461.0 2.7 slice.1825
  466.7 2.3 abs_reduce_fusion
  472.5 3.2 convert_reduce_fusion.4
  484.2 26.8 %convert_reduce_fusion = (f32[2048]{0:T(1024)S(1)}, bf16[1024,2048]{1,0:T(8,128)(2,1)S(1)}) fusion(f32[1024,2048]{1,0:T(8,128)} %get-tuple-element.116, bf16[256,512]{1,0:T(8,128)(2,1)} %copy-done.91, bf16[256,512]{1,0:T(8,128)(2,1)} %copy-done.90, bf16[256,512]{1,0:T(8,128)(2,1)S(1)} %copy-done.89, bf16[256,512]{1,0:T(8,128)(2,1)S(1)} %get-tuple-element.286, ...), kind=kOutput, calls=%fused_computation.6 | convolution fusion | flops 4401920000 | bytes 27279360 | tf_op jit(solution)/shard_map/dot_general | solution.py:342
  511.0 4.5 fusion.131
  518.7 6.9 collective-permute-start.35
  526.3 7.1 fusion.130
  537.0 6.3 fusion.128
  548.9 2.6 multiply_reduce_fusion
  555.4 2.4 fusion.102
  563.3 8.9 collective-permute-done.60
  576.7 2.4 convert_reduce_fusion.5
  579.1 12.2 %collective-permute-done.61 = bf16[256,512]{1,0:T(8,128)(2,1)S(1)} collective-permute-done((bf16[256,512]{1,0:T(8,128)(2,1)S(1)}, bf16[256,512]{1,0:T(8,128)(2,1)S(1)}, u32[]{:S(2)}, u32[]{:S(2)}) %collective-permute-start.61) | collective-permute-done | bytes 262176 | tf_op jit(solution)/shard_map/ppermute | solution.py:139
  591.3 3.7 collective-permute-start.36
  599.6 3.8 convolution_convert_fusion.g_ref
  603.6 34.3 %attn_bwd.1 = (bf16[1024,512]{1,0:T(8,128)(2,1)S(1)}, bf16[1024,512]{1,0:T(8,128)(2,1)S(1)}, bf16[1024,512]{1,0:T(8,128)(2,1)S(1)}) custom-call(s32[1024,1]{1,0:T(8,128)S(1)} %copy-done.3, s32[1024,1]{1,0:T(8,128)S(1)} %copy-done.1, s32[1,1024]{1,0:T(1,128)S(1)} %copy-done.5, f32[1024,128]{1,0:T(8,128)S(1)} %get-tuple-element.19.lse_ref, ...), custom_call_target="tpu_custom_call" | custom-call | flops 5368709120 | bytes 7340032 | tf_op jit(solution)/shard_map/attn_bwd/pallas_call | solution.py:119
  638.1 3.4 fusion.94
  642.1 2.4 fusion.96
  644.8 5.1 add_add_fusion
  649.9 2.8 slice.1823
  655.7 4.2 fusion.129
  663.5 2.3 fusion.113
  680.5 2.6 fusion.127
  683.2 2.5 fusion.126
  685.8 2.5 fusion.125
  715.1 2.3 pad_maximum_fusion.14
  725.4 3.2 multiply_reduce_fusion.2
  730.7 2.8 fusion.105
  737.7 113.4 %all-reduce.2.cloned.1.call-done = f32[16384]{0:T(1024)} async-done(((f32[16384]{0:T(1024)}), f32[16384]{0:T(1024)}) %all-reduce.2.cloned.1.call-update) | async-done | bytes 65552 | tf_op jit(solution)/shard_map/psum | solution.py:372
  858.2 7.8 collective-permute-done.41
  867.2 2.4 collective-permute-start.46
  873.1 8.9 collective-permute-done.45
  889.0 11.5 %collective-permute-done.52 = bf16[2,256,640]{2,1,0:T(8,128)(2,1)S(1)} collective-permute-done((bf16[2,256,640]{2,1,0:T(8,128)(2,1)S(1)}, bf16[2,256,640]{2,1,0:T(8,128)(2,1)S(1)}, u32[]{:S(2)}, u32[]{:S(2)}) %collective-permute-start.52) | collective-permute-done | bytes 655392 | tf_op jit(solution)/shard_map/ppermute | solution.py:134
  903.0 2.6 collective-permute-start.53
  907.6 3.3 collective-permute-start.50
  910.9 35.9 %collective-permute-done.38 = bf16[512,1024]{0,1:T(8,128)(2,1)S(1)} collective-permute-done((bf16[512,1024]{0,1:T(8,128)(2,1)S(1)}, bf16[512,1024]{0,1:T(8,128)(2,1)S(1)}, u32[]{:S(2)}, u32[]{:S(2)}) %collective-permute-start.38) | collective-permute-done | bytes 1048608 | tf_op jit(solution)/shard_map/ppermute | solution.py:283
  949.8 3.5 all-to-all-start.1
  959.7 5.6 all-to-all-done.1
  965.3 6.5 all-to-all-start.3
  973.7 10.1 %all-to-all-done.3 = bf16[8,64,1024]{2,1,0:T(8,128)(2,1)S(1)} async-done(((bf16[8,64,1024]{2,1,0:T(8,128)(2,1)}), bf16[8,64,1024]{2,1,0:T(8,128)(2,1)S(1)}, u32[]{:S(2)}, u32[]{:S(2)}) %all-to-all-start.3) | async-done | bytes 1048608 | tf_op jit(solution)/shard_map/all_to_all | solution.py:284
  (1008 shorter events, 239.6 us)
Async XLA Ops:
  9.2 32.6 %collective-permute-start.3 = (bf16[128,384]{0,1:T(8,128)(2,1)}, bf16[128,384]{0,1:T(8,128)(2,1)}, u32[]{:S(2)}, u32[]{:S(2)}) collective-permute-start(bf16[128,384]{0,1:T(8,128)(2,1)} %pad_maximum_fusion.24), channel_id=1, source_target_pairs={{0,4},{4,0},{8,12},{12,8},{16,20},{20,16},{24,28},{28,24},{1,5},{5... | collective-permute-start | bytes 294920 | tf_op jit(solution)/shard_map/ppermute | solution.py:134
  9.3 103.9 %all-to-all-start = ((bf16[8,64,1024]{2,1,0:T(8,128)(2,1)}), bf16[8,64,1024]{2,1,0:T(8,128)(2,1)S(1)}, u32[]{:S(2)}, u32[]{:S(2)}) async-start(bf16[8,64,1024]{2,1,0:T(8,128)(2,1)} %bitcast.672), calls=%async_computation | async-start | bytes 2097152 | tf_op jit(solution)/shard_map/all_to_all | solution.py:279
  15.6 34.1 %collective-permute-start.11 = (bf16[128,640]{1,0:T(8,128)(2,1)}, bf16[128,640]{1,0:T(8,128)(2,1)}, u32[]{:S(2)}, u32[]{:S(2)}) collective-permute-start(bf16[128,640]{1,0:T(8,128)(2,1)} %pad_maximum_fusion.23), channel_id=1, source_target_pairs={{0,4},{4,0},{8,12},{12,8},{16,20},{20,16},{24,28},{28,24},{1,5},{5... | collective-permute-start | bytes 491528 | tf_op jit(solution)/shard_map/ppermute | solution.py:134
  16.4 30.8 %collective-permute-start.21 = (bf16[128,512]{1,0:T(8,128)(2,1)}, bf16[128,512]{1,0:T(8,128)(2,1)}, u32[]{:S(2)}, u32[]{:S(2)}) collective-permute-start(bf16[128,512]{1,0:T(8,128)(2,1)} %bitcast.116), channel_id=1, source_target_pairs={{0,4},{4,0},{8,12},{12,8},{16,20},{20,16},{24,28},{28,24},{1,5},{5... | collective-permute-start | bytes 393224 | tf_op jit(solution)/shard_map/ppermute | solution.py:134
  43.0 9.4 collective-permute-start.4
  44.3 19.1 %collective-permute-start.5 = (bf16[256,384]{1,0:T(8,128)(2,1)S(1)}, bf16[256,384]{1,0:T(8,128)(2,1)S(1)}, u32[]{:S(2)}, u32[]{:S(2)}) collective-permute-start(bf16[256,384]{1,0:T(8,128)(2,1)S(1)} %bitcast.657), channel_id=1, source_target_pairs={{0,2},{1,3},{2,0},{3,1},{4,6},{5,7},{6,4},{7,5},{8,10},{9,11},{10,... | collective-permute-start | bytes 589832 | tf_op jit(solution)/shard_map/ppermute | solution.py:139
  46.4 17.7 %collective-permute-start.6 = (bf16[256,384]{1,0:T(8,128)(2,1)S(1)}, bf16[256,384]{1,0:T(8,128)(2,1)S(1)}, u32[]{:S(2)}, u32[]{:S(2)}) collective-permute-start(bf16[256,384]{1,0:T(8,128)(2,1)S(1)} %bitcast.658), channel_id=1, source_target_pairs={{0,3},{1,0},{2,1},{3,2},{4,7},{5,4},{6,5},{7,6},{8,11},{9,8},{10,9... | collective-permute-start | bytes 589832 | tf_op jit(solution)/shard_map/ppermute | solution.py:139
  48.2 28.0 %collective-permute-start.22 = (bf16[256,512]{1,0:T(8,128)(2,1)S(1)}, bf16[256,512]{1,0:T(8,128)(2,1)S(1)}, u32[]{:S(2)}, u32[]{:S(2)}) collective-permute-start(bf16[256,512]{1,0:T(8,128)(2,1)S(1)} %bitcast.674), channel_id=1, source_target_pairs={{0,1},{1,2},{2,3},{3,0},{4,5},{5,6},{6,7},{7,4},{8,9},{9,10},{10,1... | collective-permute-start | bytes 786440 | tf_op jit(solution)/shard_map/ppermute | solution.py:139
  49.7 45.6 %collective-permute-start.23 = (bf16[256,512]{1,0:T(8,128)(2,1)S(1)}, bf16[256,512]{1,0:T(8,128)(2,1)S(1)}, u32[]{:S(2)}, u32[]{:S(2)}) collective-permute-start(bf16[256,512]{1,0:T(8,128)(2,1)S(1)} %bitcast.675), channel_id=1, source_target_pairs={{0,2},{1,3},{2,0},{3,1},{4,6},{5,7},{6,4},{7,5},{8,10},{9,11},{10,... | collective-permute-start | bytes 786440 | tf_op jit(solution)/shard_map/ppermute | solution.py:139
  52.4 44.3 %collective-permute-start.24 = (bf16[256,512]{1,0:T(8,128)(2,1)S(1)}, bf16[256,512]{1,0:T(8,128)(2,1)S(1)}, u32[]{:S(2)}, u32[]{:S(2)}) collective-permute-start(bf16[256,512]{1,0:T(8,128)(2,1)S(1)} %bitcast.676), channel_id=1, source_target_pairs={{0,3},{1,0},{2,1},{3,2},{4,7},{5,4},{6,5},{7,6},{8,11},{9,8},{10,9... | collective-permute-start | bytes 786440 | tf_op jit(solution)/shard_map/ppermute | solution.py:139
  63.4 35.5 %collective-permute-start.12 = (bf16[256,640]{1,0:T(8,128)(2,1)S(1)}, bf16[256,640]{1,0:T(8,128)(2,1)S(1)}, u32[]{:S(2)}, u32[]{:S(2)}) collective-permute-start(bf16[256,640]{1,0:T(8,128)(2,1)S(1)} %bitcast.651), channel_id=1, source_target_pairs={{0,1},{1,2},{2,3},{3,0},{4,5},{5,6},{6,7},{7,4},{8,9},{9,10},{10,1... | collective-permute-start | bytes 983048 | tf_op jit(solution)/shard_map/ppermute | solution.py:139
  64.1 43.8 %collective-permute-start.13 = (bf16[256,640]{1,0:T(8,128)(2,1)S(1)}, bf16[256,640]{1,0:T(8,128)(2,1)S(1)}, u32[]{:S(2)}, u32[]{:S(2)}) collective-permute-start(bf16[256,640]{1,0:T(8,128)(2,1)S(1)} %bitcast.652), channel_id=1, source_target_pairs={{0,2},{1,3},{2,0},{3,1},{4,6},{5,7},{6,4},{7,5},{8,10},{9,11},{10,... | collective-permute-start | bytes 983048 | tf_op jit(solution)/shard_map/ppermute | solution.py:139
  76.2 33.1 %collective-permute-start.14 = (bf16[256,640]{1,0:T(8,128)(2,1)S(1)}, bf16[256,640]{1,0:T(8,128)(2,1)S(1)}, u32[]{:S(2)}, u32[]{:S(2)}) collective-permute-start(bf16[256,640]{1,0:T(8,128)(2,1)S(1)} %bitcast.653), channel_id=1, source_target_pairs={{0,3},{1,0},{2,1},{3,2},{4,7},{5,4},{6,5},{7,6},{8,11},{9,8},{10,9... | collective-permute-start | bytes 983048 | tf_op jit(solution)/shard_map/ppermute | solution.py:139
  95.3 26.4 %collective-permute-start.7 = (bf16[4,256,384]{2,1,0:T(8,128)(2,1)}, bf16[4,256,384]{2,1,0:T(8,128)(2,1)}, u32[]{:S(2)}, u32[]{:S(2)}) collective-permute-start(bf16[4,256,384]{2,1,0:T(8,128)(2,1)} %pad_maximum_fusion.18), channel_id=1, source_target_pairs={{0,8},{4,12},{8,0},{12,4},{16,24},{20,28},{24,16},{28,20},{1,9},{5... | collective-permute-start | bytes 2359304 | tf_op jit(solution)/shard_map/ppermute | solution.py:134
  96.7 28.2 %collective-permute-start.8 = (bf16[4,256,384]{2,1,0:T(8,128)(2,1)}, bf16[4,256,384]{2,1,0:T(8,128)(2,1)}, u32[]{:S(2)}, u32[]{:S(2)}) collective-permute-start(bf16[4,256,384]{2,1,0:T(8,128)(2,1)} %pad_maximum_fusion.18), channel_id=1, source_target_pairs={{0,16},{4,20},{8,24},{12,28},{16,0},{20,4},{24,8},{28,12},{1,17},{... | collective-permute-start | bytes 2359304 | tf_op jit(solution)/shard_map/ppermute | solution.py:134
  98.9 76.7 %collective-permute-start.25 = (bf16[4,256,512]{2,1,0:T(8,128)(2,1)}, bf16[4,256,512]{2,1,0:T(8,128)(2,1)}, u32[]{:S(2)}, u32[]{:S(2)}) collective-permute-start(bf16[4,256,512]{2,1,0:T(8,128)(2,1)} %pad_maximum_fusion.15), channel_id=1, source_target_pairs={{0,8},{4,12},{8,0},{12,4},{16,24},{20,28},{24,16},{28,20},{1,9},{5... | collective-permute-start | bytes 3145736 | tf_op jit(solution)/shard_map/ppermute | solution.py:134
  107.9 70.3 %collective-permute-start.26 = (bf16[4,256,512]{2,1,0:T(8,128)(2,1)}, bf16[4,256,512]{2,1,0:T(8,128)(2,1)}, u32[]{:S(2)}, u32[]{:S(2)}) collective-permute-start(bf16[4,256,512]{2,1,0:T(8,128)(2,1)} %pad_maximum_fusion.15), channel_id=1, source_target_pairs={{0,16},{4,20},{8,24},{12,28},{16,0},{20,4},{24,8},{28,12},{1,17},{... | collective-permute-start | bytes 3145736 | tf_op jit(solution)/shard_map/ppermute | solution.py:134
  110.6 78.0 %collective-permute-start.15 = (bf16[4,256,640]{2,1,0:T(8,128)(2,1)}, bf16[4,256,640]{2,1,0:T(8,128)(2,1)}, u32[]{:S(2)}, u32[]{:S(2)}) collective-permute-start(bf16[4,256,640]{2,1,0:T(8,128)(2,1)} %pad_maximum_fusion.12), channel_id=1, source_target_pairs={{0,8},{4,12},{8,0},{12,4},{16,24},{20,28},{24,16},{28,20},{1,9},{5... | collective-permute-start | bytes 3932168 | tf_op jit(solution)/shard_map/ppermute | solution.py:134
  113.2 61.9 %all-to-all-start.2 = ((bf16[8,64,1024]{2,1,0:T(8,128)(2,1)}), bf16[8,64,1024]{2,1,0:T(8,128)(2,1)S(1)}, u32[]{:S(2)}, u32[]{:S(2)}) async-start(bf16[8,64,1024]{2,1,0:T(8,128)(2,1)} %bitcast.673), calls=%async_computation.2 | async-start | bytes 2097152 | tf_op jit(solution)/shard_map/all_to_all | solution.py:279
  117.8 733.3 %all-reduce.2.cloned.1.call-start = ((), (), s32[]{:S(2)}) async-start(), calls=%async_computation.4 | async-start | bytes 131072 | tf_op jit(solution)/shard_map/psum | solution.py:372
  123.4 59.4 %collective-permute-start.9 = (bf16[2,256,384]{2,1,0:T(8,128)(2,1)}, bf16[2,256,384]{2,1,0:T(8,128)(2,1)}, u32[]{:S(2)}, u32[]{:S(2)}) collective-permute-start(bf16[2,256,384]{2,1,0:T(8,128)(2,1)} %slice.1353), channel_id=1, source_target_pairs={{0,16},{4,20},{8,24},{12,28},{16,0},{20,4},{24,8},{28,12},{1,17},{... | collective-permute-start | bytes 1179656 | tf_op jit(solution)/shard_map/ppermute | solution.py:134
  126.6 57.7 %collective-permute-start.10 = (bf16[2,256,384]{2,1,0:T(8,128)(2,1)}, bf16[2,256,384]{2,1,0:T(8,128)(2,1)}, u32[]{:S(2)}, u32[]{:S(2)}) collective-permute-start(bf16[2,256,384]{2,1,0:T(8,128)(2,1)} %slice.1356), channel_id=1, source_target_pairs={{0,8},{4,12},{8,0},{12,4},{16,24},{20,28},{24,16},{28,20},{1,9},{5... | collective-permute-start | bytes 1179656 | tf_op jit(solution)/shard_map/ppermute | solution.py:134
  175.6 26.6 %collective-permute-start.16 = (bf16[4,256,640]{2,1,0:T(8,128)(2,1)}, bf16[4,256,640]{2,1,0:T(8,128)(2,1)S(1)}, u32[]{:S(2)}, u32[]{:S(2)}) collective-permute-start(bf16[4,256,640]{2,1,0:T(8,128)(2,1)} %pad_maximum_fusion.12), channel_id=1, source_target_pairs={{0,16},{4,20},{8,24},{12,28},{16,0},{20,4},{24,8},{28,12},{1,17},{... | collective-permute-start | bytes 3932168 | tf_op jit(solution)/shard_map/ppermute | solution.py:134
  178.2 26.0 %collective-permute-start = (bf16[512,1024]{0,1:T(8,128)(2,1)}, bf16[512,1024]{0,1:T(8,128)(2,1)S(1)}, u32[]{:S(2)}, u32[]{:S(2)}) collective-permute-start(bf16[512,1024]{0,1:T(8,128)(2,1)} %copy.185), channel_id=1, source_target_pairs={{0,0},{1,4},{2,1},{3,5},{4,2},{5,6},{6,3},{7,7},{8,8},{9,12},{10,9... | collective-permute-start | bytes 3145736 | tf_op jit(solution)/shard_map/ppermute | solution.py:280
  182.8 44.1 %collective-permute-start.1 = (bf16[512,1024]{0,1:T(8,128)(2,1)}, bf16[512,1024]{0,1:T(8,128)(2,1)S(1)}, u32[]{:S(2)}, u32[]{:S(2)}) collective-permute-start(bf16[512,1024]{0,1:T(8,128)(2,1)} %copy.185), channel_id=1, source_target_pairs={{0,1},{1,5},{2,0},{3,4},{4,3},{5,7},{6,2},{7,6},{8,9},{9,13},{10,8... | collective-permute-start | bytes 3145736 | tf_op jit(solution)/shard_map/ppermute | solution.py:280
  184.3 55.4 %collective-permute-start.32 = (bf16[512,1024]{0,1:T(8,128)(2,1)S(1)}, bf16[512,1024]{0,1:T(8,128)(2,1)S(1)}, u32[]{:S(2)}, u32[]{:S(2)}) collective-permute-start(bf16[512,1024]{0,1:T(8,128)(2,1)S(1)} %copy.200), channel_id=1, source_target_pairs={{0,0},{1,4},{2,1},{3,5},{4,2},{5,6},{6,3},{7,7},{8,8},{9,12},{10,9... | collective-permute-start | bytes 3145736 | tf_op jit(solution)/shard_map/ppermute | solution.py:280
  188.6 62.3 %collective-permute-start.33 = (bf16[512,1024]{0,1:T(8,128)(2,1)S(1)}, bf16[512,1024]{0,1:T(8,128)(2,1)S(1)}, u32[]{:S(2)}, u32[]{:S(2)}) collective-permute-start(bf16[512,1024]{0,1:T(8,128)(2,1)S(1)} %copy.200), channel_id=1, source_target_pairs={{0,1},{1,5},{2,0},{3,4},{4,3},{5,7},{6,2},{7,6},{8,9},{9,13},{10,8... | collective-permute-start | bytes 3145736 | tf_op jit(solution)/shard_map/ppermute | solution.py:280
  202.2 121.5 %collective-permute-start.27 = (bf16[2,256,512]{2,1,0:T(8,128)(2,1)S(1)}, bf16[2,256,512]{2,1,0:T(8,128)(2,1)}, u32[]{:S(2)}, u32[]{:S(2)}) collective-permute-start(bf16[2,256,512]{2,1,0:T(8,128)(2,1)S(1)} %slice.1442), channel_id=1, source_target_pairs={{0,16},{4,20},{8,24},{12,28},{16,0},{20,4},{24,8},{28,12},{1,17},{... | collective-permute-start | bytes 1572872 | tf_op jit(solution)/shard_map/ppermute | solution.py:134
  204.2 120.7 %collective-permute-start.28 = (bf16[2,256,512]{2,1,0:T(8,128)(2,1)S(1)}, bf16[2,256,512]{2,1,0:T(8,128)(2,1)}, u32[]{:S(2)}, u32[]{:S(2)}) collective-permute-start(bf16[2,256,512]{2,1,0:T(8,128)(2,1)S(1)} %slice.1445), channel_id=1, source_target_pairs={{0,8},{4,12},{8,0},{12,4},{16,24},{20,28},{24,16},{28,20},{1,9},{5... | collective-permute-start | bytes 1572872 | tf_op jit(solution)/shard_map/ppermute | solution.py:134
  226.9 61.3 %collective-permute-start.17 = (bf16[2,256,640]{2,1,0:T(8,128)(2,1)S(1)}, bf16[2,256,640]{2,1,0:T(8,128)(2,1)S(1)}, u32[]{:S(2)}, u32[]{:S(2)}) collective-permute-start(bf16[2,256,640]{2,1,0:T(8,128)(2,1)S(1)} %slice.1405), channel_id=1, source_target_pairs={{0,16},{4,20},{8,24},{12,28},{16,0},{20,4},{24,8},{28,12},{1,17},{... | collective-permute-start | bytes 1966088 | tf_op jit(solution)/shard_map/ppermute | solution.py:134
  239.7 49.1 %collective-permute-start.18 = (bf16[2,256,640]{2,1,0:T(8,128)(2,1)S(1)}, bf16[2,256,640]{2,1,0:T(8,128)(2,1)S(1)}, u32[]{:S(2)}, u32[]{:S(2)}) collective-permute-start(bf16[2,256,640]{2,1,0:T(8,128)(2,1)S(1)} %slice.1408), channel_id=1, source_target_pairs={{0,8},{4,12},{8,0},{12,4},{16,24},{20,28},{24,16},{28,20},{1,9},{5... | collective-permute-start | bytes 1966088 | tf_op jit(solution)/shard_map/ppermute | solution.py:134
  258.1 31.5 %collective-permute-start.2 = (bf16[512,1024]{0,1:T(8,128)(2,1)S(1)}, bf16[512,1024]{0,1:T(8,128)(2,1)}, u32[]{:S(2)}, u32[]{:S(2)}) collective-permute-start(bf16[512,1024]{0,1:T(8,128)(2,1)S(1)} %add_convert_fusion.5), channel_id=1, source_target_pairs={{0,4},{4,0},{8,12},{12,8},{16,20},{20,16},{24,28},{28,24},{1,5},{5... | collective-permute-start | bytes 3145736 | tf_op jit(solution)/shard_map/ppermute | solution.py:134
  330.8 58.2 %collective-permute-start.20 = (bf16[512,1024]{0,1:T(8,128)(2,1)S(1)}, bf16[512,1024]{0,1:T(8,128)(2,1)S(1)}, u32[]{:S(2)}, u32[]{:S(2)}) collective-permute-start(bf16[512,1024]{0,1:T(8,128)(2,1)S(1)} %add_convert_fusion.2), channel_id=1, source_target_pairs={{0,4},{4,0},{8,12},{12,8},{16,20},{20,16},{24,28},{28,24},{1,5},{5... | collective-permute-start | bytes 3145736 | tf_op jit(solution)/shard_map/ppermute | solution.py:134
  475.7 8.4 collective-permute-start.34
  480.3 427.3 %collective-permute-start.30 = (bf16[512,1024]{0,1:T(8,128)(2,1)}, bf16[512,1024]{0,1:T(8,128)(2,1)}, u32[]{:S(2)}, u32[]{:S(2)}) collective-permute-start(bf16[512,1024]{0,1:T(8,128)(2,1)} %bitcast.137), channel_id=1, source_target_pairs={{0,0},{4,1},{1,2},{5,3},{2,4},{6,5},{3,6},{7,7},{8,8},{12,9},{9,10... | collective-permute-start | bytes 3145736 | tf_op jit(solution)/shard_map/ppermute | solution.py:283
  482.2 425.4 %collective-permute-start.31 = (bf16[512,1024]{0,1:T(8,128)(2,1)}, bf16[512,1024]{0,1:T(8,128)(2,1)}, u32[]{:S(2)}, u32[]{:S(2)}) collective-permute-start(bf16[512,1024]{0,1:T(8,128)(2,1)} %bitcast.137), channel_id=1, source_target_pairs={{1,0},{5,1},{0,2},{4,3},{3,4},{7,5},{2,6},{6,7},{9,8},{13,9},{8,10... | collective-permute-start | bytes 3145736 | tf_op jit(solution)/shard_map/ppermute | solution.py:283
  518.7 28.8 %collective-permute-start.35 = (bf16[512,1024]{0,1:T(8,128)(2,1)}, bf16[512,1024]{0,1:T(8,128)(2,1)}, u32[]{:S(2)}, u32[]{:S(2)}) collective-permute-start(bf16[512,1024]{0,1:T(8,128)(2,1)} %slice.1824), channel_id=1, source_target_pairs={{0,4},{4,0},{8,12},{12,8},{16,20},{20,16},{24,28},{28,24},{1,5},{5... | collective-permute-start | bytes 3145736 | tf_op jit(solution)/shard_map/ppermute | solution.py:134
  533.8 25.0 %collective-permute-start.59 = (bf16[2,2,256,512]{3,2,1,0:T(8,128)(2,1)S(1)}, bf16[2,2,256,512]{3,2,1,0:T(8,128)(2,1)S(1)}, u32[]{:S(2)}, u32[]{:S(2)}) collective-permute-start(bf16[2,2,256,512]{3,2,1,0:T(8,128)(2,1)S(1)} %pad_maximum_fusion.17), channel_id=1, source_target_pairs={{0,16},{4,20},{8,24},{12,28},{16,0},{20,4},{24,8},{28,12},{1,17},{... | collective-permute-start | bytes 3145736 | tf_op jit(solution)/shard_map/ppermute | solution.py:134
  535.7 25.7 %collective-permute-start.56 = (bf16[2,2,256,512]{3,2,1,0:T(8,128)(2,1)S(1)}, bf16[2,2,256,512]{3,2,1,0:T(8,128)(2,1)S(1)}, u32[]{:S(2)}, u32[]{:S(2)}) collective-permute-start(bf16[2,2,256,512]{3,2,1,0:T(8,128)(2,1)S(1)} %pad_maximum_fusion.16), channel_id=1, source_target_pairs={{0,8},{4,12},{8,0},{12,4},{16,24},{20,28},{24,16},{28,20},{1,9},{5... | collective-permute-start | bytes 3145736 | tf_op jit(solution)/shard_map/ppermute | solution.py:134
  559.0 13.2 %collective-permute-start.60 = (bf16[2,256,512]{2,1,0:T(8,128)(2,1)S(1)}, bf16[2,256,512]{2,1,0:T(8,128)(2,1)S(1)}, u32[]{:S(2)}, u32[]{:S(2)}) collective-permute-start(bf16[2,256,512]{2,1,0:T(8,128)(2,1)S(1)} %fusion.49), channel_id=1, source_target_pairs={{0,8},{4,12},{8,0},{12,4},{16,24},{20,28},{24,16},{28,20},{1,9},{5... | collective-permute-start | bytes 1572872 | tf_op jit(solution)/shard_map/ppermute | solution.py:134
  561.5 12.8 %collective-permute-start.57 = (bf16[2,256,512]{2,1,0:T(8,128)(2,1)S(1)}, bf16[2,256,512]{2,1,0:T(8,128)(2,1)S(1)}, u32[]{:S(2)}, u32[]{:S(2)}) collective-permute-start(bf16[2,256,512]{2,1,0:T(8,128)(2,1)S(1)} %fusion.46), channel_id=1, source_target_pairs={{0,16},{4,20},{8,24},{12,28},{16,0},{20,4},{24,8},{28,12},{1,17},{... | collective-permute-start | bytes 1572872 | tf_op jit(solution)/shard_map/ppermute | solution.py:134
  572.5 18.9 %collective-permute-start.61 = (bf16[256,512]{1,0:T(8,128)(2,1)S(1)}, bf16[256,512]{1,0:T(8,128)(2,1)S(1)}, u32[]{:S(2)}, u32[]{:S(2)}) collective-permute-start(bf16[256,512]{1,0:T(8,128)(2,1)S(1)} %get-tuple-element.284), channel_id=1, source_target_pairs={{0,2},{1,3},{2,0},{3,1},{4,6},{5,7},{6,4},{7,5},{8,10},{9,11},{10,... | collective-permute-start | bytes 786440 | tf_op jit(solution)/shard_map/ppermute | solution.py:139
  572.5 22.5 %collective-permute-start.62 = (bf16[256,512]{1,0:T(8,128)(2,1)S(1)}, bf16[256,512]{1,0:T(8,128)(2,1)S(1)}, u32[]{:S(2)}, u32[]{:S(2)}) collective-permute-start(bf16[256,512]{1,0:T(8,128)(2,1)S(1)} %get-tuple-element.285), channel_id=1, source_target_pairs={{0,1},{1,2},{2,3},{3,0},{4,5},{5,6},{6,7},{7,4},{8,9},{9,10},{10,1... | collective-permute-start | bytes 786440 | tf_op jit(solution)/shard_map/ppermute | solution.py:139
  574.6 20.4 %collective-permute-start.58 = (bf16[256,512]{1,0:T(8,128)(2,1)S(1)}, bf16[256,512]{1,0:T(8,128)(2,1)S(1)}, u32[]{:S(2)}, u32[]{:S(2)}) collective-permute-start(bf16[256,512]{1,0:T(8,128)(2,1)S(1)} %fusion.65), channel_id=1, source_target_pairs={{0,3},{1,0},{2,1},{3,2},{4,7},{5,4},{6,5},{7,6},{8,11},{9,8},{10,9... | collective-permute-start | bytes 786440 | tf_op jit(solution)/shard_map/ppermute | solution.py:139
  652.7 71.4 %collective-permute-start.37 = (bf16[512,1024]{0,1:T(8,128)(2,1)}, bf16[512,1024]{0,1:T(8,128)(2,1)}, u32[]{:S(2)}, u32[]{:S(2)}) collective-permute-start(bf16[512,1024]{0,1:T(8,128)(2,1)} %slice.1823), channel_id=1, source_target_pairs={{0,4},{4,0},{8,12},{12,8},{16,20},{20,16},{24,28},{28,24},{1,5},{5... | collective-permute-start | bytes 3145736 | tf_op jit(solution)/shard_map/ppermute | solution.py:134
  689.5 29.2 %collective-permute-start.43 = (bf16[2,2,256,384]{2,3,1,0:T(8,128)(2,1)}, bf16[2,2,256,384]{2,3,1,0:T(8,128)(2,1)}, u32[]{:S(2)}, u32[]{:S(2)}) collective-permute-start(bf16[2,2,256,384]{2,3,1,0:T(8,128)(2,1)} %pad_maximum_fusion.20), channel_id=1, source_target_pairs={{0,16},{4,20},{8,24},{12,28},{16,0},{20,4},{24,8},{28,12},{1,17},{... | collective-permute-start | bytes 2359304 | tf_op jit(solution)/shard_map/ppermute | solution.py:134
  693.9 28.1 %collective-permute-start.40 = (bf16[2,2,256,384]{2,3,1,0:T(8,128)(2,1)}, bf16[2,2,256,384]{2,3,1,0:T(8,128)(2,1)}, u32[]{:S(2)}, u32[]{:S(2)}) collective-permute-start(bf16[2,2,256,384]{2,3,1,0:T(8,128)(2,1)} %pad_maximum_fusion.19), channel_id=1, source_target_pairs={{0,8},{4,12},{8,0},{12,4},{16,24},{20,28},{24,16},{28,20},{1,9},{5... | collective-permute-start | bytes 2359304 | tf_op jit(solution)/shard_map/ppermute | solution.py:134
  718.7 148.5 %collective-permute-start.51 = (bf16[2,2,256,640]{3,2,1,0:T(8,128)(2,1)}, bf16[2,2,256,640]{3,2,1,0:T(8,128)(2,1)}, u32[]{:S(2)}, u32[]{:S(2)}) collective-permute-start(bf16[2,2,256,640]{3,2,1,0:T(8,128)(2,1)} %pad_maximum_fusion.14), channel_id=1, source_target_pairs={{0,16},{4,20},{8,24},{12,28},{16,0},{20,4},{24,8},{28,12},{1,17},{... | collective-permute-start | bytes 3932168 | tf_op jit(solution)/shard_map/ppermute | solution.py:134
  721.9 148.9 %collective-permute-start.48 = (bf16[2,2,256,640]{3,2,1,0:T(8,128)(2,1)}, bf16[2,2,256,640]{3,2,1,0:T(8,128)(2,1)}, u32[]{:S(2)}, u32[]{:S(2)}) collective-permute-start(bf16[2,2,256,640]{3,2,1,0:T(8,128)(2,1)} %pad_maximum_fusion.13), channel_id=1, source_target_pairs={{0,8},{4,12},{8,0},{12,4},{16,24},{20,28},{24,16},{28,20},{1,9},{5... | collective-permute-start | bytes 3932168 | tf_op jit(solution)/shard_map/ppermute | solution.py:134
  724.2 131.5 %collective-permute-start.44 = (bf16[2,256,384]{1,2,0:T(8,128)(2,1)}, bf16[2,256,384]{1,2,0:T(8,128)(2,1)}, u32[]{:S(2)}, u32[]{:S(2)}) collective-permute-start(bf16[2,256,384]{1,2,0:T(8,128)(2,1)} %fusion.54), channel_id=1, source_target_pairs={{0,8},{4,12},{8,0},{12,4},{16,24},{20,28},{24,16},{28,20},{1,9},{5... | collective-permute-start | bytes 1179656 | tf_op jit(solution)/shard_map/ppermute | solution.py:134
  855.6 10.4 %collective-permute-start.41 = (bf16[2,256,384]{1,2,0:T(8,128)(2,1)}, bf16[2,256,384]{1,2,0:T(8,128)(2,1)S(1)}, u32[]{:S(2)}, u32[]{:S(2)}) collective-permute-start(bf16[2,256,384]{1,2,0:T(8,128)(2,1)} %fusion.51), channel_id=1, source_target_pairs={{0,16},{4,20},{8,24},{12,28},{16,0},{20,4},{24,8},{28,12},{1,17},{... | collective-permute-start | bytes 1179656 | tf_op jit(solution)/shard_map/ppermute | solution.py:134
  866.0 15.9 %collective-permute-start.45 = (bf16[256,384]{0,1:T(8,128)(2,1)S(1)}, bf16[256,384]{0,1:T(8,128)(2,1)S(1)}, u32[]{:S(2)}, u32[]{:S(2)}) collective-permute-start(bf16[256,384]{0,1:T(8,128)(2,1)S(1)} %get-tuple-element.296), channel_id=1, source_target_pairs={{0,2},{1,3},{2,0},{3,1},{4,6},{5,7},{6,4},{7,5},{8,10},{9,11},{10,... | collective-permute-start | bytes 589832 | tf_op jit(solution)/shard_map/ppermute | solution.py:139
  867.2 16.6 %collective-permute-start.46 = (bf16[256,384]{0,1:T(8,128)(2,1)S(1)}, bf16[256,384]{0,1:T(8,128)(2,1)S(1)}, u32[]{:S(2)}, u32[]{:S(2)}) collective-permute-start(bf16[256,384]{0,1:T(8,128)(2,1)S(1)} %get-tuple-element.297), channel_id=1, source_target_pairs={{0,1},{1,2},{2,3},{3,0},{4,5},{5,6},{6,7},{7,4},{8,9},{9,10},{10,1... | collective-permute-start | bytes 589832 | tf_op jit(solution)/shard_map/ppermute | solution.py:139
  870.8 14.3 %collective-permute-start.42 = (bf16[256,384]{0,1:T(8,128)(2,1)S(1)}, bf16[256,384]{0,1:T(8,128)(2,1)S(1)}, u32[]{:S(2)}, u32[]{:S(2)}) collective-permute-start(bf16[256,384]{0,1:T(8,128)(2,1)S(1)} %fusion.66), channel_id=1, source_target_pairs={{0,3},{1,0},{2,1},{3,2},{4,7},{5,4},{6,5},{7,6},{8,11},{9,8},{10,9... | collective-permute-start | bytes 589832 | tf_op jit(solution)/shard_map/ppermute | solution.py:139
  881.9 64.8 %collective-permute-start.38 = (bf16[512,1024]{0,1:T(8,128)(2,1)S(1)}, bf16[512,1024]{0,1:T(8,128)(2,1)S(1)}, u32[]{:S(2)}, u32[]{:S(2)}) collective-permute-start(bf16[512,1024]{0,1:T(8,128)(2,1)S(1)} %bitcast.670), channel_id=1, source_target_pairs={{0,0},{4,1},{1,2},{5,3},{2,4},{6,5},{3,6},{7,7},{8,8},{12,9},{9,10... | collective-permute-start | bytes 3145736 | tf_op jit(solution)/shard_map/ppermute | solution.py:283
  883.9 16.6 %collective-permute-start.52 = (bf16[2,256,640]{2,1,0:T(8,128)(2,1)S(1)}, bf16[2,256,640]{2,1,0:T(8,128)(2,1)S(1)}, u32[]{:S(2)}, u32[]{:S(2)}) collective-permute-start(bf16[2,256,640]{2,1,0:T(8,128)(2,1)S(1)} %fusion.44), channel_id=1, source_target_pairs={{0,8},{4,12},{8,0},{12,4},{16,24},{20,28},{24,16},{28,20},{1,9},{5... | collective-permute-start | bytes 1966088 | tf_op jit(solution)/shard_map/ppermute | solution.py:134
  887.0 16.0 %collective-permute-start.49 = (bf16[2,256,640]{2,1,0:T(8,128)(2,1)S(1)}, bf16[2,256,640]{2,1,0:T(8,128)(2,1)S(1)}, u32[]{:S(2)}, u32[]{:S(2)}) collective-permute-start(bf16[2,256,640]{2,1,0:T(8,128)(2,1)S(1)} %fusion.41), channel_id=1, source_target_pairs={{0,16},{4,20},{8,24},{12,28},{16,0},{20,4},{24,8},{28,12},{1,17},{... | collective-permute-start | bytes 1966088 | tf_op jit(solution)/shard_map/ppermute | solution.py:134
  900.5 46.3 %collective-permute-start.39 = (bf16[512,1024]{0,1:T(8,128)(2,1)S(1)}, bf16[512,1024]{0,1:T(8,128)(2,1)S(1)}, u32[]{:S(2)}, u32[]{:S(2)}) collective-permute-start(bf16[512,1024]{0,1:T(8,128)(2,1)S(1)} %bitcast.671), channel_id=1, source_target_pairs={{1,0},{5,1},{0,2},{4,3},{3,4},{7,5},{2,6},{6,7},{9,8},{13,9},{8,10... | collective-permute-start | bytes 3145736 | tf_op jit(solution)/shard_map/ppermute | solution.py:283
  903.0 52.2 %collective-permute-start.53 = (bf16[256,640]{1,0:T(8,128)(2,1)}, bf16[256,640]{1,0:T(8,128)(2,1)}, u32[]{:S(2)}, u32[]{:S(2)}) collective-permute-start(bf16[256,640]{1,0:T(8,128)(2,1)} %get-tuple-element.272), channel_id=1, source_target_pairs={{0,2},{1,3},{2,0},{3,1},{4,6},{5,7},{6,4},{7,5},{8,10},{9,11},{10,... | collective-permute-start | bytes 983048 | tf_op jit(solution)/shard_map/ppermute | solution.py:139
  907.6 47.5 %collective-permute-start.54 = (bf16[256,640]{1,0:T(8,128)(2,1)}, bf16[256,640]{1,0:T(8,128)(2,1)}, u32[]{:S(2)}, u32[]{:S(2)}) collective-permute-start(bf16[256,640]{1,0:T(8,128)(2,1)} %get-tuple-element.273), channel_id=1, source_target_pairs={{0,1},{1,2},{2,3},{3,0},{4,5},{5,6},{6,7},{7,4},{8,9},{9,10},{10,1... | collective-permute-start | bytes 983048 | tf_op jit(solution)/shard_map/ppermute | solution.py:139
  907.6 47.5 %collective-permute-start.50 = (bf16[256,640]{1,0:T(8,128)(2,1)}, bf16[256,640]{1,0:T(8,128)(2,1)}, u32[]{:S(2)}, u32[]{:S(2)}) collective-permute-start(bf16[256,640]{1,0:T(8,128)(2,1)} %fusion.64), channel_id=1, source_target_pairs={{0,3},{1,0},{2,1},{3,2},{4,7},{5,4},{6,5},{7,6},{8,11},{9,8},{10,9... | collective-permute-start | bytes 983048 | tf_op jit(solution)/shard_map/ppermute | solution.py:139
  949.8 15.5 %all-to-all-start.1 = ((bf16[8,64,1024]{2,1,0:T(8,128)(2,1)}), bf16[8,64,1024]{2,1,0:T(8,128)(2,1)S(1)}, u32[]{:S(2)}, u32[]{:S(2)}) async-start(bf16[8,64,1024]{2,1,0:T(8,128)(2,1)} %bitcast.138), calls=%async_computation.1 | async-start | bytes 2097152 | tf_op jit(solution)/shard_map/all_to_all | solution.py:284
  957.4 14.5 %collective-permute-start.55 = (bf16[128,640]{1,0:T(8,128)(2,1)S(1)}, bf16[128,640]{1,0:T(8,128)(2,1)S(1)}, u32[]{:S(2)}, u32[]{:S(2)}) collective-permute-start(bf16[128,640]{1,0:T(8,128)(2,1)S(1)} %dynamic-slice_convert_fusion), channel_id=1, source_target_pairs={{0,4},{4,0},{8,12},{12,8},{16,20},{20,16},{24,28},{28,24},{1,5},{5... | collective-permute-start | bytes 491528 | tf_op jit(solution)/shard_map/ppermute | solution.py:134
  965.3 18.5 %all-to-all-start.3 = ((bf16[8,64,1024]{2,1,0:T(8,128)(2,1)}), bf16[8,64,1024]{2,1,0:T(8,128)(2,1)S(1)}, u32[]{:S(2)}, u32[]{:S(2)}) async-start(bf16[8,64,1024]{2,1,0:T(8,128)(2,1)} %bitcast.146), calls=%async_computation.3 | async-start | bytes 2097152 | tf_op jit(solution)/shard_map/all_to_all | solution.py:284
  (278 other events, 7643.4 us)
Sparse Core Ops, SparseCore 0:
  730.1 120.9 all-reduce.1

commit v2 on v1

--- a/solution.py
+++ b/solution.py
@@ -28,16 +28,21 @@
     return pull(row_grad)
 
 
-def attn_fwd_kernel(qpos_ref, qstart_ref, kpos_ref, q_ref, k_ref, v_ref, o_ref, lse_ref):
+PAIR = 2 * DH
+
+
+def attn_fwd_kernel(qpos_ref, qstart_ref, kpos_ref, qkv_ref, o_ref, lse_ref):
+    first = pl.multiple_of(pl.program_id(0) * QB, QB)
     kpos = kpos_ref[...]
     allowed = (kpos <= qpos_ref[...]) & (kpos >= qstart_ref[...])
     bias = jnp.where(allowed, 0.0, MASKED_OUT)
-    lane = lax.broadcasted_iota(jnp.int32, (1, 2 * DH), 1)
+    lane = lax.broadcasted_iota(jnp.int32, (1, PAIR), 1)
     wide = lax.broadcasted_iota(jnp.int32, lse_ref.shape, 1)
     stats = jnp.zeros(lse_ref.shape, F32)
-    for pair in range(q_ref.shape[1] // (2 * DH)):
-        cols = slice(pair * 2 * DH, (pair + 1) * 2 * DH)
-        query, key, value = q_ref[:, cols], k_ref[:, cols], v_ref[:, cols]
+    for pair in range(o_ref.shape[1] // PAIR):
+        at = 3 * pair * PAIR
+        query = qkv_ref[pl.ds(first, QB), at:at + PAIR]
+        key, value = qkv_ref[:, at + PAIR:at + 2 * PAIR], qkv_ref[:, at + 2 * PAIR:at + 3 * PAIR]
         total = jnp.zeros(query.shape, F32)
         for side in range(2):
             mine = (lane >= side * DH) & (lane < (side + 1) * DH)
@@ -49,28 +54,29 @@
             prob = (expo * (1.0 / norm)).astype(BF)
             total += jnp.dot(prob, jnp.where(mine, value, jnp.zeros_like(value)), preferred_element_type=F32)
             stats = jnp.where(wide == pair * 2 + side, peak + jnp.log(norm), stats)
-        o_ref[:, cols] = total.astype(BF)
+        o_ref[:, pair * PAIR:(pair + 1) * PAIR] = total.astype(BF)
     lse_ref[...] = stats
 
 
-def attn_forward(qpos, qstart, kpos, q, k, v):
-    rows, width = q.shape
+def attn_forward(qpos, qstart, kpos, qkv):
+    rows, width = qkv.shape[0], qkv.shape[1] // 3
     col = pl.BlockSpec((QB, 1), lambda i: (i, 0))
-    full = pl.BlockSpec((rows, width), lambda i: (0, 0))
+    full = pl.BlockSpec(qkv.shape, lambda i: (0, 0))
     return pl.pallas_call(
         attn_fwd_kernel,
         grid=(rows // QB,),
-        in_specs=[col, col, pl.BlockSpec((1, rows), lambda i: (0, 0)), pl.BlockSpec((QB, width), lambda i: (i, 0)), full, full],
+        in_specs=[col, col, pl.BlockSpec((1, rows), lambda i: (0, 0)), full],
         out_specs=[pl.BlockSpec((QB, width), lambda i: (i, 0)), pl.BlockSpec((QB, 128), lambda i: (i, 0))],
         out_shape=[jax.ShapeDtypeStruct((rows, width), BF), jax.ShapeDtypeStruct((rows, 128), F32)],
         cost_estimate=pl.CostEstimate(flops=4 * rows * rows * width, bytes_accessed=8 * rows * width, transcendentals=rows * rows * width // DH),
         compiler_params=pltpu.CompilerParams(vmem_limit_bytes=48 << 20),
         name="attn_fwd",
-    )(qpos, qstart, kpos, q, k, v)
-
-
-def attn_bwd_kernel(qpos_ref, qstart_ref, kpos_ref, lse_ref, q_ref, g_ref, k_ref, v_ref, dq_ref, dk_ref, dv_ref, dk_acc, dv_acc):
+    )(qpos, qstart, kpos, qkv)
+
+
+def attn_bwd_kernel(qpos_ref, qstart_ref, kpos_ref, lse_ref, g_ref, qkv_ref, d_ref, dk_acc, dv_acc):
     step = pl.program_id(0)
+    first = pl.multiple_of(step * QB, QB)
 
     @pl.when(step == 0)
     def _():
@@ -80,10 +86,13 @@
     kpos = kpos_ref[...]
     allowed = (kpos <= qpos_ref[...]) & (kpos >= qstart_ref[...])
     bias = jnp.where(allowed, 0.0, MASKED_OUT)
-    lane = lax.broadcasted_iota(jnp.int32, (1, 2 * DH), 1)
-    for pair in range(q_ref.shape[1] // (2 * DH)):
-        cols = slice(pair * 2 * DH, (pair + 1) * 2 * DH)
-        query, grad, key, value = q_ref[:, cols], g_ref[:, cols], k_ref[:, cols], v_ref[:, cols]
+    lane = lax.broadcasted_iota(jnp.int32, (1, PAIR), 1)
+    for pair in range(g_ref.shape[1] // PAIR):
+        at = 3 * pair * PAIR
+        query = qkv_ref[pl.ds(first, QB), at:at + PAIR]
+        key, value = qkv_ref[:, at + PAIR:at + 2 * PAIR], qkv_ref[:, at + 2 * PAIR:at + 3 * PAIR]
+        cols = slice(pair * PAIR, (pair + 1) * PAIR)
+        grad = g_ref[:, cols]
         dq = jnp.zeros(query.shape, F32)
         dk = jnp.zeros(key.shape, F32)
         dv = jnp.zeros(key.shape, F32)
@@ -100,33 +109,35 @@
             dq += jnp.dot(gscore, jnp.where(mine, key, jnp.zeros_like(key)), preferred_element_type=F32)
             dk += lax.dot_general(gscore, part, (((0,), (0,)), ((), ())), preferred_element_type=F32)
             dv += lax.dot_general(prob.astype(BF), gpart, (((0,), (0,)), ((), ())), preferred_element_type=F32)
-        dq_ref[:, cols] = (dq * 0.125).astype(BF)
+        d_ref[pl.ds(first, QB), at:at + PAIR] = (dq * 0.125).astype(BF)
         dk_acc[:, cols] += dk
         dv_acc[:, cols] += dv
 
     @pl.when(step == pl.num_programs(0) - 1)
     def _():
-        dk_ref[...] = dk_acc[...].astype(BF)
-        dv_ref[...] = dv_acc[...].astype(BF)
-
-
-def attn_backward(qpos, qstart, kpos, lse, q, grad, k, v):
-    rows, width = q.shape
+        for pair in range(g_ref.shape[1] // PAIR):
+            at = 3 * pair * PAIR
+            cols = slice(pair * PAIR, (pair + 1) * PAIR)
+            d_ref[:, at + PAIR:at + 2 * PAIR] = dk_acc[:, cols].astype(BF)
+            d_ref[:, at + 2 * PAIR:at + 3 * PAIR] = dv_acc[:, cols].astype(BF)
+
+
+def attn_backward(qpos, qstart, kpos, lse, grad, qkv):
+    rows, width = grad.shape
     col = pl.BlockSpec((QB, 1), lambda i: (i, 0))
-    blk = pl.BlockSpec((QB, width), lambda i: (i, 0))
-    full = pl.BlockSpec((rows, width), lambda i: (0, 0))
-    wide = jax.ShapeDtypeStruct((rows, width), BF)
+    full = pl.BlockSpec(qkv.shape, lambda i: (0, 0))
     return pl.pallas_call(
         attn_bwd_kernel,
         grid=(rows // QB,),
-        in_specs=[col, col, pl.BlockSpec((1, rows), lambda i: (0, 0)), pl.BlockSpec((QB, 128), lambda i: (i, 0)), blk, blk, full, full],
-        out_specs=[blk, full, full],
-        out_shape=[wide, wide, wide],
+        in_specs=[col, col, pl.BlockSpec((1, rows), lambda i: (0, 0)), pl.BlockSpec((QB, 128), lambda i: (i, 0)),
+                  pl.BlockSpec((QB, width), lambda i: (i, 0)), full],
+        out_specs=full,
+        out_shape=jax.ShapeDtypeStruct(qkv.shape, BF),
         scratch_shapes=[pltpu.VMEM((rows, width), F32), pltpu.VMEM((rows, width), F32)],
         cost_estimate=pl.CostEstimate(flops=10 * rows * rows * width, bytes_accessed=14 * rows * width, transcendentals=rows * rows * width // DH),
         compiler_params=pltpu.CompilerParams(vmem_limit_bytes=48 << 20),
         name="attn_bwd",
-    )(qpos, qstart, kpos, lse, q, grad, k, v)
+    )(qpos, qstart, kpos, lse, grad, qkv)
 
 
 def swap_dp(x, bit):
@@ -233,6 +244,342 @@
     return near, far
 
 
+MESH = pl.DeviceIdType.MESH
+LANES = 4
+ANY = pl.BlockSpec(memory_space=pl.ANY)
+IN_VMEM = pl.BlockSpec(memory_space=pltpu.VMEM)
+
+
+def meet(dp, lane, n_dp):
+    barrier = pltpu.get_barrier_semaphore()
+    count = 0
+    for d in range(1, n_dp):
+        pl.semaphore_signal(barrier, inc=1, device_id=(dp ^ d, lane), device_id_type=MESH)
+        count += 1
+    for k in range(1, LANES):
+        for c in range(2):
+            pl.semaphore_signal(barrier, inc=1, device_id=(dp ^ c, lax.rem(lane + k, LANES)), device_id_type=MESH)
+            count += 1
+    pl.semaphore_wait(barrier, count)
+
+
+def deal_route(dp, lane):
+    chip, core = dp // 2, dp % 2
+    spot = chip * 2 + lane % 2
+    return (spot, 2 * core + lane // 2), (spot, 2 * core + 1 - lane // 2)
+
+
+def home_route(dp, lane):
+    chip, core = dp // 2, dp % 2
+    pack, half = lane // 2, lane % 2
+    return (chip * 2 + pack, core + 2 * half), (chip * 2 + pack, core + 2 * (1 - half))
+
+
+def send(src, dst, send_sem, recv_sem, device):
+    return pltpu.make_async_remote_copy(src_ref=src, dst_ref=dst, send_sem=send_sem, recv_sem=recv_sem, device_id=device, device_id_type=MESH)
+
+
+def gather_kernel(widths, own, other, small, tok, cot, *rest):
+    mats, (near_t, far_t, near_c, far_c, small_out), rest = rest[:4], rest[4:9], rest[9:]
+    moved_t, moved_c, loc, s_c, r_c, s_z, r_z, s_p, r_p, s_d, r_d, s_t, r_t, s_b, r_b = rest
+    dp, lane = lax.axis_index("dp"), lax.axis_index("tensor")
+    n_dp = 8
+    core = dp % 2
+    wd = own.shape[0]
+    up = lax.rem(lane + 1, LANES)
+    meet(dp, lane, n_dp)
+    block = tok.shape[0] // n_dp
+    started, deals = [], []
+    for i, (src, dst) in enumerate(((tok, moved_t), (cot, moved_c))):
+        here = pl.ds(pl.multiple_of(dp * block, block), block)
+        keep = pltpu.make_async_copy(src.at[here], dst.at[here], loc.at[i])
+        keep.start()
+        copies = []
+        for d in range(1, n_dp):
+            there = pl.ds(pl.multiple_of((dp ^ d) * block, block), block)
+            copies.append(send(src.at[there], dst.at[here], s_t.at[i, d], r_t.at[i, d], (dp ^ d, lane)))
+        deals.append((keep, copies))
+    feat = pl.ds(pl.multiple_of(core * wd, wd), wd)
+    at, locals_, firsts = 0, [], []
+    for g, w in enumerate(widths):
+        dst = mats[g].at[feat, 0:w]
+        locals_.append(pltpu.make_async_copy(own.at[:, at:at + w], dst, loc.at[2 + g]))
+        firsts.append(send(other.at[:, at:at + w], dst, s_c.at[g], r_c.at[g], (dp ^ 1, lane)))
+        locals_[-1].start()
+        firsts[-1].start()
+        at += w
+    for c in deals[0][1]:
+        c.start()
+    smalls = []
+    for k in range(1, LANES):
+        rows = small.shape[0]
+        smalls.append(send(small, small_out.at[k * rows:(k + 1) * rows], s_b.at[k], r_b.at[k], (dp, lax.rem(lane + k, LANES))))
+        smalls[-1].start()
+    keep_small = pltpu.make_async_copy(small, small_out.at[0:small.shape[0]], loc.at[6])
+    keep_small.start()
+
+    def turn_copy(g, t):
+        w = widths[g]
+        return send(mats[g].at[0:2 * wd, t * w:(t + 1) * w], mats[g].at[0:2 * wd, (t + 1) * w:(t + 2) * w], s_z.at[g, t], r_z.at[g, t], (dp, up))
+
+    def plane_copy(g, k, side):
+        w = widths[g]
+        return send(mats[g].at[0:2 * wd, k * w:(k + 1) * w], mats[g].at[2 * wd * side:2 * wd * (side + 1), k * w:(k + 1) * w],
+                    s_p.at[g, k, side - 1], r_p.at[g, k, side - 1], (dp ^ (2 * side), lane))
+
+    def far_copy(g, k):
+        w = widths[g]
+        side, via = (1, 2) if k < LANES // 2 else (2, 1)
+        return send(mats[g].at[2 * wd * side:2 * wd * (side + 1), k * w:(k + 1) * w], mats[g].at[6 * wd:8 * wd, k * w:(k + 1) * w],
+                    s_d.at[g, k], r_d.at[g, k], (dp ^ (2 * via), lane))
+
+    n_g = len(widths)
+    turns = [[turn_copy(g, t) for t in range(LANES - 1)] for g in range(n_g)]
+    planes = [[[plane_copy(g, k, side) for side in (1, 2)] for k in range(LANES)] for g in range(n_g)]
+    fars = [[far_copy(g, k) for k in range(LANES)] for g in range(n_g)]
+
+    def ready(g, k):
+        if k < LANES - 1:
+            turns[g][k].start()
+        for c in planes[g][k]:
+            c.start()
+
+    for g in range(n_g):
+        locals_[g].wait()
+        firsts[g].wait_recv()
+        ready(g, 0)
+    near, far = deal_route(dp, lane)
+    is_self = (near[0] == dp) & (near[1] == lane)
+
+    def deal_on(i, moved, near_out, far_out):
+        deals[i][0].wait()
+        for c in deals[i][1]:
+            c.wait_recv()
+        stay = pltpu.make_async_copy(moved, near_out, loc.at[7 + i])
+        go = send(moved, near_out, s_t.at[i, 0], r_t.at[i, 0], near)
+        off = send(moved, far_out, s_b.at[0 if i == 0 else 4], r_b.at[0 if i == 0 else 4], far)
+        pl.when(is_self)(lambda: stay.start())
+        pl.when(jnp.logical_not(is_self))(lambda: go.start())
+        off.start()
+        return stay, go, off
+
+    routes = [deal_on(0, moved_t, near_t, far_t)]
+    for t in range(LANES - 1):
+        for g in range(n_g):
+            turns[g][t].wait_recv()
+            ready(g, t + 1)
+        if t == 0:
+            for c in deals[1][1]:
+                c.start()
+    for g in range(n_g):
+        for k in range(LANES):
+            side = 0 if k < LANES // 2 else 1
+            planes[g][k][side].wait_recv()
+            fars[g][k].start()
+    routes.append(deal_on(1, moved_c, near_c, far_c))
+    for g in range(n_g):
+        for k in range(LANES):
+            planes[g][k][1 if k < LANES // 2 else 0].wait_recv()
+            fars[g][k].wait_recv()
+    for stay, go, off in routes:
+        pl.when(is_self)(lambda: stay.wait())
+        pl.when(jnp.logical_not(is_self))(lambda: go.wait())
+        off.wait()
+    keep_small.wait()
+    for c in smalls:
+        c.wait()
+    for i in range(2):
+        for c in deals[i][1]:
+            c.wait_send()
+    for g in range(n_g):
+        firsts[g].wait_send()
+        for c in turns[g]:
+            c.wait_send()
+        for k in range(LANES):
+            for c in planes[g][k]:
+                c.wait_send()
+            fars[g][k].wait_send()
+
+
+def gather_call(widths, own, other, small, tok, cot):
+    d = own.shape[0] * 8
+    n = len(widths)
+    tile = jax.ShapeDtypeStruct(tok.shape, BF)
+    dma = pltpu.SemaphoreType.DMA
+    return pl.pallas_call(
+        partial(gather_kernel, widths),
+        in_specs=[IN_VMEM, IN_VMEM, IN_VMEM, IN_VMEM, IN_VMEM],
+        out_specs=[ANY] * n + [IN_VMEM] * 5,
+        out_shape=[jax.ShapeDtypeStruct((d, LANES * w), BF) for w in widths] + [tile] * 4
+        + [jax.ShapeDtypeStruct((LANES * small.shape[0], small.shape[1]), F32)],
+        scratch_shapes=[pltpu.VMEM(tok.shape, BF), pltpu.VMEM(tok.shape, BF), dma((10,)), dma((n,)), dma((n,)), dma((n, 3)), dma((n, 3)),
+                        dma((n, 4, 2)), dma((n, 4, 2)), dma((n, 4)), dma((n, 4)), dma((2, 8)), dma((2, 8)), dma((5,)), dma((5,))],
+        compiler_params=pltpu.CompilerParams(collective_id=1, has_side_effects=True, vmem_limit_bytes=48 << 20),
+        name="gather",
+    )(own, other, small, tok, cot)
+
+
+def scatter_kernel(widths, mask_ref, vec_ref, res, grd, *rest):
+    n_g = len(widths)
+    grads, rest = rest[:n_g], rest[n_g:]
+    outs, (out_res, out_grd, out_vec), rest = rest[:n_g], rest[n_g:n_g + 3], rest[n_g + 3:]
+    first, second, summed, turned, third, done = (rest[i * n_g:(i + 1) * n_g] for i in range(6))
+    rest = rest[6 * n_g:]
+    near_in, far_in, moved, vec_in, loc, s_1, r_1, s_2, r_2, s_z, r_z, s_c, r_c, s_t, r_t, s_v, r_v = rest
+    dp, lane = lax.axis_index("dp"), lax.axis_index("tensor")
+    n_dp = 8
+    core = dp % 2
+    per = grads[0].shape[0] // 4
+    wd = per // 2
+    meet(dp, lane, n_dp)
+    near, far = home_route(dp, lane)
+    is_self = (near[0] == dp) & (near[1] == lane)
+    backs = []
+    for i, src in enumerate((res, grd)):
+        stay = pltpu.make_async_copy(src, near_in.at[i], loc.at[i])
+        go = send(src, near_in.at[i], s_t.at[i, 0], r_t.at[i, 0], near)
+        off = send(src, far_in.at[i], s_t.at[i, 8], r_t.at[i, 8], far)
+        pl.when(is_self)(lambda: stay.start())
+        pl.when(jnp.logical_not(is_self))(lambda: go.start())
+        off.start()
+        backs.append((stay, go, off))
+
+    def first_copies(g, k):
+        w = widths[g]
+        cols = slice(k * w, (k + 1) * w)
+        side = 1 if k < 2 else 2
+        return [send(grads[g].at[q * per:(q + 1) * per, cols], first[g].at[i, :, cols], s_1.at[g, k, i], r_1.at[g, k, i], (dp ^ (2 * side), lane))
+                for i, q in enumerate((3, side))]
+
+    def second_copy(g, k):
+        w = widths[g]
+        cols = slice(k * w, (k + 1) * w)
+        side = 2 if k < 2 else 1
+        return send(summed[g].at[:, cols], second[g].at[:, cols], s_2.at[g, k], r_2.at[g, k], (dp ^ (2 * side), lane))
+
+    def turn_copy(g, k):
+        w = widths[g]
+        return send(summed[g].at[:, k * w:(k + 1) * w], turned[g].at[k], s_z.at[g, k], r_z.at[g, k], (dp, lax.rem(lane + LANES - k, LANES)))
+
+    firsts = [[first_copies(g, k) for k in range(LANES)] for g in range(n_g)]
+    seconds = [[second_copy(g, k) for k in range(LANES)] for g in range(n_g)]
+    turns = [[None] + [turn_copy(g, k) for k in range(1, LANES)] for g in range(n_g)]
+    for g in range(n_g):
+        for i in range(2):
+            for k in range(LANES):
+                firsts[g][k][i].start()
+
+    out_vec[...] = vec_ref[...]
+    partners = [(dp ^ 1, lane), (dp ^ 2, lane), (dp ^ 4, lane), (dp, lane ^ 1), (dp, lane ^ 2)]
+
+    def vec_round(i):
+        c = send(out_vec, vec_in.at[i], s_v.at[i], r_v.at[i], partners[i])
+        c.start()
+        return c
+
+    def vec_end(c, i):
+        c.wait()
+        out_vec[...] = out_vec[...] + vec_in[i]
+
+    rounds = 0
+    for g in range(n_g):
+        for k in range(LANES):
+            w = widths[g]
+            cols = slice(k * w, (k + 1) * w)
+            firsts[g][k][0].wait_recv()
+            q = 2 if k < 2 else 1
+            summed[g][:, cols] = (grads[g][q * per:(q + 1) * per, cols].astype(F32) + first[g][0, :, cols].astype(F32)).astype(BF)
+            seconds[g][k].start()
+        if rounds < 5:
+            c = vec_round(rounds)
+            vec_end(c, rounds)
+            rounds += 1
+    while rounds < 5:
+        c = vec_round(rounds)
+        vec_end(c, rounds)
+        rounds += 1
+
+    block = res.shape[0] // n_dp
+    here = pl.ds(pl.multiple_of(dp * block, block), block)
+    deals = []
+    for i, dst in enumerate((out_res, out_grd)):
+        stay, go, off = backs[i]
+        pl.when(is_self)(lambda: stay.wait())
+        pl.when(jnp.logical_not(is_self))(lambda: go.wait())
+        off.wait()
+        moved[i] = jnp.where(mask_ref[...] > 0, near_in[i].astype(F32), far_in[i].astype(F32)).astype(BF)
+        keep = pltpu.make_async_copy(moved.at[i, here], dst.at[here], loc.at[2 + i])
+        keep.start()
+        copies = []
+        for d in range(1, n_dp):
+            there = pl.ds(pl.multiple_of((dp ^ d) * block, block), block)
+            copies.append(send(moved.at[i, there], dst.at[here], s_t.at[i, d], r_t.at[i, d], (dp ^ d, lane)))
+            copies[-1].start()
+        deals.append((keep, copies))
+
+    for g in range(n_g):
+        for k in (1, 2, 3, 0):
+            w = widths[g]
+            cols = slice(k * w, (k + 1) * w)
+            firsts[g][k][1].wait_recv()
+            seconds[g][k].wait()
+            summed[g][:, cols] = (grads[g][0:per, cols].astype(F32) + first[g][1, :, cols].astype(F32) + second[g][:, cols].astype(F32)).astype(BF)
+            if k:
+                turns[g][k].start()
+
+    lasts = []
+    for g in range(n_g):
+        w = widths[g]
+        for k in range(1, LANES):
+            turns[g][k].wait_recv()
+        done[g][...] = summed[g][:, 0:w].astype(F32) + turned[g][1].astype(F32) + turned[g][2].astype(F32) + turned[g][3].astype(F32)
+        mine = pl.ds(pl.multiple_of(core * wd, wd), wd)
+        other = pl.ds(pl.multiple_of((1 - core) * wd, wd), wd)
+        third[g][0] = done[g][other, :].astype(BF)
+        outs[g][core] = done[g][mine, :]
+        c = send(third[g].at[0], third[g].at[1], s_c.at[g], r_c.at[g], (dp ^ 1, lane))
+        c.start()
+        lasts.append(c)
+    for g in range(n_g):
+        lasts[g].wait()
+        outs[g][1 - core] = third[g][1].astype(F32)
+    for keep, copies in deals:
+        keep.wait()
+        for c in copies:
+            c.wait()
+    for g in range(n_g):
+        for k in range(LANES):
+            for c in firsts[g][k]:
+                c.wait_send()
+            if k:
+                turns[g][k].wait_send()
+
+
+def scatter_call(widths, mask, vec, res, grd, grads):
+    n = len(widths)
+    d = grads[0].shape[0]
+    per = d // 4
+    dma = pltpu.SemaphoreType.DMA
+    vm = pltpu.VMEM
+    tile = jax.ShapeDtypeStruct(res.shape, BF)
+    scratch = (
+        [vm((2, per, LANES * w), BF) for w in widths] + [vm((per, LANES * w), BF) for w in widths] + [vm((per, LANES * w), BF) for w in widths]
+        + [vm((LANES, per, w), BF) for w in widths] + [vm((2, per // 2, w), BF) for w in widths] + [vm((per, w), F32) for w in widths]
+        + [vm((2,) + res.shape, BF)] * 3 + [vm((5,) + vec.shape, F32)]
+        + [dma((4,)), dma((n, 4, 2)), dma((n, 4, 2)), dma((n, 4)), dma((n, 4)), dma((n, 4)), dma((n, 4)), dma((n,)), dma((n,)),
+           dma((2, 9)), dma((2, 9)), dma((5,)), dma((5,))]
+    )
+    return pl.pallas_call(
+        partial(scatter_kernel, widths),
+        in_specs=[IN_VMEM] * (4 + n),
+        out_specs=[IN_VMEM] * (n + 3),
+        out_shape=[jax.ShapeDtypeStruct((2, per // 2, w), F32) for w in widths] + [tile, tile, jax.ShapeDtypeStruct(vec.shape, F32)],
+        scratch_shapes=scratch,
+        compiler_params=pltpu.CompilerParams(collective_id=2, has_side_effects=True, vmem_limit_bytes=62 << 20),
+        name="scatter",
+    )(mask, vec, res, grd, *grads)
+
+
 def feature_turn(x):
     n = lax.axis_size("dp") // 2
     chip = lax.axis_index("dp") // 2
@@ -288,21 +635,28 @@
         return (lax.dynamic_slice_in_dim(x, core * w, w, x.ndim - 1), lax.dynamic_slice_in_dim(x, (1 - core) * w, w, x.ndim - 1))
 
     qm, qo = halves(w_qkv)
-    flat = lambda x: jnp.concatenate([x[0], x[1], x[2]], axis=1)
-    qkv_blocks = gather_weights(flat(qm), flat(qo))
     om, oo = halves(w_o.T)
     um, uo = halves(w_1)
     dm, do = halves(w_2.T)
-    up_blocks = gather_weights(jnp.concatenate([om, um], axis=1), jnp.concatenate([oo, uo], axis=1))
-    down_blocks = gather_weights(dm, do)
+    own = jnp.concatenate([qm[0], qm[1], qm[2], om, um, dm], axis=1)
+    other = jnp.concatenate([qo[0], qo[1], qo[2], oo, uo, do], axis=1)
     hw, fw = om.shape[1], um.shape[1]
-
-    biases = lax.all_gather(jnp.concatenate([b_qv.reshape(-1), b_1]), "tensor")
+    widths = (3 * hw, hw, fw, fw)
+    small = jnp.concatenate([halves(b_qv[0:1])[0], halves(b_qv[1:2])[0], halves(b_1[None])[0]], axis=1)
+    small = jnp.concatenate([small, jnp.zeros((7, small.shape[1]), F32)])
     order = (lane - jnp.arange(lanes)) % lanes
-    biases = jnp.take(biases, order, axis=0)
-    cut_bias = lambda x: lax.dynamic_slice_in_dim(x, core * (x.shape[1] // 2), x.shape[1] // 2, 1).reshape(-1)
-    nq = b_qv.shape[1]
-    bias_q, bias_v, bias_1 = cut_bias(biases[:, :nq]), cut_bias(biases[:, nq:2 * nq]), cut_bias(biases[:, 2 * nq:])
+    kernels = n_dp == 8 and lanes == LANES
+    if kernels:
+        wq, wo, w1, w2, near_t, far_t, near_c, far_c, smalls = gather_call(widths, own, other, small, tokens, cotangent)
+        smalls = smalls[::8]
+        dealt_tok, dealt_cot = jnp.where(keep, near_t, far_t), jnp.where(keep, near_c, far_c)
+    else:
+        blocks = gather_weights(own, other)
+        wq, wo, w1, w2 = (weight_of(blocks, sum(widths[:i]), w) for i, w in enumerate(widths))
+        dealt_tok, dealt_cot = deal_in(tokens), deal_in(cotangent)
+        smalls = jnp.take(lax.all_gather(small[0], "tensor"), order, axis=0)
+    bias_q, bias_v, bias_1 = smalls[:, :hw], smalls[:, hw:2 * hw], smalls[:, 2 * hw:].reshape(-1)
+    bias_qkv = jnp.concatenate([bias_q, jnp.zeros_like(bias_q), bias_v], axis=1).reshape(-1)
     gain, shift = feature_turn(ln_gain), feature_turn(ln_bias)
     bias_o, bias_2 = feature_turn(b_o[None])[0], feature_turn(b_2[None])[0]
 
@@ -312,77 +666,76 @@
     def fold(x):
         return x[:rows] + swap_dp(x[rows:].astype(BF), 1).astype(F32)
 
-    hidden = feature_turn(deal_in(tokens)).astype(F32)
-    normed_in = join(scaled_norm(hidden, gain[0], shift[0]).astype(BF))
-    weights_q, weights_k, weights_v = (weight_of(qkv_blocks, i * hw, hw) for i in range(3))
     mm = partial(jnp.dot, preferred_element_type=F32)
     mm_t = lambda a, b: lax.dot_general(a, b, (((1,), (1,)), ((), ())), preferred_element_type=F32)
     mm_g = lambda a, b: lax.dot_general(a, b, (((0,), (0,)), ((), ())), preferred_element_type=F32)
-    q = (mm(normed_in, weights_q) + bias_q).astype(BF)
-    k = mm(normed_in, weights_k).astype(BF)
-    v = (mm(normed_in, weights_v) + bias_v).astype(BF)
-    heads_out, lse = attn_forward(qpos, qstart, kpos, q, k, v)
-    weights_o = weight_of(up_blocks, 0, hw)
-    attn_out = fold(mm_t(heads_out, weights_o)) + bias_o
+    hidden = feature_turn(dealt_tok).astype(F32)
+    normed_in = join(scaled_norm(hidden, gain[0], shift[0]).astype(BF))
+    qkv = (mm(normed_in, wq) + bias_qkv).astype(BF)
+    heads_out, lse = attn_forward(qpos, qstart, kpos, qkv)
+    attn_out = fold(mm_t(heads_out, wo)) + bias_o
     first_sum = hidden + scaled_norm(attn_out, gain[1], shift[1])
     normed_mid = join(scaled_norm(first_sum, gain[2], shift[2]).astype(BF))
-    weights_1 = weight_of(up_blocks, hw, fw)
-    pre_act = mm(normed_mid, weights_1) + bias_1
+    pre_act = mm(normed_mid, w1) + bias_1
     act = jax.nn.gelu(pre_act, approximate=False).astype(BF)
-    weights_2 = weight_of(down_blocks, 0, fw)
-    ffn_out = fold(mm_t(act, weights_2)) + bias_2
-    result = first_sum + scaled_norm(ffn_out, gain[3], shift[3])
-    output = deal_out(feature_turn(result.astype(BF)))
-
-    grad_result = feature_turn(deal_in(cotangent)).astype(F32)
+    ffn_out = fold(mm_t(act, w2)) + bias_2
+    result = feature_turn((first_sum + scaled_norm(ffn_out, gain[3], shift[3])).astype(BF))
+
+    grad_result = feature_turn(dealt_cot).astype(F32)
     grad_ffn, gain_3, shift_3 = norm_back(ffn_out, gain[3], shift[3], grad_result)
     grad_ffn_low = grad_ffn.astype(BF)
     bias_2_grad = jnp.sum(grad_ffn_low.astype(F32), axis=0)
     grad_ffn_full = join(grad_ffn_low)
-    grad_act = mm(grad_ffn_full, weights_2)
-    down_grad = scatter_grads([mm_g(grad_ffn_full, act)])
+    grad_act = mm(grad_ffn_full, w2)
+    down_part = mm_g(grad_ffn_full, act).astype(BF)
     _, gelu_pull = jax.vjp(partial(jax.nn.gelu, approximate=False), pre_act)
     grad_pre = gelu_pull(grad_act)[0].astype(BF)
     bias_1_grad = jnp.sum(grad_pre.astype(F32), axis=0)
-    grad_mid = fold(mm_t(grad_pre, weights_1))
-    up_part = mm_g(normed_mid, grad_pre)
+    grad_mid = fold(mm_t(grad_pre, w1))
+    up_part = mm_g(normed_mid, grad_pre).astype(BF)
     grad_first_part, gain_2, shift_2 = norm_back(first_sum, gain[2], shift[2], grad_mid)
     grad_first = grad_result + grad_first_part
     grad_attn, gain_1, shift_1 = norm_back(attn_out, gain[1], shift[1], grad_first)
     grad_attn_low = grad_attn.astype(BF)
     bias_o_grad = jnp.sum(grad_attn_low.astype(F32), axis=0)
     grad_attn_full = join(grad_attn_low)
-    grad_heads = mm(grad_attn_full, weights_o).astype(BF)
-    out_up_grad = scatter_grads([mm_g(grad_attn_full, heads_out), up_part])
-    grad_q, grad_k, grad_v = attn_backward(qpos, qstart, kpos, lse, q, grad_heads, k, v)
-    bias_q_grad = jnp.sum(grad_q.astype(F32), axis=0)
-    bias_v_grad = jnp.sum(grad_v.astype(F32), axis=0)
-    grad_in = fold(mm_t(grad_q, weights_q) + mm_t(grad_k, weights_k) + mm_t(grad_v, weights_v))
+    grad_heads = mm(grad_attn_full, wo).astype(BF)
+    out_part = mm_g(grad_attn_full, heads_out).astype(BF)
+    grad_qkv = attn_backward(qpos, qstart, kpos, lse, grad_heads, qkv)
+    bias_qkv_grad = jnp.sum(grad_qkv.astype(F32), axis=0).reshape(lanes, 3, hw)
+    grad_in = fold(mm_t(grad_qkv, wq))
+    qkv_part = mm_g(normed_in, grad_qkv).astype(BF)
     grad_hidden_part, gain_0, shift_0 = norm_back(hidden, gain[0], shift[0], grad_in)
-    input_grad = deal_out(feature_turn((grad_first + grad_hidden_part).astype(BF)))
-    qkv_grad = scatter_grads([mm_g(normed_in, g) for g in (grad_q, grad_k, grad_v)])
+    grad_hidden = feature_turn((grad_first + grad_hidden_part).astype(BF))
 
     def by_lane(x):
         x = jnp.take(x.reshape(lanes, -1), order, axis=0)
         both_halves = jnp.stack([jnp.where(core == 0, x, 0.0), jnp.where(core == 1, x, 0.0)], axis=1)
         return both_halves.reshape(-1)
 
+    d = tokens.shape[1]
     stack = jnp.stack([gain_0, gain_1, gain_2, gain_3, shift_0, shift_1, shift_2, shift_3, bias_o_grad, bias_2_grad])
-    vector = jnp.concatenate([feature_turn(stack).reshape(-1), by_lane(bias_q_grad), by_lane(bias_v_grad), by_lane(bias_1_grad)])
-    vector = lax.psum(vector, both)
-    d = tokens.shape[1]
+    vector = jnp.concatenate([feature_turn(stack).reshape(-1), by_lane(bias_qkv_grad[:, 0]), by_lane(bias_qkv_grad[:, 2]), by_lane(bias_1_grad)])
+    parts = [qkv_part, out_part, up_part, down_part]
+    if kernels:
+        mask = jnp.broadcast_to(keep_home.astype(jnp.int32), (rows, 128))[:, :1]
+        *shards, output, input_grad, vector = scatter_call(widths, mask, vector.reshape(-1, 128), result, grad_hidden, parts)
+        vector = vector.reshape(-1)
+    else:
+        output, input_grad = deal_out(result), deal_out(grad_hidden)
+        vector = lax.psum(vector, both)
+        shards = [scatter_grads([p.astype(F32)]) for p in parts]
     gain_total, shift_total = vector[:4 * d].reshape(4, d), vector[4 * d:8 * d].reshape(4, d)
     bias_o_total, bias_2_total = vector[8 * d:9 * d], vector[9 * d:10 * d]
-    e = d
-    own = lambda x: lax.dynamic_slice_in_dim(x.reshape(lanes, -1), lane, 1, 0)[0]
-    bias_qv_total = jnp.stack([own(vector[10 * d:10 * d + e]), own(vector[10 * d + e:10 * d + 2 * e])])
-    bias_1_total = own(vector[10 * d + 2 * e:])
+    mine = lambda x: lax.dynamic_slice_in_dim(x.reshape(lanes, -1), lane, 1, 0)[0]
+    bias_qv_total = jnp.stack([mine(vector[10 * d:11 * d]), mine(vector[11 * d:12 * d])])
+    bias_1_total = mine(vector[12 * d:])
 
     spread = lambda x: jnp.concatenate([x[0], x[1]], axis=-1)
+    qkv_grad, out_grad, up_grad, down_grad = shards
     qkv_out = jnp.stack([spread(qkv_grad[:, :, i * hw:(i + 1) * hw]) for i in range(3)])
     return (
-        output, input_grad, qkv_out,
-        spread(out_up_grad[:, :, :hw]).T, spread(out_up_grad[:, :, hw:]), spread(down_grad).T,
+        output, input_grad, qkv_out, spread(out_grad).T, spread(up_grad), spread(down_grad).T,
         bias_qv_total, bias_o_total, bias_1_total, bias_2_total, gain_total, shift_total,
     )
 

time: 1010 us -> 618 us (0.61); the launches traced: 993 us -> 613 us
  waiting for transfers between devices: 339 us -> 4.85 us
  Pallas kernels: 54.8 us -> 388 us
  starting transfers between devices: 136 us -> 13.5 us
  other arithmetic: 164 us -> 55.8 us
  matrix products: 155 us -> 89 us
  local copies, waits for them, and re-layouts: 114 us -> 60.3 us
  between operations: 19 us -> 2.42 us
  blocking collectives: 10.5 us -> 0 us
    pallas_call x0 -> x2, Pallas kernels: none -> 332 us  [the longest x1 190 us: scatter_call(): pl.pallas_call(partial(scatter_kernel, widths), in_specs=[IN_VMEM] * (4 +...]
    ppermute x26 -> x0, waiting for transfers between devices: 133 us -> none  [the longest x18 51.9 us: turn(): return lax.ppermute(x, 'tensor', [(i, (i + shift) % n) for i in range(n)])]
    psum x1 -> x0, waiting for transfers between devices: 113 us -> none  [body(): vector = lax.psum(vector, both)]
    all_to_all x4 -> x0, waiting for transfers between devices: 61.1 us -> none  [the longest x2 45.3 us: deal_in(): moved = lax.all_to_all(x, 'dp', split_axis=0, concat_axis=0, tiled=True)]
    concatenate x5 -> x2, other arithmetic: 59.5 us -> 0.01 us  [the longest x1 0.01 us: body(): jnp.concatenate([halves(b_qv[0:1])[0], halves(b_qv[1:2])[0], halves(b_1[N...]
    ppermute x38 -> x8, starting transfers between devices: 65 us -> 13.5 us  [swap_dp(): return lax.ppermute(x, 'dp', [(i, i ^ bit) for i in range(n)])]
    ppermute x26 -> x0, starting transfers between devices: 51 us -> none  [the longest x18 36.1 us: turn(): return lax.ppermute(x, 'tensor', [(i, (i + shift) % n) for i in range(n)])]
    dot_general x6 -> x4, matrix products: 66.6 us -> 17.2 us  [body(): lax.dot_general(a, b, (((1,), (1,)), ((), ())), preferred_element_type=F32)]
  transfers between devices with their start and end apart: 69 -> 8, of which waited for: 22 -> 2; matrix products, arithmetic and copies ran while one was open for 33% -> 9% of each run, Pallas kernels for 6% -> 0%
where the time goes in v2:
time: 618 us; the launch traced here: 613 us
  Pallas kernels  388 us (63%)
  matrix products  89 us (14%)
  local copies, waits for them, and re-layouts  60.3 us (10%)
  other arithmetic  55.8 us (9%)
  starting transfers between devices  13.5 us (2%)
    pallas_call x1, Pallas kernels, scatter_call(): pl.pallas_call(partial(scatter_kernel, widths), in_specs=[IN_VMEM] * (4 +...  190 us
    pallas_call x1, Pallas kernels, gather_call(): pl.pallas_call(partial(gather_kernel, widths), in_specs=[IN_VMEM, IN_VMEM...  142 us
    pallas_call x1, Pallas kernels, attn_backward(): pl.pallas_call(attn_bwd_kernel, grid=(rows // QB,), in_specs=[col, col, p...  35.1 us
    dot_general x4, matrix products, body(): lax.dot_general(a, b, (((0,), (0,)), ((), ())), preferred_element_type=F32)  25.7 us
    dot_general x1, matrix products, body(): pre_act = mm(normed_mid, w1) + bias_1  24.4 us
    pallas_call x1, Pallas kernels, attn_forward(): pl.pallas_call(attn_fwd_kernel, grid=(rows // QB,), in_specs=[col, col, p...  20.1 us
    dot_general x4, matrix products, body(): lax.dot_general(a, b, (((1,), (1,)), ((), ())), preferred_element_type=F32)  17.2 us
    unnamed x154, local copies, waits for them, and re-layouts  17 us
  transfers between devices with their start and end apart: 8, of which 2 were waited for; matrix products, arithmetic and copies ran while one was open for 9% of the time, Pallas kernels for 0%

profile of v2, /device:TPU:1, one launch (start us, length us, event | category | flops | bytes accessed | tf_op | source)
XLA Modules:
  0.0 613.4 jit_solution(11970372601097874447)
XLA Ops:
  5.3 1.0 constant_dynamic-slice_fusion.5
  10.1 142.4 %gather.21 = (bf16[1024,1536]{1,0:T(8,128)(2,1)}, bf16[1024,512]{1,0:T(8,128)(2,1)S(1)}, bf16[1024,2048]{1,0:T(8,128)(2,1)}, bf16[1024,2048]{1,0:T(8,128)(2,1)},...) custom-call(bf16[128,1536]{1,0:T(8,128)(2,1)S(1)} %bitcast_dynamic-u, ...), custom_call_target="tpu_custom_call" | custom-call | tf_op jit(solution)/shard_map/gather/pallas_call | solution.py:409
  152.5 1.2 broadcast_select_fusion
  153.8 1.7 reshape.612
  155.5 1.4 copy.137
  157.4 1.5 fusion.35
  160.0 1.3 convert_reduce_fusion.2
  161.9 2.9 copy.139
  164.8 3.0 add_convert_fusion.4
  167.8 12.0 %collective-permute-start = (bf16[512,1024]{0,1:T(8,128)(2,1)}, bf16[512,1024]{0,1:T(8,128)(2,1)}, u32[]{:S(2)}, u32[]{:S(2)}) collective-permute-start(bf16[512,1024]{0,1:T(8,128)(2,1)} %add_convert_fusion.4), channel_id=1, source_target_pairs={{0,4},{4,0},{8,12},{12,8},{16,20},{20,16},{24,28},{28,24},{1,5},{5... | collective-permute-start | bytes 3145736 | tf_op jit(solution)/shard_map/ppermute | solution.py:145
  183.0 6.0 add_convert_fusion.1.qkv_ref
  189.0 20.1 %attn_fwd.1 = (bf16[1024,512]{1,0:T(8,128)(2,1)S(1)}, f32[1024,128]{1,0:T(8,128)S(1)}) custom-call(s32[1024,1]{1,0:T(8,128)S(1)} %select_n.361.qpos_ref, s32[1024,1]{1,0:T(8,128)S(1)} %copy.147.qstart_ref, s32[1,1024]{1,0:T(1,128)S(1)} %compare_select_fusion.kpos_ref, bf16[1024,1536]{1,0:T(8,128)(2,1)S(1)} %add_convert_fusion.1.qkv_ref), custom_call_target="tpu_custom_call" | custom-call | flops 2147483648 | bytes 4194304 | tf_op jit(solution)/shard_map/attn_fwd/pallas_call | solution.py:65
  209.2 3.2 fusion.78
  212.4 1.7 slice.316
  214.6 2.3 collective-permute-done.1
  216.9 1.9 abs_reduce_fusion.2
  220.1 1.0 copy-done.11
  222.9 2.5 collective-permute-done.2
  225.4 24.4 %multiply_convert_fusion = (bf16[1024,2048]{1,0:T(8,128)(2,1)S(1)}, f32[1024,2048]{1,0:T(8,128)}, f32[1024,2048]{1,0:T(8,128)}) fusion(f32[2048]{0:T(1024)S(1)} %bitcast.245, bf16[1024,2048]{1,0:T(8,128)(2,1)S(1)} %copy-done.48, bf16[512,1024]{0,1:T(8,128)(2,1)S(1)} %collective-permute-done.2, bf16[512,1024]{0,1:T(8,128)(2,1)S(1)} %add_convert_fusion.3), kind=kOutput, calls=%fused_computation.7 | convolution fusion | flops 4437573632 | bytes 27271168 | tf_op jit(solution)/shard_map/dot_general | solution.py:679
  249.8 4.5 fusion.79
  254.4 1.9 copy-done.20
  256.3 1.2 slice.315
  257.7 2.6 reshape.615
  260.3 1.4 copy.144
  261.7 1.2 reverse_select_fusion.5
  262.8 3.2 fusion.32
  266.0 3.2 copy.146
  269.3 2.2 abs_reduce_fusion
  271.7 1.3 copy-done.13
  274.2 1.5 fusion.25
  275.7 3.4 convert_reduce_fusion.3
  280.3 1.4 fusion.34.mask_ref
  281.7 1.9 fusion.33
  283.6 2.3 copy.153
  285.9 1.8 reverse_select_fusion.3
  287.7 13.0 %convert_reduce_fusion = (f32[2048]{0:T(1024)S(1)}, bf16[1024,2048]{1,0:T(8,128)(2,1)S(1)}) fusion(f32[1024,2048]{1,0:T(8,128)} %get-tuple-element.154, bf16[1024,2048]{1,0:T(8,128)(2,1)} %get-tuple-element.41, bf16[512,1024]{0,1:T(8,128)(2,1)} %collective-permute-done.4, bf16[512,1024]{0,1:T(8,128)(2,1)} %get-tuple-element.145, ...), kind=kOutput, calls=%fused_computation.5 | convolution fusion | flops 4334811136 | bytes 27279360 | tf_op jit(solution)/shard_map/dot_general | solution.py:689
  300.8 4.5 fusion.80
  305.3 1.3 slice.314
  306.8 1.2 reverse_select_fusion.2
  308.0 3.3 copy.155
  311.3 2.6 reshape.623.res
  314.4 9.4 %convolution_convert_fusion.1.rest_3_ = bf16[1024,2048]{1,0:T(8,128)(2,1)} fusion(bf16[1024,2048]{1,0:T(8,128)(2,1)} %copy-done.54, bf16[512,1024]{0,1:T(8,128)(2,1)} %collective-permute-done.4, bf16[512,1024]{0,1:T(8,128)(2,1)} %get-tuple-element.145), kind=kOutput, calls=%fused_computation.24 | convolution fusion | flops 4301258752 | bytes 10485760 | tf_op jit(solution)/shard_map/dot_general | solution.py:671
  323.8 2.6 multiply_reduce_fusion.1
  326.4 2.0 fusion.69
  330.6 2.5 fusion.64
  333.8 1.3 multiply_reduce_fusion.2
  335.2 2.0 convert_reduce_fusion.4
  337.7 6.0 convolution_convert_fusion.2.rest_2_
  343.9 2.6 convolution_convert_fusion.4.g_ref
  346.5 35.1 %attn_bwd.1 = bf16[1024,1536]{1,0:T(8,128)(2,1)S(1)} custom-call(s32[1024,1]{1,0:T(8,128)S(1)} %copy-done.5, s32[1024,1]{1,0:T(8,128)S(1)} %copy-done.3, s32[1,1024]{1,0:T(1,128)S(1)} %compare_select_fusion.kpos_ref, f32[1024,128]{1,0:T(8,128)S(1)} %copy-done.8, bf16[1024,512]{1,0:T(8,128)(2,1)S(1)} %convolution_convert_fusion.4.g_ref, ...), custom_call_target="tpu_custom_call" | custom-call | flops 5368709120 | bytes 7340032 | tf_op jit(solution)/shard_map/attn_bwd/pallas_call | solution.py:129
  382.1 1.4 copy-done.51
  383.5 5.0 fusion.81
  389.7 1.9 slice.313
  391.8 3.5 convolution_convert_fusion.3.rest_1_
  395.3 6.8 %convolution_convert_fusion.rest_0_ = bf16[1024,1536]{1,0:T(8,128)(2,1)} fusion(bf16[1024,1536]{1,0:T(8,128)(2,1)S(1)} %attn_bwd.1, bf16[512,1024]{0,1:T(8,128)(2,1)} %collective-permute-done, bf16[512,1024]{0,1:T(8,128)(2,1)} %add_convert_fusion.4), kind=kOutput, calls=%fused_computation.23 | convolution fusion | flops 3226992640 | bytes 8388608 | tf_op jit(solution)/shard_map/dot_general | solution.py:671
  402.2 1.0 multiply_reduce_fusion
  407.5 1.1 copy.158
  408.6 1.5 reshape.625.grd
  411.2 190.0 %scatter.1 = (f32[2,128,384]{2,1,0:T(8,128)}, f32[2,128,128]{2,1,0:T(8,128)}, f32[2,128,512]{2,1,0:T(8,128)}, f32[2,128,512]{2,1,0:T(8,128)}, bf16[512,1024]{1,0...) custom-call(s32[512,1]{1,0:T(8,128)} %fusion.34.mask_ref, f32[128,128]{1,0:T(8,128)} %maximum_bitcast_fusion.5.vec_ref, ...), custom_call_target="tpu_custom_call" | custom-call | tf_op jit(solution)/shard_map/scatter/pallas_call | solution.py:572
  601.1 1.4 slice_bitcast_fusion.21
  606.8 1.0 slice_bitcast_fusion.11
  608.0 1.0 copy.160
  611.3 1.0 copy.203
  612.2 1.0 copy.204
  (299 shorter events, 37.7 us)
Async XLA Ops:
  0.6 9.4 %copy-start.29 = (bf16[128,1024]{1,0:T(8,128)(2,1)S(1)}, bf16[128,1024]{1,0:T(8,128)(2,1)}, u32[]{:S(2)}) copy-start(bf16[128,1024]{1,0:T(8,128)(2,1)} %param.22) | copy-start | bytes 786436
  157.1 1.9 copy-start.42
  157.1 1.9 copy-start.43
  157.4 3.8 copy-start.36
  159.4 5.3 copy-start.32
  160.0 4.7 copy-start.30
  161.3 3.5 copy-start.34
  161.8 2.9 copy-start.40
  161.8 2.9 copy-start.38
  167.8 15.2 %collective-permute-start = (bf16[512,1024]{0,1:T(8,128)(2,1)}, bf16[512,1024]{0,1:T(8,128)(2,1)}, u32[]{:S(2)}, u32[]{:S(2)}) collective-permute-start(bf16[512,1024]{0,1:T(8,128)(2,1)} %add_convert_fusion.4), channel_id=1, source_target_pairs={{0,4},{4,0},{8,12},{12,8},{16,20},{20,16},{24,28},{28,24},{1,5},{5... | collective-permute-start | bytes 3145736 | tf_op jit(solution)/shard_map/ppermute | solution.py:145
  181.7 7.4 %copy-start.2 = (s32[1024,1]{1,0:T(8,128)}, s32[1024,1]{1,0:T(8,128)S(1)}, u32[]{:S(2)}) copy-start(s32[1024,1]{1,0:T(8,128)S(1)} %copy.147.qstart_ref) | copy-start | bytes 12292
  182.3 6.7 %copy-start.4 = (s32[1024,1]{1,0:T(8,128)}, s32[1024,1]{1,0:T(8,128)S(1)}, u32[]{:S(2)}) copy-start(s32[1024,1]{1,0:T(8,128)S(1)} %select_n.361.qpos_ref) | copy-start | bytes 12292
  189.0 20.1 %copy-start.6 = (bf16[1024,1536]{1,0:T(8,128)(2,1)}, bf16[1024,1536]{1,0:T(8,128)(2,1)S(1)}, u32[]{:S(2)}) copy-start(bf16[1024,1536]{1,0:T(8,128)(2,1)S(1)} %add_convert_fusion.1.qkv_ref) | copy-start | bytes 9437188
  209.1 3.2 copy-start
  209.1 3.2 copy-start.7
  212.4 1.8 copy-start.46
  212.4 1.9 copy-start.47
  214.1 2.7 collective-permute-start.1
  218.8 1.4 copy-start.9
  218.8 2.3 copy-start.11
  221.9 3.5 copy-start.48
  222.7 27.1 %copy-start.21 = (bf16[512,1024]{0,1:T(8,128)(2,1)}, bf16[512,1024]{0,1:T(8,128)(2,1)S(1)}, u32[]{:S(2)}) copy-start(bf16[512,1024]{0,1:T(8,128)(2,1)S(1)} %add_convert_fusion.3) | copy-start | bytes 3145732
  222.7 2.7 collective-permute-start.2
  225.4 24.4 %copy-start.52 = (bf16[512,1024]{0,1:T(8,128)(2,1)}, bf16[512,1024]{0,1:T(8,128)(2,1)S(1)}, u32[]{:S(2)}) copy-start(bf16[512,1024]{0,1:T(8,128)(2,1)S(1)} %collective-permute-done.2) | copy-start | bytes 3145732
  225.4 24.4 %copy-start.50 = (bf16[1024,2048]{1,0:T(8,128)(2,1)S(1)}, bf16[1024,2048]{1,0:T(8,128)(2,1)}, u32[]{:S(2)}) copy-start(bf16[1024,2048]{1,0:T(8,128)(2,1)} %get-tuple-element.41) | copy-start | bytes 12582916
  249.8 4.6 copy-start.54
  254.4 1.9 copy-start.20
  257.5 11.8 %collective-permute-start.3 = (bf16[512,1024]{0,1:T(8,128)(2,1)}, bf16[512,1024]{0,1:T(8,128)(2,1)}, u32[]{:S(2)}, u32[]{:S(2)}) collective-permute-start(bf16[512,1024]{0,1:T(8,128)(2,1)} %slice.315), channel_id=1, source_target_pairs={{0,4},{4,0},{8,12},{12,8},{16,20},{20,16},{24,28},{28,24},{1,5},{5... | collective-permute-start | bytes 3145736 | tf_op jit(solution)/shard_map/ppermute | solution.py:145
  271.5 1.6 copy-start.13
  279.1 8.6 %collective-permute-start.4 = (bf16[512,1024]{0,1:T(8,128)(2,1)}, bf16[512,1024]{0,1:T(8,128)(2,1)}, u32[]{:S(2)}, u32[]{:S(2)}) collective-permute-start(bf16[512,1024]{0,1:T(8,128)(2,1)} %get-tuple-element.145), channel_id=1, source_target_pairs={{0,4},{4,0},{8,12},{12,8},{16,20},{20,16},{24,28},{28,24},{1,5},{5... | collective-permute-start | bytes 3145736 | tf_op jit(solution)/shard_map/ppermute | solution.py:145
  287.7 13.1 %copy-start.49 = (bf16[1024,2048]{1,0:T(8,128)(2,1)S(1)}, bf16[1024,2048]{1,0:T(8,128)(2,1)}, u32[]{:S(2)}) copy-start(bf16[1024,2048]{1,0:T(8,128)(2,1)} %get-tuple-element.40) | copy-start | bytes 12582916
  300.8 4.6 copy-start.55
  305.3 2.7 copy-start.17
  306.6 17.2 %collective-permute-start.5 = (bf16[512,1024]{0,1:T(8,128)(2,1)}, bf16[512,1024]{0,1:T(8,128)(2,1)}, u32[]{:S(2)}, u32[]{:S(2)}) collective-permute-start(bf16[512,1024]{0,1:T(8,128)(2,1)} %slice.314), channel_id=1, source_target_pairs={{0,4},{4,0},{8,12},{12,8},{16,20},{20,16},{24,28},{28,24},{1,5},{5... | collective-permute-start | bytes 3145736 | tf_op jit(solution)/shard_map/ppermute | solution.py:145
  314.4 9.4 %copy-start.18 = (f32[1024,1024]{0,1:T(8,128)S(1)}, f32[1024,1024]{0,1:T(8,128)}, u32[]{:S(2)}) copy-start(f32[1024,1024]{0,1:T(8,128)} %copy-done.17) | copy-start | bytes 12582916
  328.4 1.6 copy-start.10
  328.4 2.2 copy-start.14
  333.1 2.0 copy-start.15
  333.8 3.9 copy-start.56
  335.1 2.6 copy-start.22
  335.1 2.6 copy-start.53
  337.1 6.7 %copy-start.25 = (bf16[512,1024]{0,1:T(8,128)(2,1)}, bf16[512,1024]{0,1:T(8,128)(2,1)S(1)}, u32[]{:S(2)}) copy-start(bf16[512,1024]{0,1:T(8,128)(2,1)S(1)} %get-tuple-element.147) | copy-start | bytes 3145732
  337.1 6.7 %collective-permute-start.6 = (bf16[512,1024]{0,1:T(8,128)(2,1)S(1)}, bf16[512,1024]{0,1:T(8,128)(2,1)}, u32[]{:S(2)}, u32[]{:S(2)}) collective-permute-start(bf16[512,1024]{0,1:T(8,128)(2,1)S(1)} %get-tuple-element.147), channel_id=1, source_target_pairs={{0,4},{4,0},{8,12},{12,8},{16,20},{20,16},{24,28},{28,24},{1,5},{5... | collective-permute-start | bytes 3145736 | tf_op jit(solution)/shard_map/ppermute | solution.py:145
  343.8 2.7 copy-start.3
  343.8 2.7 copy-start.5
  343.8 2.7 copy-start.8
  381.6 1.9 copy-start.51
  389.6 2.2 copy-start.1
  389.6 2.2 copy-start.26
  391.6 10.5 %collective-permute-start.7 = (bf16[512,1024]{0,1:T(8,128)(2,1)S(1)}, bf16[512,1024]{0,1:T(8,128)(2,1)S(1)}, u32[]{:S(2)}, u32[]{:S(2)}) collective-permute-start(bf16[512,1024]{0,1:T(8,128)(2,1)S(1)} %slice.313), channel_id=1, source_target_pairs={{0,4},{4,0},{8,12},{12,8},{16,20},{20,16},{24,28},{28,24},{1,5},{5... | collective-permute-start | bytes 3145736 | tf_op jit(solution)/shard_map/ppermute | solution.py:145
  395.3 6.8 %copy-start.12 = (f32[512,2,2,256]{0,3,2,1:T(8,128)S(1)}, f32[512,2,2,256]{0,3,2,1:T(8,128)}, u32[]{:S(2)}) copy-start(f32[512,2,2,256]{0,3,2,1:T(8,128)} %copy.139) | copy-start | bytes 6291460
  395.3 6.8 %copy-start.19 = (f32[1024,1024]{0,1:T(8,128)S(1)}, f32[1024,1024]{0,1:T(8,128)}, u32[]{:S(2)}) copy-start(f32[1024,1024]{0,1:T(8,128)} %fusion.81) | copy-start | bytes 12582916
  395.3 6.8 %copy-start.31 = (f32[512]{0:T(512)S(1)}, f32[512]{0:T(512)}, u32[]{:S(2)}) copy-start(f32[512]{0:T(512)} %copy-done.30) | copy-start | bytes 6148
  395.3 6.8 %copy-start.33 = (f32[2,2,2,128]{3,1,2,0:T(2,128)S(1)}, f32[2,2,2,128]{3,1,2,0:T(2,128)}, u32[]{:S(2)}) copy-start(f32[2,2,2,128]{3,1,2,0:T(2,128)} %copy-done.32) | copy-start | bytes 12292
  395.3 6.9 %copy-start.35 = (f32[512]{0:T(512)S(1)}, f32[512]{0:T(512)}, u32[]{:S(2)}) copy-start(f32[512]{0:T(512)} %copy-done.34) | copy-start | bytes 6148
  395.3 6.9 %copy-start.39 = (f32[512]{0:T(512)S(1)}, f32[512]{0:T(512)}, u32[]{:S(2)}) copy-start(f32[512]{0:T(512)} %copy-done.38) | copy-start | bytes 6148
  402.1 1.1 copy-start.41
  403.3 0.7 copy-start.44
  404.0 1.6 copy-start.16
  404.0 1.6 copy-start.37
  601.1 6.7 %copy-start.28 = (f32[2,128,512]{2,1,0:T(8,128)S(1)}, f32[2,128,512]{2,1,0:T(8,128)}, u32[]{:S(2)}) copy-start(f32[2,128,512]{2,1,0:T(8,128)} %get-tuple-element.46) | copy-start | bytes 1572868
  601.1 6.8 %copy-start.27 = (f32[2,128,512]{2,1,0:T(8,128)S(1)}, f32[2,128,512]{2,1,0:T(8,128)}, u32[]{:S(2)}) copy-start(f32[2,128,512]{2,1,0:T(8,128)} %get-tuple-element.47) | copy-start | bytes 1572868
  608.0 3.3 copy-start.24
  609.6 2.6 copy-start.23
  (1 other events, 0.7 us)

commit v3 on v2

--- a/solution.py
+++ b/solution.py
@@ -279,64 +279,109 @@
     return pltpu.make_async_remote_copy(src_ref=src, dst_ref=dst, send_sem=send_sem, recv_sem=recv_sem, device_id=device, device_id_type=MESH)
 
 
-def gather_kernel(widths, own, other, small, tok, cot, *rest):
-    mats, (near_t, far_t, near_c, far_c, small_out), rest = rest[:4], rest[4:9], rest[9:]
-    moved_t, moved_c, loc, s_c, r_c, s_z, r_z, s_p, r_p, s_d, r_d, s_t, r_t, s_b, r_b = rest
+DEAL_CUTS = 4
+
+
+def norm_parts(x):
+    peak = jnp.max(jnp.abs(x), axis=-1, keepdims=True) + NORM_EPS
+    u = x * (1.0 / peak)
+    c = u - jnp.mean(u, axis=-1, keepdims=True)
+    return c, lax.rsqrt(jnp.mean(c * c, axis=-1, keepdims=True) + NORM_EPS)
+
+
+def norm_rows(x, gain, shift):
+    c, r = norm_parts(x)
+    return c * r * gain + shift
+
+
+def dot_t(a, b):
+    return lax.dot_general(a, b, (((1,), (1,)), ((), ())), preferred_element_type=F32)
+
+
+class Sems:
+    def __init__(self, ref):
+        self.ref, self.used = ref, 0
+
+    def take(self, count=1):
+        self.used += count
+        return self.used - count
+
+
+FWD_SEMS = 320
+
+
+def forward_kernel(widths, own, other, small, tok, cot, keep, qpos, qstart, kpos, vec, *rest):
+    outs, rest = rest[:18], rest[18:]
+    (wq_o, wo_o, w1_o, w2_o, h_o, xin_o, qkv_o, heads_o, lse_o, attn_o, first_o, xmid_o, act_o, dg_o, ffn_o, res_o, grd_o, small_o) = outs
+    (wq, wo, w1, w2, moved, cand, h, xin, qkv, heads, lse, part, sbuf, rbuf, first, xmid, act, dg, stage, small_in, sem_ref) = rest
+    mats = (wq, wo, w1, w2)
+    sems = Sems(sem_ref)
     dp, lane = lax.axis_index("dp"), lax.axis_index("tensor")
     n_dp = 8
-    core = dp % 2
+    core, chip = dp % 2, dp // 2
+    rows, d = tok.shape
     wd = own.shape[0]
+    quarter = d // 4
     up = lax.rem(lane + 1, LANES)
+    n_g = len(widths)
+    mate = (dp ^ 1, lane)
+    ends = []
+
+    def local(src, dst):
+        c = pltpu.make_async_copy(src, dst, sem_ref.at[sems.take()])
+        return c
+
+    def remote(src, dst, device):
+        s, r = sems.take(), sems.take()
+        c = send(src, dst, sem_ref.at[s], sem_ref.at[r], device)
+        ends.append(c.wait_send)
+        return c
+
     meet(dp, lane, n_dp)
-    block = tok.shape[0] // n_dp
-    started, deals = [], []
-    for i, (src, dst) in enumerate(((tok, moved_t), (cot, moved_c))):
-        here = pl.ds(pl.multiple_of(dp * block, block), block)
-        keep = pltpu.make_async_copy(src.at[here], dst.at[here], loc.at[i])
-        keep.start()
+    block = rows // n_dp
+    here = pl.ds(pl.multiple_of(dp * block, block), block)
+    deals = []
+    for i, src in enumerate((tok, cot)):
+        stay = local(src.at[here], moved.at[i, here])
         copies = []
-        for d in range(1, n_dp):
-            there = pl.ds(pl.multiple_of((dp ^ d) * block, block), block)
-            copies.append(send(src.at[there], dst.at[here], s_t.at[i, d], r_t.at[i, d], (dp ^ d, lane)))
-        deals.append((keep, copies))
+        for k in range(1, n_dp):
+            there = pl.ds(pl.multiple_of((dp ^ k) * block, block), block)
+            copies.append(remote(src.at[there], moved.at[i, here], (dp ^ k, lane)))
+        deals.append((stay, copies))
+
+    def deal_start(i):
+        deals[i][0].start()
+        for c in deals[i][1]:
+            c.start()
+
+    deal_start(0)
     feat = pl.ds(pl.multiple_of(core * wd, wd), wd)
-    at, locals_, firsts = 0, [], []
+    at, stays, pairs = 0, [], []
     for g, w in enumerate(widths):
         dst = mats[g].at[feat, 0:w]
-        locals_.append(pltpu.make_async_copy(own.at[:, at:at + w], dst, loc.at[2 + g]))
-        firsts.append(send(other.at[:, at:at + w], dst, s_c.at[g], r_c.at[g], (dp ^ 1, lane)))
-        locals_[-1].start()
-        firsts[-1].start()
+        stays.append(local(own.at[:, at:at + w], dst))
+        pairs.append(remote(other.at[:, at:at + w], dst, mate))
+        stays[g].start()
+        pairs[g].start()
         at += w
-    for c in deals[0][1]:
+    n_s = small.shape[0]
+    smalls = [remote(small, small_in.at[k], (dp, lax.rem(lane + k, LANES))) for k in range(1, LANES)]
+    for c in smalls:
         c.start()
-    smalls = []
-    for k in range(1, LANES):
-        rows = small.shape[0]
-        smalls.append(send(small, small_out.at[k * rows:(k + 1) * rows], s_b.at[k], r_b.at[k], (dp, lax.rem(lane + k, LANES))))
-        smalls[-1].start()
-    keep_small = pltpu.make_async_copy(small, small_out.at[0:small.shape[0]], loc.at[6])
-    keep_small.start()
-
-    def turn_copy(g, t):
+    small_in[0] = small[...]
+
+    def area(g, q, k):
         w = widths[g]
-        return send(mats[g].at[0:2 * wd, t * w:(t + 1) * w], mats[g].at[0:2 * wd, (t + 1) * w:(t + 2) * w], s_z.at[g, t], r_z.at[g, t], (dp, up))
-
-    def plane_copy(g, k, side):
-        w = widths[g]
-        return send(mats[g].at[0:2 * wd, k * w:(k + 1) * w], mats[g].at[2 * wd * side:2 * wd * (side + 1), k * w:(k + 1) * w],
-                    s_p.at[g, k, side - 1], r_p.at[g, k, side - 1], (dp ^ (2 * side), lane))
-
-    def far_copy(g, k):
-        w = widths[g]
-        side, via = (1, 2) if k < LANES // 2 else (2, 1)
-        return send(mats[g].at[2 * wd * side:2 * wd * (side + 1), k * w:(k + 1) * w], mats[g].at[6 * wd:8 * wd, k * w:(k + 1) * w],
-                    s_d.at[g, k], r_d.at[g, k], (dp ^ (2 * via), lane))
-
-    n_g = len(widths)
-    turns = [[turn_copy(g, t) for t in range(LANES - 1)] for g in range(n_g)]
-    planes = [[[plane_copy(g, k, side) for side in (1, 2)] for k in range(LANES)] for g in range(n_g)]
-    fars = [[far_copy(g, k) for k in range(LANES)] for g in range(n_g)]
+        return mats[g].at[2 * wd * q:2 * wd * (q + 1), k * w:(k + 1) * w]
+
+    turns = [[remote(area(g, 0, t), area(g, 0, t + 1), (dp, up)) for t in range(LANES - 1)] for g in range(n_g)]
+    planes = [[[remote(area(g, 0, k), area(g, side, k), (dp ^ (2 * side), lane)) for side in (1, 2)] for k in range(LANES)] for g in range(n_g)]
+    fars = []
+    for g in range(n_g):
+        fars.append([])
+        for k in range(LANES):
+            side, via = (1, 2) if k < LANES // 2 else (2, 1)
+            fars[g].append(remote(area(g, side, k), area(g, 3, k), (dp ^ (2 * via), lane)))
 
     def ready(g, k):
         if k < LANES - 1:
@@ -344,79 +389,314 @@
         for c in planes[g][k]:
             c.start()
 
-    for g in range(n_g):
-        locals_[g].wait()
-        firsts[g].wait_recv()
+    def pair_in(g):
+        stays[g].wait()
+        pairs[g].wait_recv()
         ready(g, 0)
-    near, far = deal_route(dp, lane)
-    is_self = (near[0] == dp) & (near[1] == lane)
-
-    def deal_on(i, moved, near_out, far_out):
+
+    def turn_in(g, t):
+        turns[g][t].wait_recv()
+        ready(g, t + 1)
+
+    def far_go(g, k):
+        planes[g][k][0 if k < LANES // 2 else 1].wait_recv()
+        fars[g][k].start()
+
+    def all_in(g):
+        for k in range(LANES):
+            planes[g][k][1 if k < LANES // 2 else 0].wait_recv()
+            fars[g][k].wait_recv()
+
+    pack = lane // 2
+    spot = chip * 2 + lane % 2
+    to_near, to_far = (spot, core + 1), (spot, 3 * core)
+    same_side = lane // 2 == core
+    slot = jnp.where(same_side, 1, 0)
+    is_self = (lane == 3 * core) & (spot == dp)
+    to_far_remote = same_side & jnp.logical_not(is_self)
+    is_near = lane == pack + 1
+    cut = rows // DEAL_CUTS
+
+    class Route:
+        def __init__(self, i):
+            a0, b0, f0 = sems.take(DEAL_CUTS), sems.take(DEAL_CUTS), sems.take(DEAL_CUTS)
+            got = sems.take(2 * DEAL_CUTS)
+            self.got = got
+            self.near, self.far, self.self_, self.hand, self.wait0, self.wait1 = [], [], [], [], [], []
+            for n in range(DEAL_CUTS):
+                rs = slice(n * cut, (n + 1) * cut)
+                src = moved.at[i, rs]
+                self.near.append(send(src, cand.at[i, slot, rs], sem_ref.at[a0 + n], sem_ref.at[got + n * 2 + slot], to_near))
+                self.far.append(send(src, cand.at[i, 0, rs], sem_ref.at[b0 + n], sem_ref.at[got + n * 2], to_far))
+                self.self_.append(pltpu.make_async_copy(src, cand.at[i, 0, rs], sem_ref.at[got + n * 2]))
+                self.hand.append(send(cand.at[i, 0, rs], cand.at[i, 1, rs], sem_ref.at[f0 + n], sem_ref.at[got + n * 2 + 1], (dp, 3 * pack)))
+                self.wait0.append(send(src, cand.at[i, 0, rs], sem_ref.at[b0 + n], sem_ref.at[got + n * 2], to_far))
+                self.wait1.append(send(src, cand.at[i, 1, rs], sem_ref.at[b0 + n], sem_ref.at[got + n * 2 + 1], to_far))
+
+        def start(self):
+            for n in range(DEAL_CUTS):
+                self.near[n].start()
+                pl.when(to_far_remote)(lambda: self.far[n].start())
+                pl.when(is_self)(lambda: self.self_[n].start())
+
+        def arrive(self, n):
+            pl.when(is_self)(lambda: self.self_[n].wait())
+            pl.when(jnp.logical_not(is_self))(lambda: self.wait0[n].wait_recv())
+            pl.when(is_near)(lambda: self.hand[n].start())
+            self.wait1[n].wait_recv()
+
+        def finish(self):
+            for n in range(DEAL_CUTS):
+                self.near[n].wait_send()
+                pl.when(to_far_remote)(lambda: self.far[n].wait_send())
+                pl.when(is_near)(lambda: self.hand[n].wait_send())
+
+    routes = [Route(0), Route(1)]
+
+    def deal_on(i):
         deals[i][0].wait()
         for c in deals[i][1]:
             c.wait_recv()
-        stay = pltpu.make_async_copy(moved, near_out, loc.at[7 + i])
-        go = send(moved, near_out, s_t.at[i, 0], r_t.at[i, 0], near)
-        off = send(moved, far_out, s_b.at[0 if i == 0 else 4], r_b.at[0 if i == 0 else 4], far)
-        pl.when(is_self)(lambda: stay.start())
-        pl.when(jnp.logical_not(is_self))(lambda: go.start())
-        off.start()
-        return stay, go, off
-
-    routes = [deal_on(0, moved_t, near_t, far_t)]
+        routes[i].start()
+
+    def choose(i, n):
+        rs = slice(n * cut, (n + 1) * cut)
+        on = keep[rs, :] > 0
+        parts = []
+        for q in range(4):
+            cols = pl.ds(pl.multiple_of((chip ^ q) * quarter, quarter), quarter)
+            parts.append(jnp.where(on, cand[i, 0, rs, cols].astype(F32), cand[i, 1, rs, cols].astype(F32)))
+        return jnp.concatenate(parts, axis=1)
+
+    out_copies = []
+
+    def put(src, dst):
+        c = local(src, dst)
+        c.start()
+        out_copies.append(c)
+
+    pair_in(0)
+    turn_in(0, 0)
+    turn_in(0, 1)
+    deal_on(0)
+    turn_in(0, 2)
+    pending = []
+    for g in (1, 2, 3):
+        pending.append((lambda g=g: pair_in(g)))
     for t in range(LANES - 1):
-        for g in range(n_g):
-            turns[g][t].wait_recv()
-            ready(g, t + 1)
-        if t == 0:
-            for c in deals[1][1]:
-                c.start()
-    for g in range(n_g):
+        for g in (1, 2, 3):
+            pending.append((lambda g=g, t=t: turn_in(g, t)))
+    for g in (1, 2, 3):
         for k in range(LANES):
-            side = 0 if k < LANES // 2 else 1
-            planes[g][k][side].wait_recv()
-            fars[g][k].start()
-    routes.append(deal_on(1, moved_c, near_c, far_c))
-    for g in range(n_g):
-        for k in range(LANES):
-            planes[g][k][1 if k < LANES // 2 else 0].wait_recv()
-            fars[g][k].wait_recv()
-    for stay, go, off in routes:
-        pl.when(is_self)(lambda: stay.wait())
-        pl.when(jnp.logical_not(is_self))(lambda: go.wait())
-        off.wait()
-    keep_small.wait()
+            pending.append((lambda g=g, k=k: far_go(g, k)))
+    pending.append(lambda: deal_start(1))
+    pending.append(lambda: deal_on(1))
+
+    def pump(count):
+        for _ in range(min(count, len(pending))):
+            pending.pop(0)()
+
+    for k in range(LANES):
+        far_go(0, k)
+    pump(3)
+    joins = []
+
+    def join_send(x, n, size):
+        c = remote(x.at[n * size:(n + 1) * size], x.at[rows + n * size:rows + (n + 1) * size], mate)
+        c.start()
+        joins.append(c)
+
+    gains = lambda i: vec[i:i + 1, :]
+    for n in range(DEAL_CUTS):
+        rs = slice(n * cut, (n + 1) * cut)
+        routes[0].arrive(n)
+        x = choose(0, n)
+        h[rs, :] = x.astype(BF)
+        xin[rs, :] = norm_rows(x, gains(0), gains(4)).astype(BF)
+        join_send(xin, n, cut)
+    pump(3)
     for c in smalls:
+        c.wait_recv()
+    all_in(0)
+    for c in joins:
+        c.wait_recv()
+    put(wq, wq_o)
+    put(h, h_o)
+    put(xin, xin_o)
+    w = widths[0]
+    third = w // 3
+    for k in range(LANES):
+        cols = slice(k * w, (k + 1) * w)
+        row = small_in[k, 0:1, :]
+        bias = jnp.concatenate([row[:, 0:third], jnp.zeros((1, third), F32), row[:, third:2 * third]], axis=1)
+
+        def project(r, carry, cols=cols, bias=bias):
+            rs = pl.ds(pl.multiple_of(r * QB, QB), QB)
+            qkv[rs, cols] = (jnp.dot(xin[rs, :], wq[:, cols], preferred_element_type=F32) + bias).astype(BF)
+            return carry
+
+        lax.fori_loop(0, 2 * rows // QB, project, 0)
+    put(qkv, qkv_o)
+    pump(3)
+
+    def attend(i, carry):
+        begin = pl.multiple_of(i * QB, QB)
+        rs = pl.ds(begin, QB)
+        allowed = (kpos[...] <= qpos[rs, :]) & (kpos[...] >= qstart[rs, :])
+        bias = jnp.where(allowed, 0.0, MASKED_OUT)
+        attn_block(rs, bias, qkv, heads, lse)
+        return carry
+
+    for i in range(2):
+        lax.fori_loop(2 * i, 2 * i + 2, attend, 0)
+        pump(6)
+    put(heads, heads_o)
+    put(lse, lse_o)
+    all_in(1)
+    put(wo, wo_o)
+
+    def fold(x, w_ref, which):
+        copies = []
+        per = 2
+        size = rows // per
+        for n in range(per):
+            rs = slice(rows + n * size, rows + (n + 1) * size)
+            sbuf[which, n * size:(n + 1) * size] = dot_t(x[rs, :], w_ref[...]).astype(BF)
+            c = remote(sbuf.at[which, n * size:(n + 1) * size], rbuf.at[which, n * size:(n + 1) * size], mate)
+            c.start()
+            copies.append(c)
+        for n in range(per):
+            rs = slice(n * size, (n + 1) * size)
+            part[rs, :] = dot_t(x[rs, :], w_ref[...])
+        return copies
+
+    copies = fold(heads, wo, 0)
+    pump(3)
+    joins.clear()
+    size = rows // 2
+    for n in range(2):
+        copies[n].wait_recv()
+
+        def middle(m, carry, n=n):
+            rs = pl.ds(pl.multiple_of(n * size + m * cut, cut), cut)
+            y = part[rs, :] + rbuf[0, rs].astype(F32) + gains(8)
+            part[rs, :] = y
+            f = h[rs, :].astype(F32) + norm_rows(y, gains(1), gains(5))
+            first[rs, :] = f
+            xmid[rs, :] = norm_rows(f, gains(2), gains(6)).astype(BF)
+            return carry
+
+        lax.fori_loop(0, size // cut, middle, 0)
+        join_send(xmid, n, size)
+    attn_put = local(part, attn_o)
+    attn_put.start()
+    put(first, first_o)
+    pump(4)
+    all_in(2)
+    put(w1, w1_o)
+    for c in joins:
+        c.wait_recv()
+    put(xmid, xmid_o)
+    w = widths[2]
+    for k in range(LANES):
+        cols = slice(k * w, (k + 1) * w)
+        bias = small_in[k, 0:1, 2 * third:2 * third + w]
+
+        def hidden_units(r, carry, cols=cols, bias=bias):
+            rs = pl.ds(pl.multiple_of(r * QB, QB), QB)
+            pre = jnp.dot(xmid[rs, :], w1[:, cols], preferred_element_type=F32) + bias
+            cdf = 0.5 + 0.5 * lax.erf(pre * 0.7071067811865476)
+            act[rs, cols] = (pre * cdf).astype(BF)
+            dg[rs, cols] = (cdf + pre * (0.3989422804014327 * jnp.exp(-0.5 * pre * pre))).astype(BF)
+            return carry
+
+        lax.fori_loop(0, 2 * rows // QB, hidden_units, 0)
+        pump(3)
+    pump(len(pending))
+    put(act, act_o)
+    put(dg, dg_o)
+    all_in(3)
+    put(w2, w2_o)
+    attn_put.wait()
+    copies = fold(act, w2, 1)
+    for n in range(DEAL_CUTS):
+        routes[1].arrive(n)
+        rs = slice(n * cut, (n + 1) * cut)
+        stage[1, rs] = choose(1, n).astype(BF)
+    put(stage.at[1], grd_o)
+    for n in range(2):
+        copies[n].wait_recv()
+
+        def last(m, carry, n=n):
+            rs = pl.ds(pl.multiple_of(n * size + m * cut, cut), cut)
+            y = part[rs, :] + rbuf[1, rs].astype(F32) + gains(9)
+            part[rs, :] = y
+            out = first[rs, :] + norm_rows(y, gains(3), gains(7))
+            for q in range(4):
+                cols = pl.ds(pl.multiple_of((chip ^ q) * quarter, quarter), quarter)
+                stage[0, rs, cols] = out[:, q * quarter:(q + 1) * quarter].astype(BF)
+            return carry
+
+        lax.fori_loop(0, size // cut, last, 0)
+    put(part, ffn_o)
+    put(stage.at[0], res_o)
+    put(small_in, small_o)
+    for c in out_copies:
         c.wait()
     for i in range(2):
-        for c in deals[i][1]:
-            c.wait_send()
-    for g in range(n_g):
-        firsts[g].wait_send()
-        for c in turns[g]:
-            c.wait_send()
-        for k in range(LANES):
-            for c in planes[g][k]:
-                c.wait_send()
-            fars[g][k].wait_send()
-
-
-def gather_call(widths, own, other, small, tok, cot):
-    d = own.shape[0] * 8
-    n = len(widths)
-    tile = jax.ShapeDtypeStruct(tok.shape, BF)
-    dma = pltpu.SemaphoreType.DMA
+        routes[i].finish()
+    for wait in ends:
+        wait()
+
+
+def attn_block(rs, bias, qkv, heads, lse):
+    lane = lax.broadcasted_iota(jnp.int32, (1, PAIR), 1)
+    wide = lax.broadcasted_iota(jnp.int32, (QB, 128), 1)
+    stats = jnp.zeros((QB, 128), F32)
+    for pair in range(heads.shape[1] // PAIR):
+        at = 3 * pair * PAIR
+        query = qkv[rs, at:at + PAIR]
+        key, value = qkv[:, at + PAIR:at + 2 * PAIR], qkv[:, at + 2 * PAIR:at + 3 * PAIR]
+        total = jnp.zeros(query.shape, F32)
+        for side in range(2):
+            mine = (lane >= side * DH) & (lane < (side + 1) * DH)
+            piece = jnp.where(mine, query * 0.125, 0.0).astype(BF)
+            score = dot_t(piece, key) + bias
+            peak = jnp.max(score, axis=-1, keepdims=True)
+            expo = jnp.exp(score - peak)
+            norm = jnp.sum(expo, axis=-1, keepdims=True)
+            prob = (expo * (1.0 / norm)).astype(BF)
+            total += jnp.dot(prob, jnp.where(mine, value, jnp.zeros_like(value)), preferred_element_type=F32)
+            stats = jnp.where(wide == pair * 2 + side, peak + jnp.log(norm), stats)
+        heads[rs, pair * PAIR:(pair + 1) * PAIR] = total.astype(BF)
+    lse[rs, :] = stats
+
+
+def forward_call(widths, own, other, small, tok, cot, keep, qpos, qstart, kpos, vec):
+    rows, d = tok.shape
+    both = 2 * rows
+    vm = pltpu.VMEM
+    hidden = LANES * widths[2]
+    mats = [(d, LANES * w) for w in widths]
+    shape = jax.ShapeDtypeStruct
+    out = [shape(m, BF) for m in mats] + [
+        shape((rows, d), BF), shape((both, d), BF), shape((both, LANES * widths[0]), BF), shape((both, LANES * widths[1]), BF), shape((both, 128), F32),
+        shape((rows, d), F32), shape((rows, d), F32), shape((both, d), BF), shape((both, hidden), BF), shape((both, hidden), BF),
+        shape((rows, d), F32), shape((rows, d), BF), shape((rows, d), BF), shape((LANES,) + small.shape, F32)]
+    scratch = [vm(m, BF) for m in mats] + [
+        vm((2, rows, d), BF), vm((2, 2, rows, d), BF), vm((rows, d), BF), vm((both, d), BF), vm((both, LANES * widths[0]), BF),
+        vm((both, LANES * widths[1]), BF), vm((both, 128), F32), vm((rows, d), F32), vm((2, rows, d), BF), vm((2, rows, d), BF),
+        vm((rows, d), F32), vm((both, d), BF), vm((both, hidden), BF), vm((both, hidden), BF), vm((2, rows, d), BF),
+        vm((LANES,) + small.shape, F32), pltpu.SemaphoreType.DMA((FWD_SEMS,))]
     return pl.pallas_call(
-        partial(gather_kernel, widths),
-        in_specs=[IN_VMEM, IN_VMEM, IN_VMEM, IN_VMEM, IN_VMEM],
-        out_specs=[ANY] * n + [IN_VMEM] * 5,
-        out_shape=[jax.ShapeDtypeStruct((d, LANES * w), BF) for w in widths] + [tile] * 4
-        + [jax.ShapeDtypeStruct((LANES * small.shape[0], small.shape[1]), F32)],
-        scratch_shapes=[pltpu.VMEM(tok.shape, BF), pltpu.VMEM(tok.shape, BF), dma((10,)), dma((n,)), dma((n,)), dma((n, 3)), dma((n, 3)),
-                        dma((n, 4, 2)), dma((n, 4, 2)), dma((n, 4)), dma((n, 4)), dma((2, 8)), dma((2, 8)), dma((5,)), dma((5,))],
-        compiler_params=pltpu.CompilerParams(collective_id=1, has_side_effects=True, vmem_limit_bytes=48 << 20),
-        name="gather",
-    )(own, other, small, tok, cot)
+        partial(forward_kernel, widths),
+        in_specs=[IN_VMEM] * 10,
+        out_specs=[ANY] * len(out),
+        out_shape=out,
+        scratch_shapes=scratch,
+        compiler_params=pltpu.CompilerParams(collective_id=1, has_side_effects=True, vmem_limit_bytes=67043328),
+        name="forward",
+    )(own, other, small, tok, cot, keep, qpos, qstart, kpos, vec)
 
 
 def scatter_kernel(widths, mask_ref, vec_ref, res, grd, *rest):
@@ -646,50 +926,52 @@
     small = jnp.concatenate([small, jnp.zeros((7, small.shape[1]), F32)])
     order = (lane - jnp.arange(lanes)) % lanes
     kernels = n_dp == 8 and lanes == LANES
+    gain, shift = feature_turn(ln_gain), feature_turn(ln_bias)
+    bias_o, bias_2 = feature_turn(b_o[None])[0], feature_turn(b_2[None])[0]
+
+    def join(x):
+        return jnp.concatenate([x, swap_dp(x, 1)], axis=0)
+
+    def fold(x):
+        return x[:rows] + swap_dp(x[rows:].astype(BF), 1).astype(F32)
+
+    mm = partial(jnp.dot, preferred_element_type=F32)
+    mm_t = lambda a, b: lax.dot_general(a, b, (((1,), (1,)), ((), ())), preferred_element_type=F32)
+    mm_g = lambda a, b: lax.dot_general(a, b, (((0,), (0,)), ((), ())), preferred_element_type=F32)
     if kernels:
-        wq, wo, w1, w2, near_t, far_t, near_c, far_c, smalls = gather_call(widths, own, other, small, tokens, cotangent)
-        smalls = smalls[::8]
-        dealt_tok, dealt_cot = jnp.where(keep, near_t, far_t), jnp.where(keep, near_c, far_c)
+        vec = jnp.concatenate([gain, shift, bias_o[None], bias_2[None], jnp.zeros((6, tokens.shape[1]), F32)])
+        (wq, wo, w1, w2, hid, normed_in, qkv, heads_out, lse, attn_out, first_sum, normed_mid, act, dgelu, ffn_out, result, dealt_cot,
+         _) = forward_call(widths, own, other, small, tokens, cotangent, keep.astype(jnp.int32), qpos, qstart, kpos, vec)
+        hidden = hid.astype(F32)
+        grad_result = dealt_cot.astype(F32)
     else:
         blocks = gather_weights(own, other)
         wq, wo, w1, w2 = (weight_of(blocks, sum(widths[:i]), w) for i, w in enumerate(widths))
-        dealt_tok, dealt_cot = deal_in(tokens), deal_in(cotangent)
         smalls = jnp.take(lax.all_gather(small[0], "tensor"), order, axis=0)
-    bias_q, bias_v, bias_1 = smalls[:, :hw], smalls[:, hw:2 * hw], smalls[:, 2 * hw:].reshape(-1)
-    bias_qkv = jnp.concatenate([bias_q, jnp.zeros_like(bias_q), bias_v], axis=1).reshape(-1)
-    gain, shift = feature_turn(ln_gain), feature_turn(ln_bias)
-    bias_o, bias_2 = feature_turn(b_o[None])[0], feature_turn(b_2[None])[0]
-
-    def join(x):
-        return jnp.concatenate([x, swap_dp(x, 1)], axis=0)
-
-    def fold(x):
-        return x[:rows] + swap_dp(x[rows:].astype(BF), 1).astype(F32)
-
-    mm = partial(jnp.dot, preferred_element_type=F32)
-    mm_t = lambda a, b: lax.dot_general(a, b, (((1,), (1,)), ((), ())), preferred_element_type=F32)
-    mm_g = lambda a, b: lax.dot_general(a, b, (((0,), (0,)), ((), ())), preferred_element_type=F32)
-    hidden = feature_turn(dealt_tok).astype(F32)
-    normed_in = join(scaled_norm(hidden, gain[0], shift[0]).astype(BF))
-    qkv = (mm(normed_in, wq) + bias_qkv).astype(BF)
-    heads_out, lse = attn_forward(qpos, qstart, kpos, qkv)
-    attn_out = fold(mm_t(heads_out, wo)) + bias_o
-    first_sum = hidden + scaled_norm(attn_out, gain[1], shift[1])
-    normed_mid = join(scaled_norm(first_sum, gain[2], shift[2]).astype(BF))
-    pre_act = mm(normed_mid, w1) + bias_1
-    act = jax.nn.gelu(pre_act, approximate=False).astype(BF)
-    ffn_out = fold(mm_t(act, w2)) + bias_2
-    result = feature_turn((first_sum + scaled_norm(ffn_out, gain[3], shift[3])).astype(BF))
-
-    grad_result = feature_turn(dealt_cot).astype(F32)
+        bias_q, bias_v, bias_1 = smalls[:, :hw], smalls[:, hw:2 * hw], smalls[:, 2 * hw:].reshape(-1)
+        bias_qkv = jnp.concatenate([bias_q, jnp.zeros_like(bias_q), bias_v], axis=1).reshape(-1)
+        hidden = feature_turn(deal_in(tokens)).astype(F32)
+        normed_in = join(scaled_norm(hidden, gain[0], shift[0]).astype(BF))
+        qkv = (mm(normed_in, wq) + bias_qkv).astype(BF)
+        heads_out, lse = attn_forward(qpos, qstart, kpos, qkv)
+        attn_out = fold(mm_t(heads_out, wo)) + bias_o
+        first_sum = hidden + scaled_norm(attn_out, gain[1], shift[1])
+        normed_mid = join(scaled_norm(first_sum, gain[2], shift[2]).astype(BF))
+        pre_act = mm(normed_mid, w1) + bias_1
+        cdf = 0.5 + 0.5 * lax.erf(pre_act * 0.7071067811865476)
+        act = (pre_act * cdf).astype(BF)
+        dgelu = (cdf + pre_act * (0.3989422804014327 * jnp.exp(-0.5 * pre_act * pre_act))).astype(BF)
+        ffn_out = fold(mm_t(act, w2)) + bias_2
+        result = feature_turn((first_sum + scaled_norm(ffn_out, gain[3], shift[3])).astype(BF))
+        grad_result = feature_turn(deal_in(cotangent)).astype(F32)
+
     grad_ffn, gain_3, shift_3 = norm_back(ffn_out, gain[3], shift[3], grad_result)
     grad_ffn_low = grad_ffn.astype(BF)
     bias_2_grad = jnp.sum(grad_ffn_low.astype(F32), axis=0)
     grad_ffn_full = join(grad_ffn_low)
     grad_act = mm(grad_ffn_full, w2)
     down_part = mm_g(grad_ffn_full, act).astype(BF)
-    _, gelu_pull = jax.vjp(partial(jax.nn.gelu, approximate=False), pre_act)
-    grad_pre = gelu_pull(grad_act)[0].astype(BF)
+    grad_pre = (grad_act * dgelu.astype(F32)).astype(BF)
     bias_1_grad = jnp.sum(grad_pre.astype(F32), axis=0)
     grad_mid = fold(mm_t(grad_pre, w1))
     up_part = mm_g(normed_mid, grad_pre).astype(BF)

time: 618 us -> 559 us (0.905)
  matrix products: 89 us -> 44.8 us
  Pallas kernels: 388 us -> 420 us
  local copies, waits for them, and re-layouts: 60.3 us -> 43.8 us
  other arithmetic: 55.8 us -> 41.4 us
  starting transfers between devices: 13.5 us -> 2.19 us
    pallas_call x2 -> x1, Pallas kernels: 162 us -> 200 us  [forward_call(): pl.pallas_call(partial(forward_kernel, widths), in_specs=[IN_VMEM] * 10,...]
    dot_general x2 -> x0, matrix products: 30.4 us -> none  [the longest x1 24.4 us: body(): pre_act = mm(normed_mid, w1) + bias_1]
    ppermute x8 -> x4, starting transfers between devices: 13.5 us -> 2.19 us  [swap_dp(): return lax.ppermute(x, 'dp', [(i, i ^ bit) for i in range(n)])]
    dot_general x4 -> x2, matrix products: 17.2 us -> 8.13 us  [body(): lax.dot_general(a, b, (((1,), (1,)), ((), ())), preferred_element_type=F32)]
    reshape x8 -> x3, local copies, waits for them, and re-layouts: 9.91 us -> 2.32 us  [feature_turn(): y = x.reshape(lead + (2,) * bits + (width,))]
    convert_element_type x4 -> x1, other arithmetic: 8.09 us -> 1.39 us  [body(): keep.astype(jnp.int32)]
    unnamed x154 -> x119, local copies, waits for them, and re-layouts: 17 us -> 19.3 us
  transfers between devices with their start and end apart: 8 -> 4, of which waited for: 2 -> 0; matrix products, arithmetic and copies ran while one was open for 9% -> 6% of each run, Pallas kernels for 0% -> 0%
where the time goes in v3:
time: 559 us; the launch traced here: 554 us
  Pallas kernels  420 us (75%)
  matrix products  44.8 us (8%)
  local copies, waits for them, and re-layouts  43.8 us (8%)
  other arithmetic  41.4 us (7%)
    pallas_call x1, Pallas kernels, forward_call(): pl.pallas_call(partial(forward_kernel, widths), in_specs=[IN_VMEM] * 10,...  200 us
    pallas_call x1, Pallas kernels, scatter_call(): pl.pallas_call(partial(scatter_kernel, widths), in_specs=[IN_VMEM] * (4 +...  185 us
    pallas_call x1, Pallas kernels, attn_backward(): pl.pallas_call(attn_bwd_kernel, grid=(rows // QB,), in_specs=[col, col, p...  35.1 us
    dot_general x4, matrix products, body(): lax.dot_general(a, b, (((0,), (0,)), ((), ())), preferred_element_type=F32)  25.4 us
    unnamed x119, local copies, waits for them, and re-layouts  19.3 us
  transfers between devices with their start and end apart: 4, of which 0 were waited for; matrix products, arithmetic and copies ran while one was open for 6% of the time, Pallas kernels for 0%

profile of v3, /device:TPU:1, one launch (start us, length us, event | category | flops | bytes accessed | tf_op | source)
XLA Modules:
  0.0 553.9 jit_solution(6534718335177074230)
XLA Ops:
  0.7 0.8 fusion.55
  1.5 1.4 select_reduce_fusion.2
  3.0 1.2 fusion.32
  4.2 0.7 broadcast_compare_fusion
  5.6 1.4 fusion.24.keep
  7.0 0.8 reshape.574
  7.9 0.7 reshape.576
  9.5 0.8 constant_dynamic-update-slice_fusion.7
  10.2 0.8 constant_dynamic-update-slice_fusion.6
  11.0 0.8 constant_dynamic-update-slice_fusion.5
  11.9 0.8 constant_dynamic-update-slice_fusion.1
  12.9 1.0 constant_dynamic-slice_fusion.5
  15.0 1.0 copy.110.qstart.qstart_ref
  16.6 1.3 compare_select_fusion.kpos.kpos_ref
  17.9 0.9 select_n.322.qpos.qpos_ref
  19.4 1.3 concatenate.110.vec
  20.6 199.9 %forward.1 = (bf16[1024,1536]{1,0:T(8,128)(2,1)}, bf16[1024,512]{1,0:T(8,128)(2,1)}, bf16[1024,2048]{1,0:T(8,128)(2,1)}, bf16[1024,2048]{1,0:T(8,128)(2,1)}, bf1...) custom-call(bf16[128,1536]{1,0:T(8,128)(2,1)} %copy-done.22, ...), custom_call_target="tpu_custom_call" | custom-call | tf_op jit(solution)/shard_map/forward/pallas_call | solution.py:691
  220.6 2.0 abs_reduce_fusion.2
  224.0 1.9 fusion.22
  225.9 0.8 fusion.51
  227.3 1.9 convert_reduce_fusion.4
  229.2 1.1 collective-permute-start
  231.3 0.8 copy-done.6
  235.1 1.4 fusion.23.mask_ref
  237.1 8.7 %convert_reduce_fusion = (f32[2048]{0:T(1024)S(1)}, bf16[1024,2048]{1,0:T(8,128)(2,1)S(1)}) fusion(bf16[1024,2048]{1,0:T(8,128)(2,1)} %get-tuple-element.42, bf16[1024,2048]{1,0:T(8,128)(2,1)} %get-tuple-element.41, bf16[512,1024]{1,0:T(8,128)(2,1)} %collective-permute-done, bf16[512,1024]{1,0:T(8,128)(2,1)} %get-tuple-element.143), kind=kOutput, calls=%fused_computation.3 | convolution fusion | flops 4309645312 | bytes 14688256 | tf_op jit(solution)/shard_map/dot_general | solution.py:972
  245.8 4.7 fusion.56
  250.6 1.9 copy-done.14
  252.5 1.1 slice.232
  254.3 9.5 %convolution_convert_fusion.1.rest_3_ = bf16[1024,2048]{1,0:T(8,128)(2,1)} fusion(bf16[1024,2048]{1,0:T(8,128)(2,1)} %get-tuple-element.53, bf16[512,1024]{1,0:T(8,128)(2,1)} %collective-permute-done, bf16[512,1024]{1,0:T(8,128)(2,1)} %get-tuple-element.143), kind=kOutput, calls=%fused_computation.7 | convolution fusion | flops 4301258752 | bytes 10485760 | tf_op jit(solution)/shard_map/dot_general | solution.py:940
  263.8 1.6 multiply_reduce_fusion.1
  265.4 0.9 fusion.50
  266.8 1.1 copy-done.7
  268.2 2.6 multiply_reduce_fusion.2
  270.8 0.8 fusion.49
  272.5 0.9 convert_reduce_fusion.5
  274.2 1.2 copy-done.40
  275.4 6.5 %convolution_convert_fusion.2.rest_2_ = bf16[1024,2048]{1,0:T(8,128)(2,1)} fusion(bf16[1024,1024]{1,0:T(8,128)(2,1)S(1)} %copy-done.40, bf16[1024,2048]{1,0:T(8,128)(2,1)S(1)} %copy-done.43), kind=kOutput, calls=%fused_computation.8 | convolution fusion | flops 4297064448 | bytes 10485760 | tf_op jit(solution)/shard_map/dot_general | solution.py:940
  282.0 2.6 convolution_convert_fusion.4.g_ref
  284.7 35.1 %attn_bwd.1 = bf16[1024,1536]{1,0:T(8,128)(2,1)S(1)} custom-call(s32[1024,1]{1,0:T(8,128)S(1)} %copy-done.1, s32[1024,1]{1,0:T(8,128)S(1)} %copy-done, s32[1,1024]{1,0:T(1,128)S(1)} %copy-done.2, f32[1024,128]{1,0:T(8,128)S(1)} %copy-done.3, bf16[1024,512]{1,0:T(8,128)(2,1)S(1)} %convolution_convert_fusion.4.g_ref, bf16[1024,1536]{1,0:T(8,128)(2,1)} %get-tuple-element.47.qkv_ref), custom_call_target="tpu_custom_call" | custom-call | flops 5368709120 | bytes 7340032 | tf_op jit(solution)/shard_map/attn_bwd/pallas_call | solution.py:129
  320.3 1.4 copy-done.38
  321.7 3.4 fusion.57
  325.1 2.0 copy-done.16
  327.1 1.1 slice.231
  330.0 4.4 convolution_convert_fusion.3.rest_1_
  334.3 5.1 convolution_convert_fusion.rest_0_
  339.4 2.3 multiply_reduce_fusion
  341.7 2.2 fusion.46
  343.9 1.0 fusion.21
  345.5 1.0 fusion.19
  346.5 0.8 reshape.584
  347.3 5.7 %rev.54 = bf16[512,2,2,256]{3,2,1,0:T(2,128)(2,1)S(1)} reverse(bf16[512,2,2,256]{3,2,1,0:T(2,128)(2,1)S(1)} %reshape.584), dimensions={2} | reverse | bytes 2097152 | tf_op jit(solution)/shard_map/jit(_flip)/rev | solution.py:872
  353.0 1.1 broadcast_select_fusion
  354.1 1.1 broadcast_select_fusion.1
  355.2 1.5 reshape.585.grd
  357.8 184.6 %scatter.1 = (f32[2,128,384]{2,1,0:T(8,128)}, f32[2,128,128]{2,1,0:T(8,128)}, f32[2,128,512]{2,1,0:T(8,128)}, f32[2,128,512]{2,1,0:T(8,128)}, bf16[512,1024]{1,0...) custom-call(s32[512,1]{1,0:T(8,128)} %fusion.23.mask_ref, f32[128,128]{1,0:T(8,128)} %maximum_bitcast_fusion.5.vec_ref, ...), custom_call_target="tpu_custom_call" | custom-call | tf_op jit(solution)/shard_map/scatter/pallas_call | solution.py:852
  542.4 1.4 slice_bitcast_fusion.16
  543.8 0.8 fusion.52
  544.6 1.1 slice_bitcast_fusion.1
  545.7 1.0 copy.122
  546.8 0.8 copy.121
  550.1 0.8 pad_maximum_fusion.6
  551.0 0.8 pad_maximum_fusion.7
  551.7 1.0 copy.163
  552.7 1.0 copy.164
  (234 shorter events, 20.2 us)
Async XLA Ops:
  4.2 11.8 %copy-start.31 = (f32[1024]{0:T(1024)S(1)}, f32[1024]{0:T(1024)}, u32[]{:S(2)}) copy-start(f32[1024]{0:T(1024)} %param.25) | copy-start | bytes 12292
  4.9 11.3 %copy-start.32 = (f32[1024]{0:T(1024)S(1)}, f32[1024]{0:T(1024)}, u32[]{:S(2)}) copy-start(f32[1024]{0:T(1024)} %param.27) | copy-start | bytes 12292
  5.6 10.8 %copy-start.33 = (f32[2,256]{1,0:T(2,128)S(1)}, f32[2,256]{1,0:T(2,128)}, u32[]{:S(2)}) copy-start(f32[2,256]{1,0:T(2,128)} %param.24) | copy-start | bytes 6148
  5.6 10.8 %copy-start.35 = (f32[1024]{0:T(1024)S(1)}, f32[1024]{0:T(1024)}, u32[]{:S(2)}) copy-start(f32[1024]{0:T(1024)} %param.26) | copy-start | bytes 12292
  7.0 9.5 %copy-start.25 = (bf16[128,1024]{1,0:T(8,128)(2,1)S(1)}, bf16[128,1024]{1,0:T(8,128)(2,1)}, u32[]{:S(2)}) copy-start(bf16[128,1024]{1,0:T(8,128)(2,1)} %param.22) | copy-start | bytes 786436
  16.6 2.2 copy-start.23
  16.6 2.2 copy-start.22
  220.6 2.2 copy-start.5
  222.8 0.8 copy-start.30
  222.8 1.2 copy-start.12
  227.3 3.0 copy-start.4
  229.2 8.0 %collective-permute-start = (bf16[512,1024]{1,0:T(8,128)(2,1)}, bf16[512,1024]{1,0:T(8,128)(2,1)}, u32[]{:S(2)}, u32[]{:S(2)}) collective-permute-start(bf16[512,1024]{1,0:T(8,128)(2,1)} %get-tuple-element.143), channel_id=1, source_target_pairs={{0,4},{4,0},{8,12},{12,8},{16,20},{20,16},{24,28},{28,24},{1,5},{5... | collective-permute-start | bytes 3145736 | tf_op jit(solution)/shard_map/ppermute | solution.py:145
  230.6 1.6 copy-start.6
  232.4 1.2 copy-start.8
  232.7 1.6 copy-start.34
  232.7 1.6 copy-start.36
  232.7 3.8 copy-start.29
  232.7 3.8 copy-start.28
  232.7 3.8 copy-start.27
  237.1 8.7 %copy-start.37 = (bf16[1024,2048]{1,0:T(8,128)(2,1)S(1)}, bf16[1024,2048]{1,0:T(8,128)(2,1)}, u32[]{:S(2)}) copy-start(bf16[1024,2048]{1,0:T(8,128)(2,1)} %get-tuple-element.43) | copy-start | bytes 12582916
  245.8 4.7 copy-start.42
  250.6 2.0 copy-start.14
  253.6 10.1 %collective-permute-start.1 = (bf16[512,1024]{1,0:T(8,128)(2,1)}, bf16[512,1024]{1,0:T(8,128)(2,1)S(1)}, u32[]{:S(2)}, u32[]{:S(2)}) collective-permute-start(bf16[512,1024]{1,0:T(8,128)(2,1)} %slice.232), channel_id=1, source_target_pairs={{0,4},{4,0},{8,12},{12,8},{16,20},{20,16},{24,28},{28,24},{1,5},{5... | collective-permute-start | bytes 3145736 | tf_op jit(solution)/shard_map/ppermute | solution.py:145
  254.3 9.5 %copy-start.15 = (f32[1024,1024]{1,0:T(8,128)S(1)}, f32[1024,1024]{1,0:T(8,128)}, u32[]{:S(2)}) copy-start(f32[1024,1024]{1,0:T(8,128)} %copy-done.14) | copy-start | bytes 12582916
  266.3 1.6 copy-start.7
  266.3 1.9 copy-start.13
  270.7 1.3 copy-start.10
  272.0 2.2 copy-start.43
  272.5 2.9 copy-start.40
  273.4 8.5 %copy-start.20 = (bf16[512,1024]{1,0:T(8,128)(2,1)}, bf16[512,1024]{1,0:T(8,128)(2,1)S(1)}, u32[]{:S(2)}) copy-start(bf16[512,1024]{1,0:T(8,128)(2,1)S(1)} %get-tuple-element.145) | copy-start | bytes 3145732
  273.5 8.5 %collective-permute-start.2 = (bf16[512,1024]{1,0:T(8,128)(2,1)S(1)}, bf16[512,1024]{1,0:T(8,128)(2,1)}, u32[]{:S(2)}, u32[]{:S(2)}) collective-permute-start(bf16[512,1024]{1,0:T(8,128)(2,1)S(1)} %get-tuple-element.145), channel_id=1, source_target_pairs={{0,4},{4,0},{8,12},{12,8},{16,20},{20,16},{24,28},{28,24},{1,5},{5... | collective-permute-start | bytes 3145736 | tf_op jit(solution)/shard_map/ppermute | solution.py:145
  275.4 6.6 %copy-start.41 = (bf16[1024,512]{1,0:T(8,128)(2,1)S(1)}, bf16[1024,512]{1,0:T(8,128)(2,1)}, u32[]{:S(2)}) copy-start(bf16[1024,512]{1,0:T(8,128)(2,1)} %get-tuple-element.46) | copy-start | bytes 3145732
  282.0 2.6 copy-start
  282.0 2.6 copy-start.1
  282.0 2.6 copy-start.2
  282.0 2.6 copy-start.3
  319.8 1.9 copy-start.38
  325.1 2.0 copy-start.16
  328.2 11.2 %collective-permute-start.3 = (bf16[512,1024]{1,0:T(8,128)(2,1)}, bf16[512,1024]{1,0:T(8,128)(2,1)}, u32[]{:S(2)}, u32[]{:S(2)}) collective-permute-start(bf16[512,1024]{1,0:T(8,128)(2,1)} %slice.231), channel_id=1, source_target_pairs={{0,4},{4,0},{8,12},{12,8},{16,20},{20,16},{24,28},{28,24},{1,5},{5... | collective-permute-start | bytes 3145736 | tf_op jit(solution)/shard_map/ppermute | solution.py:145
  329.9 4.4 copy-start.39
  334.3 5.1 copy-start.9
  334.3 5.1 copy-start.17
  343.9 1.6 copy-start.11
  542.4 4.3 copy-start.21
  544.6 2.2 copy-start.26
  545.7 1.9 copy-start.24
  546.8 4.9 copy-start.19
  550.9 1.8 copy-start.18
